TPU v7x, 32 devices: a whole 2x2x4 slice. The times are simulated.
32 devices in a mesh: slab: 8 (over z, x), pencil: 4 (over y, core).
Axes of the slice: x: 2, y: 2, z: 4, core: 2. Of those that a mesh axis runs over, the one named last changes fastest.
Arguments:
- potential: float32 [32, 128, 256], P('slab', 'pencil'), may hold values from -2.5 to 2.5
- parent_store: float32 [32, 2, 4, 128], P('slab', None, None, 'pencil'), may hold values from -520 to 520
- face_owner: int32 [8], replicated, may hold values from 0 to 7, as said below
- face_offset: int32 [8], replicated, may hold values from 0 to 3
Outputs:
- second_potential: float32 [32, 128, 256], P('slab', 'pencil')
- source: float32 [32, 128, 256], P('slab', 'pencil')
Inputs may be any that keep to these rules, and one draw needn't show every extreme that they name: The pairs (face_owner, face_offset) are all different; in every draw one owner holds exactly 4 slabs' faces.
All inputs are finite; a program needn't handle non-finite values.
Results may differ from a plain program's by a relative error of at most 0.0003.
Values sent between devices are 32-bit elements; how exact they have to be, the bound alone decides.
No kernel may reach another device: no remote copies, remote signals or barrier semaphores. Data moves between devices by JAX's collectives and lax.ppermute only.
A program may use at most 128 MiB of HBM per device.

v0:
```python
import jax
import jax.numpy as jnp
from jax import lax
from jax.sharding import PartitionSpec as P

CYCLES = 2


OMEGA = 0.8


def padded(cells, sides, width):
    for axis, dim in sides:
        count = lax.axis_size(axis)
        ends = count - 1
        head = lax.slice_in_dim(cells, 0, width, axis=dim)
        tail = lax.slice_in_dim(cells, cells.shape[dim] - width, cells.shape[dim], axis=dim)
        cells = jnp.concatenate(
            [
                lax.ppermute(tail, axis, [(i, (i + 1) % count) for i in range(ends)]),
                cells,
                lax.ppermute(head, axis, [((i + 1) % count, i) for i in range(ends)]),
            ],
            axis=dim,
        )
    return cells


def hessian_source(p):
    c = p[1:-1, 1:-1, 1:-1]
    pxx = p[1:-1, 1:-1, 2:] + p[1:-1, 1:-1, :-2] - 2.0 * c
    pyy = p[1:-1, 2:, 1:-1] + p[1:-1, :-2, 1:-1] - 2.0 * c
    pzz = p[2:, 1:-1, 1:-1] + p[:-2, 1:-1, 1:-1] - 2.0 * c
    pxy = 0.25 * (p[1:-1, 2:, 2:] - p[1:-1, :-2, 2:] - p[1:-1, 2:, :-2] + p[1:-1, :-2, :-2])
    pxz = 0.25 * (p[2:, 1:-1, 2:] - p[:-2, 1:-1, 2:] - p[2:, 1:-1, :-2] + p[:-2, 1:-1, :-2])
    pyz = 0.25 * (p[2:, 2:, 1:-1] - p[:-2, 2:, 1:-1] - p[2:, :-2, 1:-1] + p[:-2, :-2, 1:-1])
    return pxx * pyy + pxx * pzz + pyy * pzz - pxy * pxy - pxz * pxz - pyz * pyz


def apply_padded(p, level):
    c = p[1:-1, 1:-1, 1:-1]
    near = p[2:, 1:-1, 1:-1] + p[:-2, 1:-1, 1:-1]
    near = near + p[1:-1, 2:, 1:-1] + p[1:-1, :-2, 1:-1]
    near = near + p[1:-1, 1:-1, 2:] + p[1:-1, 1:-1, :-2]
    return (6.0 * c - near) * 0.25**level


def step_weight(level):
    return OMEGA / 6.0 * 4.0**level


def sweep_whole(u, rhs, level):
    return u + step_weight(level) * (rhs - apply_padded(jnp.pad(u, 1), level))


def restrict(r):
    a, b, c = r.shape
    return r.reshape(a // 2, 2, b // 2, 2, c // 2, 2).mean(axis=(1, 3, 5))


def prolong(e):
    a, b, c = e.shape
    return jnp.broadcast_to(e[:, None, :, None, :, None], (a, 2, b, 2, c, 2)).reshape(
        2 * a, 2 * b, 2 * c
    )


def is_coarsest(shape):
    return min(shape) <= 4 or any((d % 2 for d in shape))


def vcycle(u, rhs, level):
    if is_coarsest(rhs.shape):
        for sweep_count in range(8):
            u = sweep_whole(u, rhs, level)
        return u
    u = sweep_whole(u, rhs, level)
    u = sweep_whole(u, rhs, level)
    resid = rhs - apply_padded(jnp.pad(u, 1), level)
    coarse = restrict(resid)
    correction = vcycle(jnp.zeros_like(coarse), coarse, level + 1)
    u = u + prolong(correction)
    u = sweep_whole(u, rhs, level)
    u = sweep_whole(u, rhs, level)
    return u


def widen_x(p):
    return jnp.pad(p, ((0, 0), (0, 0), (1, 1)))


def rim_one(u):
    return widen_x(padded(u, (("slab", 0), ("pencil", 1)), 1))


def coarse_solve(rhs, level):
    width = rhs.shape[1]
    columns = rhs.shape[2]
    whole = lax.all_gather(rhs, ("slab", "pencil"), axis=0, tiled=True)
    whole = whole.reshape(lax.axis_size("slab"), lax.axis_size("pencil") * width, columns)
    solved = vcycle(jnp.zeros_like(whole), whole, level)
    start_y = lax.axis_index("pencil") * width
    return lax.dynamic_slice(
        solved, (lax.axis_index("slab"), start_y, jnp.int32(0)), (1, width, columns)
    )


def split_vcycle(u, rhs, level, from_zero):
    if rhs.shape[0] == 1:
        return coarse_solve(rhs, level)
    weight = step_weight(level)
    if from_zero:
        u = weight * rhs
    else:
        u = u + weight * (rhs - apply_padded(rim_one(u), level))
    u = u + weight * (rhs - apply_padded(rim_one(u), level))
    resid = rhs - apply_padded(rim_one(u), level)
    correction = split_vcycle(None, restrict(resid), level + 1, True)
    u = u + prolong(correction)
    u = u + weight * (rhs - apply_padded(rim_one(u), level))
    u = u + weight * (rhs - apply_padded(rim_one(u), level))
    return u


def on_device(potential, parent_store, face_owner, face_offset):
    depth, width, columns = potential.shape
    grown = widen_x(padded(potential, (("slab", 0), ("pencil", 1)), 1))
    source = hessian_source(grown)
    slab_index = lax.axis_index("slab")
    wanted = face_owner[slab_index] * parent_store.shape[0] + face_offset[slab_index]
    piece = lax.all_gather(parent_store, "slab", axis=0, tiled=True)
    labels = jnp.arange(piece.shape[0], dtype=jnp.int32)
    match = labels == wanted
    faces = jnp.sum(jnp.where(match[:, None, None, None], piece, 0.0), axis=0)
    rhs = -source
    rhs = rhs.at[:, :, 0].add(faces[0])
    rhs = rhs.at[:, :, columns - 1].add(faces[1])
    solved = jnp.zeros_like(rhs)
    for cycle in range(CYCLES):
        solved = split_vcycle(solved, rhs, 0, cycle == 0)
    return (solved, source)


def solution(mesh):
    in_specs = (P("slab", "pencil", None), P("slab", None, None, "pencil"), P(), P())
    out_specs = (P("slab", "pencil", None), P("slab", "pencil", None))
    return jax.shard_map(
        on_device, mesh=mesh, in_specs=in_specs, out_specs=out_specs, check_vma=False
    )
```

profile of v0, /device:TPU:0, one launch (start us, length us, event | category | flops | bytes accessed | tf_op | source)
XLA Modules:
  0.0 480.4 jit_solution(2995758600113464912)
XLA Ops:
  2.7 5.5 %collective-permute-start = (f32[1,32,256]{2,1,0:T(8,128)S(1)}, f32[1,32,256]{2,1,0:T(8,128)S(1)}, u32[]{:S(2)}, u32[]{:S(2)}) collective-permute-start(f32[1,32,256]{2,1,0:T(8,128)S(1)} %get-tuple-element.77), channel_id=1, source_target_pairs={{0,4},{4,8},{8,12},{12,16},{16,20},{20,24},{24,28},{1,5},{5,9},{9,... | collective-permute-start | bytes 98312 | tf_op jit(solution)/shard_map/ppermute | solution.py:20
  12.0 31.7 %all_gather.9 = f32[32,2,4,32]{3,2,1,0:T(4,128)S(1)} all-gather(f32[4,2,4,32]{3,2,1,0:T(4,128)} %param.9), channel_id=1, replica_groups=mesh['slab'=8,'pencil'=4] {'slab'}, dimensions={0}, use_global_device_ids=true | all-gather | bytes 36864 | tf_op jit(solution)/shard_map/all_gather | solution.py:131
  55.9 4.5 collective-permute-done.4
  63.6 4.4 collective-permute-done.6
  73.3 4.2 collective-permute-done.8
  84.8 9.8 %reshape.145 = f32[2,2,16,2,128,2]{5,4,3,2,1,0:T(8,128)} reshape(f32[4,32,256]{2,1,0:T(8,128)S(1)} %fusion.132) | data formatting | bytes 262144 | tf_op jit(solution)/shard_map/reshape | solution.py:58
  102.8 4.2 collective-permute-done.12
  118.5 4.2 collective-permute-done.16
  130.4 39.0 %all-gather = f32[256,64]{1,0:T(8,128)S(1)} all-gather(f32[8,64]{1,0:T(8,128)S(1)} %broadcast_multiply_fusion.6), channel_id=2, replica_groups=mesh['slab'=8,'pencil'=4] {'slab','pencil'}, dimensions={0}, use_global_device_ids=true | all-gather | bytes 67584 | tf_op jit(solution)/shard_map/all_gather | solution.py:99
  169.9 5.7 %reshape.147 = f32[4,2,16,2,32,2]{5,4,3,2,1,0:T(8,128)} reshape(f32[8,32,64]{2,1,0:T(8,128)S(1)} %fusion.30) | data formatting | bytes 131072 | tf_op jit(solution)/shard_map/reshape | solution.py:58
  181.6 4.9 %reshape.148 = f32[8,32,64]{2,1,0:T(8,128)S(1)} reshape(f32[4,2,16,2,32,2]{5,4,3,2,1,0:T(8,128)} %broadcast_in_dim.63) | data formatting | bytes 131072 | tf_op jit(solution)/shard_map/reshape | solution.py:63
  189.9 4.2 collective-permute-done.20
  201.7 4.2 collective-permute-done.24
  217.0 6.9 %reshape.149 = f32[4,32,256]{2,1,0:T(8,128)S(1)} reshape(f32[2,2,16,2,128,2]{5,4,3,2,1,0:T(8,128)} %broadcast_in_dim.68) | data formatting | bytes 262144 | tf_op jit(solution)/shard_map/reshape | solution.py:63
  228.7 4.2 collective-permute-done.28
  240.2 4.5 collective-permute-start.33
  246.3 4.2 collective-permute-done.32
  262.3 4.2 collective-permute-done.36
  273.7 4.3 collective-permute-start.41
  279.7 4.2 collective-permute-done.40
  291.2 4.8 %collective-permute-start.45 = (f32[1,32,256]{2,1,0:T(8,128)S(1)}, f32[1,32,256]{2,1,0:T(8,128)S(1)}, u32[]{:S(2)}, u32[]{:S(2)}) collective-permute-start(f32[1,32,256]{2,1,0:T(8,128)S(1)} %get-tuple-element.60), channel_id=1, source_target_pairs={{0,4},{4,8},{8,12},{12,16},{16,20},{20,24},{24,28},{1,5},{5,9},{9,... | collective-permute-start | bytes 98312 | tf_op jit(solution)/shard_map/ppermute | solution.py:20
  297.6 4.2 collective-permute-done.44
  309.0 9.8 %reshape.150 = f32[2,2,16,2,128,2]{5,4,3,2,1,0:T(8,128)} reshape(f32[4,32,256]{2,1,0:T(8,128)S(1)} %fusion.99) | data formatting | bytes 262144 | tf_op jit(solution)/shard_map/reshape | solution.py:58
  327.1 4.2 collective-permute-done.48
  342.5 4.2 collective-permute-done.52
  354.4 39.2 %all-gather.1 = f32[256,64]{1,0:T(8,128)S(1)} all-gather(f32[8,64]{1,0:T(8,128)S(1)} %broadcast_multiply_fusion.5), channel_id=3, replica_groups=mesh['slab'=8,'pencil'=4] {'slab','pencil'}, dimensions={0}, use_global_device_ids=true | all-gather | bytes 67584 | tf_op jit(solution)/shard_map/all_gather | solution.py:99
  394.2 5.7 %reshape.152 = f32[4,2,16,2,32,2]{5,4,3,2,1,0:T(8,128)} reshape(f32[8,32,64]{2,1,0:T(8,128)S(1)} %fusion.62) | data formatting | bytes 131072 | tf_op jit(solution)/shard_map/reshape | solution.py:58
  405.8 4.9 %reshape.153 = f32[8,32,64]{2,1,0:T(8,128)S(1)} reshape(f32[4,2,16,2,32,2]{5,4,3,2,1,0:T(8,128)} %broadcast_in_dim.69) | data formatting | bytes 131072 | tf_op jit(solution)/shard_map/reshape | solution.py:63
  414.1 4.2 collective-permute-done.56
  441.0 6.9 %reshape.154 = f32[4,32,256]{2,1,0:T(8,128)S(1)} reshape(f32[2,2,16,2,128,2]{5,4,3,2,1,0:T(8,128)} %broadcast_in_dim.74) | data formatting | bytes 262144 | tf_op jit(solution)/shard_map/reshape | solution.py:63
  452.4 4.2 collective-permute-done.64
  468.3 4.2 collective-permute-done.68
  (266 shorter events, 221.2 us)
Async XLA Ops:
  1.4 43.3 %collective-permute-start.1 = (f32[1,32,256]{2,1,0:T(8,128)S(1)}, f32[1,32,256]{2,1,0:T(8,128)S(1)}, u32[]{:S(2)}, u32[]{:S(2)}) collective-permute-start(f32[1,32,256]{2,1,0:T(8,128)S(1)} %get-tuple-element.76), channel_id=1, source_target_pairs={{4,0},{8,4},{12,8},{16,12},{20,16},{24,20},{28,24},{5,1},{9,5},{13... | collective-permute-start | bytes 98312 | tf_op jit(solution)/shard_map/ppermute | solution.py:22
  2.7 41.1 %collective-permute-start = (f32[1,32,256]{2,1,0:T(8,128)S(1)}, f32[1,32,256]{2,1,0:T(8,128)S(1)}, u32[]{:S(2)}, u32[]{:S(2)}) collective-permute-start(f32[1,32,256]{2,1,0:T(8,128)S(1)} %get-tuple-element.77), channel_id=1, source_target_pairs={{0,4},{4,8},{8,12},{12,16},{16,20},{20,24},{24,28},{1,5},{5,9},{9,... | collective-permute-start | bytes 98312 | tf_op jit(solution)/shard_map/ppermute | solution.py:20
  44.7 4.6 collective-permute-start.3
  54.3 6.1 %collective-permute-start.4 = (f32[1,32,256]{2,1,0:T(8,128)S(1)}, f32[1,32,256]{2,1,0:T(8,128)S(1)}, u32[]{:S(2)}, u32[]{:S(2)}) collective-permute-start(f32[1,32,256]{2,1,0:T(8,128)S(1)} %get-tuple-element.75), channel_id=1, source_target_pairs={{4,0},{8,4},{12,8},{16,12},{20,16},{24,20},{28,24},{5,1},{9,5},{13... | collective-permute-start | bytes 98312 | tf_op jit(solution)/shard_map/ppermute | solution.py:22
  62.3 5.7 %collective-permute-start.6 = (f32[6,1,256]{2,1,0:T(1,128)S(1)}, f32[6,1,256]{2,1,0:T(1,128)S(1)}, u32[]{:S(2)}, u32[]{:S(2)}) collective-permute-start(f32[6,1,256]{2,1,0:T(1,128)S(1)} %get-tuple-element.51), channel_id=1, source_target_pairs={{1,0},{2,1},{3,2},{5,4},{6,5},{7,6},{9,8},{10,9},{11,10},{13,12},{... | collective-permute-start | bytes 18440 | tf_op jit(solution)/shard_map/ppermute | solution.py:22
  68.3 5.0 %collective-permute-start.9 = (f32[1,32,256]{2,1,0:T(8,128)S(1)}, f32[1,32,256]{2,1,0:T(8,128)S(1)}, u32[]{:S(2)}, u32[]{:S(2)}) collective-permute-start(f32[1,32,256]{2,1,0:T(8,128)S(1)} %get-tuple-element.72), channel_id=1, source_target_pairs={{0,4},{4,8},{8,12},{12,16},{16,20},{20,24},{24,28},{1,5},{5,9},{9,... | collective-permute-start | bytes 98312 | tf_op jit(solution)/shard_map/ppermute | solution.py:20
  71.8 5.8 %collective-permute-start.8 = (f32[1,32,256]{2,1,0:T(8,128)S(1)}, f32[1,32,256]{2,1,0:T(8,128)S(1)}, u32[]{:S(2)}, u32[]{:S(2)}) collective-permute-start(f32[1,32,256]{2,1,0:T(8,128)S(1)} %get-tuple-element.73), channel_id=1, source_target_pairs={{4,0},{8,4},{12,8},{16,12},{20,16},{24,20},{28,24},{5,1},{9,5},{13... | collective-permute-start | bytes 98312 | tf_op jit(solution)/shard_map/ppermute | solution.py:22
  101.5 5.5 %collective-permute-start.12 = (f32[1,16,128]{2,1,0:T(8,128)S(1)}, f32[1,16,128]{2,1,0:T(8,128)S(1)}, u32[]{:S(2)}, u32[]{:S(2)}) collective-permute-start(f32[1,16,128]{2,1,0:T(8,128)S(1)} %get-tuple-element.109), channel_id=1, source_target_pairs={{4,0},{8,4},{12,8},{16,12},{20,16},{24,20},{28,24},{5,1},{9,5},{13... | collective-permute-start | bytes 24584 | tf_op jit(solution)/shard_map/ppermute | solution.py:22
  114.1 4.4 collective-permute-start.17
  117.2 5.5 %collective-permute-start.16 = (f32[1,16,128]{2,1,0:T(8,128)S(1)}, f32[1,16,128]{2,1,0:T(8,128)S(1)}, u32[]{:S(2)}, u32[]{:S(2)}) collective-permute-start(f32[1,16,128]{2,1,0:T(8,128)S(1)} %get-tuple-element.107), channel_id=1, source_target_pairs={{4,0},{8,4},{12,8},{16,12},{20,16},{24,20},{28,24},{5,1},{9,5},{13... | collective-permute-start | bytes 24584 | tf_op jit(solution)/shard_map/ppermute | solution.py:22
  122.7 4.2 collective-permute-start.19
  188.5 5.5 %collective-permute-start.20 = (f32[1,16,128]{2,1,0:T(8,128)S(1)}, f32[1,16,128]{2,1,0:T(8,128)S(1)}, u32[]{:S(2)}, u32[]{:S(2)}) collective-permute-start(f32[1,16,128]{2,1,0:T(8,128)S(1)} %get-tuple-element.105), channel_id=1, source_target_pairs={{4,0},{8,4},{12,8},{16,12},{20,16},{24,20},{28,24},{5,1},{9,5},{13... | collective-permute-start | bytes 24584 | tf_op jit(solution)/shard_map/ppermute | solution.py:22
  200.4 5.5 %collective-permute-start.24 = (f32[1,16,128]{2,1,0:T(8,128)S(1)}, f32[1,16,128]{2,1,0:T(8,128)S(1)}, u32[]{:S(2)}, u32[]{:S(2)}) collective-permute-start(f32[1,16,128]{2,1,0:T(8,128)S(1)} %get-tuple-element.103), channel_id=1, source_target_pairs={{4,0},{8,4},{12,8},{16,12},{20,16},{24,20},{28,24},{5,1},{9,5},{13... | collective-permute-start | bytes 24584 | tf_op jit(solution)/shard_map/ppermute | solution.py:22
  223.9 4.8 collective-permute-start.29
  227.2 5.8 %collective-permute-start.28 = (f32[1,32,256]{2,1,0:T(8,128)S(1)}, f32[1,32,256]{2,1,0:T(8,128)S(1)}, u32[]{:S(2)}, u32[]{:S(2)}) collective-permute-start(f32[1,32,256]{2,1,0:T(8,128)S(1)} %get-tuple-element.69), channel_id=1, source_target_pairs={{4,0},{8,4},{12,8},{16,12},{20,16},{24,20},{28,24},{5,1},{9,5},{13... | collective-permute-start | bytes 98312 | tf_op jit(solution)/shard_map/ppermute | solution.py:22
  240.2 6.1 %collective-permute-start.33 = (f32[1,32,256]{2,1,0:T(8,128)S(1)}, f32[1,32,256]{2,1,0:T(8,128)S(1)}, u32[]{:S(2)}, u32[]{:S(2)}) collective-permute-start(f32[1,32,256]{2,1,0:T(8,128)S(1)} %get-tuple-element.66), channel_id=1, source_target_pairs={{0,4},{4,8},{8,12},{12,16},{16,20},{20,24},{24,28},{1,5},{5,9},{9,... | collective-permute-start | bytes 98312 | tf_op jit(solution)/shard_map/ppermute | solution.py:20
  244.8 5.8 %collective-permute-start.32 = (f32[1,32,256]{2,1,0:T(8,128)S(1)}, f32[1,32,256]{2,1,0:T(8,128)S(1)}, u32[]{:S(2)}, u32[]{:S(2)}) collective-permute-start(f32[1,32,256]{2,1,0:T(8,128)S(1)} %get-tuple-element.67), channel_id=1, source_target_pairs={{4,0},{8,4},{12,8},{16,12},{20,16},{24,20},{28,24},{5,1},{9,5},{13... | collective-permute-start | bytes 98312 | tf_op jit(solution)/shard_map/ppermute | solution.py:22
  257.8 4.4 collective-permute-start.37
  260.7 5.8 %collective-permute-start.36 = (f32[1,32,256]{2,1,0:T(8,128)S(1)}, f32[1,32,256]{2,1,0:T(8,128)S(1)}, u32[]{:S(2)}, u32[]{:S(2)}) collective-permute-start(f32[1,32,256]{2,1,0:T(8,128)S(1)} %get-tuple-element.65), channel_id=1, source_target_pairs={{4,0},{8,4},{12,8},{16,12},{20,16},{24,20},{28,24},{5,1},{9,5},{13... | collective-permute-start | bytes 98312 | tf_op jit(solution)/shard_map/ppermute | solution.py:22
  273.7 5.9 %collective-permute-start.41 = (f32[1,32,256]{2,1,0:T(8,128)S(1)}, f32[1,32,256]{2,1,0:T(8,128)S(1)}, u32[]{:S(2)}, u32[]{:S(2)}) collective-permute-start(f32[1,32,256]{2,1,0:T(8,128)S(1)} %get-tuple-element.62), channel_id=1, source_target_pairs={{0,4},{4,8},{8,12},{12,16},{16,20},{20,24},{24,28},{1,5},{5,9},{9,... | collective-permute-start | bytes 98312 | tf_op jit(solution)/shard_map/ppermute | solution.py:20
  278.1 5.8 %collective-permute-start.40 = (f32[1,32,256]{2,1,0:T(8,128)S(1)}, f32[1,32,256]{2,1,0:T(8,128)S(1)}, u32[]{:S(2)}, u32[]{:S(2)}) collective-permute-start(f32[1,32,256]{2,1,0:T(8,128)S(1)} %get-tuple-element.63), channel_id=1, source_target_pairs={{4,0},{8,4},{12,8},{16,12},{20,16},{24,20},{28,24},{5,1},{9,5},{13... | collective-permute-start | bytes 98312 | tf_op jit(solution)/shard_map/ppermute | solution.py:22
  283.9 4.4 collective-permute-start.43
  291.2 6.4 %collective-permute-start.45 = (f32[1,32,256]{2,1,0:T(8,128)S(1)}, f32[1,32,256]{2,1,0:T(8,128)S(1)}, u32[]{:S(2)}, u32[]{:S(2)}) collective-permute-start(f32[1,32,256]{2,1,0:T(8,128)S(1)} %get-tuple-element.60), channel_id=1, source_target_pairs={{0,4},{4,8},{8,12},{12,16},{16,20},{20,24},{24,28},{1,5},{5,9},{9,... | collective-permute-start | bytes 98312 | tf_op jit(solution)/shard_map/ppermute | solution.py:20
  296.0 5.8 %collective-permute-start.44 = (f32[1,32,256]{2,1,0:T(8,128)S(1)}, f32[1,32,256]{2,1,0:T(8,128)S(1)}, u32[]{:S(2)}, u32[]{:S(2)}) collective-permute-start(f32[1,32,256]{2,1,0:T(8,128)S(1)} %get-tuple-element.61), channel_id=1, source_target_pairs={{4,0},{8,4},{12,8},{16,12},{20,16},{24,20},{28,24},{5,1},{9,5},{13... | collective-permute-start | bytes 98312 | tf_op jit(solution)/shard_map/ppermute | solution.py:22
  325.7 5.5 %collective-permute-start.48 = (f32[1,16,128]{2,1,0:T(8,128)S(1)}, f32[1,16,128]{2,1,0:T(8,128)S(1)}, u32[]{:S(2)}, u32[]{:S(2)}) collective-permute-start(f32[1,16,128]{2,1,0:T(8,128)S(1)} %get-tuple-element.101), channel_id=1, source_target_pairs={{4,0},{8,4},{12,8},{16,12},{20,16},{24,20},{28,24},{5,1},{9,5},{13... | collective-permute-start | bytes 24584 | tf_op jit(solution)/shard_map/ppermute | solution.py:22
  341.2 5.5 %collective-permute-start.52 = (f32[1,16,128]{2,1,0:T(8,128)S(1)}, f32[1,16,128]{2,1,0:T(8,128)S(1)}, u32[]{:S(2)}, u32[]{:S(2)}) collective-permute-start(f32[1,16,128]{2,1,0:T(8,128)S(1)} %get-tuple-element.99), channel_id=1, source_target_pairs={{4,0},{8,4},{12,8},{16,12},{20,16},{24,20},{28,24},{5,1},{9,5},{13... | collective-permute-start | bytes 24584 | tf_op jit(solution)/shard_map/ppermute | solution.py:22
  412.7 5.5 %collective-permute-start.56 = (f32[1,16,128]{2,1,0:T(8,128)S(1)}, f32[1,16,128]{2,1,0:T(8,128)S(1)}, u32[]{:S(2)}, u32[]{:S(2)}) collective-permute-start(f32[1,16,128]{2,1,0:T(8,128)S(1)} %get-tuple-element.97), channel_id=1, source_target_pairs={{4,0},{8,4},{12,8},{16,12},{20,16},{24,20},{28,24},{5,1},{9,5},{13... | collective-permute-start | bytes 24584 | tf_op jit(solution)/shard_map/ppermute | solution.py:22
  424.6 5.5 %collective-permute-start.60 = (f32[1,16,128]{2,1,0:T(8,128)S(1)}, f32[1,16,128]{2,1,0:T(8,128)S(1)}, u32[]{:S(2)}, u32[]{:S(2)}) collective-permute-start(f32[1,16,128]{2,1,0:T(8,128)S(1)} %get-tuple-element.95), channel_id=1, source_target_pairs={{4,0},{8,4},{12,8},{16,12},{20,16},{24,20},{28,24},{5,1},{9,5},{13... | collective-permute-start | bytes 24584 | tf_op jit(solution)/shard_map/ppermute | solution.py:22
  448.0 4.4 collective-permute-start.65
  450.8 5.8 %collective-permute-start.64 = (f32[1,32,256]{2,1,0:T(8,128)S(1)}, f32[1,32,256]{2,1,0:T(8,128)S(1)}, u32[]{:S(2)}, u32[]{:S(2)}) collective-permute-start(f32[1,32,256]{2,1,0:T(8,128)S(1)} %get-tuple-element.57), channel_id=1, source_target_pairs={{4,0},{8,4},{12,8},{16,12},{20,16},{24,20},{28,24},{5,1},{9,5},{13... | collective-permute-start | bytes 98312 | tf_op jit(solution)/shard_map/ppermute | solution.py:22
  463.8 4.4 collective-permute-start.69
  466.7 5.8 %collective-permute-start.68 = (f32[1,32,256]{2,1,0:T(8,128)S(1)}, f32[1,32,256]{2,1,0:T(8,128)S(1)}, u32[]{:S(2)}, u32[]{:S(2)}) collective-permute-start(f32[1,32,256]{2,1,0:T(8,128)S(1)} %get-tuple-element.55), channel_id=1, source_target_pairs={{4,0},{8,4},{12,8},{16,12},{20,16},{24,20},{28,24},{5,1},{9,5},{13... | collective-permute-start | bytes 98312 | tf_op jit(solution)/shard_map/ppermute | solution.py:22
  (40 other events, 151.4 us)
where the time goes:
time: 487 us; the launch traced here: 480 us
  starting transfers between devices  147 us (30%)
  waiting for transfers between devices  121 us (25%)
  blocking collectives  110 us (23%)
  local copies, waits for them, and re-layouts  74.5 us (15%)
  other arithmetic  24.2 us (5%)
    ppermute x36, waiting for transfers between devices, padded(): lax.ppermute(head, axis, [((i + 1) % count, i) for i in range(ends)])  117 us
    ppermute x36, starting transfers between devices, padded(): lax.ppermute(tail, axis, [(i, (i + 1) % count) for i in range(ends)])  101 us
    all_gather x2, blocking collectives, coarse_solve(): whole = lax.all_gather(rhs, ('slab', 'pencil'), axis=0, tiled=True)  78.2 us
    ppermute x36, starting transfers between devices, padded(): lax.ppermute(head, axis, [((i + 1) % count, i) for i in range(ends)])  46.7 us
    all_gather x1, blocking collectives, on_device(): piece = lax.all_gather(parent_store, 'slab', axis=0, tiled=True)  31.7 us
    reshape x4, local copies, waits for them, and re-layouts, restrict(): return r.reshape(a // 2, 2, b // 2, 2, c // 2, 2).mean(axis=(1, 3, 5))  31 us
    reshape x4, local copies, waits for them, and re-layouts, prolong(): jnp.broadcast_to(e[:, None, :, None, :, None], (a, 2, b, 2, c, 2))  23.6 us
    broadcast_in_dim x8, local copies, waits for them, and re-layouts, prolong(): jnp.broadcast_to(e[:, None, :, None, :, None], (a, 2, b, 2, c, 2))  13.9 us
  transfers between devices with their start and end apart: 72, of which 44 were waited for; matrix products, arithmetic and copies ran while one was open for 1% of the time, Pallas kernels for 0%

commit v1 on v0

--- a/solution.py
+++ b/solution.py
@@ -1,12 +1,568 @@
+from functools import partial
+
 import jax
 import jax.numpy as jnp
 from jax import lax
+from jax.experimental import pallas as pl
+from jax.experimental.pallas import tpu as pltpu
 from jax.sharding import PartitionSpec as P
 
 CYCLES = 2
-
-
 OMEGA = 0.8
+W = OMEGA / 6.0
+KEEP = 1.0 - OMEGA
+HALO = 8
+LANES = 128
+HIGHEST = lax.Precision.HIGHEST
+
+
+def is_coarsest(shape):
+    return min(shape) <= 4 or any((d % 2 for d in shape))
+
+
+def lane_iota(shape):
+    return lax.broadcasted_iota(jnp.int32, shape, len(shape) - 1)
+
+
+def row_iota(shape):
+    return lax.broadcasted_iota(jnp.int32, shape, len(shape) - 2)
+
+
+def halves(plane):
+    return plane[:, :LANES], plane[:, LANES:]
+
+
+def left_right(plane):
+    a, b = halves(plane)
+    lane = lane_iota(a.shape)
+    first = lane == 0
+    last = lane == LANES - 1
+    a1 = pltpu.roll(a, 1, 1)
+    b1 = pltpu.roll(b, 1, 1)
+    am = pltpu.roll(a, LANES - 1, 1)
+    bm = pltpu.roll(b, LANES - 1, 1)
+    left = jnp.concatenate([jnp.where(first, 0.0, a1), jnp.where(first, a1, b1)], axis=1)
+    right = jnp.concatenate([jnp.where(last, bm, am), jnp.where(last, 0.0, bm)], axis=1)
+    return left, right
+
+
+def down_up(plane):
+    rows = plane.shape[0]
+    return pltpu.roll(plane, 1, 0), pltpu.roll(plane, rows - 1, 0)
+
+
+def swept(below, here, above, q):
+    left, right = left_right(here)
+    down, up = down_up(here)
+    near = (below + above) + (left + right) + (down + up)
+    return KEEP * here + W * near + q
+
+
+def pair_rows(ref, count):
+    return ref[pl.ds(0, count, stride=2), :] + ref[pl.ds(1, count, stride=2), :]
+
+
+def spread_rows(ref, values):
+    count = values.shape[0]
+    ref[pl.ds(0, count, stride=2), :] = values
+    ref[pl.ds(1, count, stride=2), :] = values
+
+
+def halving_matrix(rows, columns):
+    i = lax.broadcasted_iota(jnp.int32, (rows, columns), 0)
+    j = lax.broadcasted_iota(jnp.int32, (rows, columns), 1)
+    return jnp.where(i // 2 == j, 0.5, 0.0)
+
+
+def doubling_matrix(rows, columns):
+    i = lax.broadcasted_iota(jnp.int32, (rows, columns), 0)
+    j = lax.broadcasted_iota(jnp.int32, (rows, columns), 1)
+    return jnp.where(i == j // 2, 1.0, 0.0)
+
+
+def mm(a, b):
+    return lax.dot_general(
+        a, b, (((1,), (0,)), ((), ())), precision=HIGHEST, preferred_element_type=jnp.float32
+    )
+
+
+def flat_sweep(u, q, shape):
+    zs, ys, xs = shape
+    rows = zs * ys
+    zero = jnp.zeros((ys, LANES), jnp.float32)
+    below = jnp.concatenate([zero, u[: rows - ys]], axis=0)
+    above = jnp.concatenate([u[ys:], zero], axis=0)
+    y = row_iota(u.shape) % ys
+    lane = lane_iota(u.shape)
+    down = jnp.where(y == 0, 0.0, pltpu.roll(u, 1, 0))
+    up = jnp.where(y == ys - 1, 0.0, pltpu.roll(u, rows - 1, 0))
+    left = pltpu.roll(u, 1, 1)
+    right = pltpu.roll(u, LANES - 1, 1)
+    out = KEEP * u + W * ((below + above) + (down + up) + (left + right)) + q
+    return jnp.where(lane < xs, out, 0.0)
+
+
+def flat_vcycle(q, shape, tmp_ref):
+    if is_coarsest(shape):
+        u = q
+        for _ in range(7):
+            u = flat_sweep(u, q, shape)
+        return u
+    zs, ys, xs = shape
+    u = flat_sweep(q, q, shape)
+    change = flat_sweep(u, q, shape) - u
+    pairs = [
+        change[2 * z * ys : (2 * z + 1) * ys] + change[(2 * z + 1) * ys : (2 * z + 2) * ys]
+        for z in range(zs // 2)
+    ]
+    half = zs * ys // 2
+    tmp_ref[pl.ds(0, half), :] = jnp.concatenate(pairs, axis=0)
+    coarse = mm(pair_rows(tmp_ref, half // 2), halving_matrix(LANES, LANES))
+    coarse_shape = (zs // 2, ys // 2, xs // 2)
+    e = flat_vcycle(coarse, coarse_shape, tmp_ref)
+    spread_rows(tmp_ref, mm(e, doubling_matrix(LANES, LANES)))
+    wide = tmp_ref[pl.ds(0, half), :]
+    planes = []
+    for z in range(zs // 2):
+        planes += [wide[z * ys : (z + 1) * ys]] * 2
+    u = u + jnp.concatenate(planes, axis=0)
+    u = flat_sweep(u, q, shape)
+    return flat_sweep(u, q, shape)
+
+
+def solve_level_one(gathered_ref, q_ref, a_ref, b_ref, tmp_ref, shape):
+    zs, ys, xs = shape
+    pencils, _, part, _ = gathered_ref.shape
+    inner = pl.ds(HALO, ys)
+    row = row_iota((ys, LANES))
+    lane = lane_iota((ys, LANES))
+    a_ref[...] = jnp.zeros_like(a_ref)
+    b_ref[...] = jnp.zeros_like(b_ref)
+    q_ref[pl.ds(0, 1)] = jnp.zeros((1,) + q_ref.shape[1:], jnp.float32)
+    q_ref[pl.ds(zs + 1, 1)] = jnp.zeros((1,) + q_ref.shape[1:], jnp.float32)
+    for part_index in range(pencils):
+        q_ref[pl.ds(1, zs), pl.ds(HALO + part_index * part, part), :] = gathered_ref[part_index]
+
+    def sweep_plane(src, z):
+        here = src[z, inner, :]
+        below = src[z - 1, inner, :]
+        above = src[z + 1, inner, :]
+        down = jnp.where(row == 0, 0.0, pltpu.roll(here, 1, 0))
+        up = jnp.where(row == ys - 1, 0.0, pltpu.roll(here, ys - 1, 0))
+        left = jnp.where(lane == 0, 0.0, pltpu.roll(here, 1, 1))
+        right = jnp.where(lane == LANES - 1, 0.0, pltpu.roll(here, LANES - 1, 1))
+        near = (below + above) + (down + up) + (left + right)
+        return here, KEEP * here + W * near + q_ref[z, inner, :]
+
+    def sweep(src, dst):
+        def body(z, carry):
+            dst[z, inner, :] = sweep_plane(src, z)[1]
+            return carry
+
+        lax.fori_loop(1, zs + 1, body, 0)
+
+    sweep(q_ref, a_ref)
+
+    def restrict(z, carry):
+        h0, s0 = sweep_plane(a_ref, 2 * z + 1)
+        h1, s1 = sweep_plane(a_ref, 2 * z + 2)
+        tmp_ref[pl.ds(pl.multiple_of(z * ys, ys), ys), :] = (s0 - h0) + (s1 - h1)
+        return carry
+
+    lax.fori_loop(0, zs // 2, restrict, 0)
+    coarse_shape = (zs // 2, ys // 2, xs // 2)
+    coarse = mm(
+        pair_rows(tmp_ref, coarse_shape[0] * coarse_shape[1]), halving_matrix(LANES, LANES)
+    )
+    e = flat_vcycle(coarse, coarse_shape, tmp_ref)
+    spread_rows(tmp_ref, mm(e, doubling_matrix(LANES, LANES)))
+
+    def correct(z, carry):
+        wide = tmp_ref[pl.ds(pl.multiple_of(z * ys, ys), ys), :]
+        a_ref[2 * z + 1, inner, :] = a_ref[2 * z + 1, inner, :] + wide
+        a_ref[2 * z + 2, inner, :] = a_ref[2 * z + 2, inner, :] + wide
+        return carry
+
+    lax.fori_loop(0, zs // 2, correct, 0)
+    sweep(a_ref, b_ref)
+    sweep(b_ref, a_ref)
+
+
+def pack_kernel(potential_ref, store_ref, out_ref):
+    depth, width, columns = potential_ref.shape
+    slots, _, _, _ = store_ref.shape
+    for z in range(depth):
+        out_ref[pl.ds(z * width, width), :] = potential_ref[z]
+    base = depth * width
+    out_ref[pl.ds(base, 8), :] = jnp.zeros((8, columns), jnp.float32)
+    for slot in range(slots):
+        for side in range(2):
+            out_ref[pl.ds(base + side * depth, depth), pl.ds(slot * width, width)] = store_ref[
+                slot, side
+            ]
+
+
+def blocks_of(own_ref, far_ref, others):
+    out = [(0, own_ref, None), (4, far_ref, None)]
+    for offset, ref in others:
+        out += [(offset, ref, 0), (offset ^ 4, ref, 1)]
+    return out
+
+
+def block_rows(ref, index, start, count):
+    if index is None:
+        return ref[pl.ds(start, count), :]
+    return ref[index, pl.ds(start, count), :]
+
+
+def edges_kernel(
+    where_ref, owner_ref, offset_ref, own_ref, far_ref, r1_ref, r2_ref, r3_ref,
+    even_ref, odd_ref, faces_ref, store_ref, rows_ref, *, depth, width
+):
+    slab = where_ref[0]
+    pencil = where_ref[1]
+    slabs = owner_ref.shape[0]
+    planes = slabs * depth
+    is_even = (pencil % 2) == 0
+    blocks = blocks_of(own_ref, far_ref, [(1, r1_ref), (2, r2_ref), (3, r3_ref)])
+    base = depth * width
+    for offset, ref, index in blocks:
+        target = slab ^ offset
+        store_ref[target] = block_rows(ref, index, base, 8)[:, :LANES]
+        for z in range(depth):
+            head = block_rows(ref, index, z * width, HALO)
+            tail = block_rows(ref, index, (z + 1) * width - HALO, HALO)
+            even_ref[target * depth + z] = jnp.where(is_even, tail, head)
+            odd_ref[target * depth + z] = jnp.where(is_even, head, tail)
+    rows_ref[...] = jnp.zeros_like(rows_ref)
+    for s in range(slabs):
+        tile = store_ref[owner_ref[s]]
+        slot = offset_ref[s]
+        picked = jnp.zeros((8, width), jnp.float32)
+        for k in range(LANES // width):
+            picked = jnp.where(slot == k, tile[:, k * width : (k + 1) * width], picked)
+        rows_ref[pl.ds(s * depth, depth), pl.ds(0, width)] = picked[:depth]
+        rows_ref[pl.ds(planes + s * depth, depth), pl.ds(0, width)] = picked[depth:]
+    faces = rows_ref[...].T
+    faces_ref[...] = faces[:width]
+    head = faces[:HALO]
+    tail = faces[width - HALO : width]
+    blank = jnp.zeros((HALO, LANES), jnp.float32)
+    even_ref[planes] = jnp.concatenate([jnp.where(is_even, tail, head), blank], axis=1)
+    odd_ref[planes] = jnp.concatenate([jnp.where(is_even, head, tail), blank], axis=1)
+
+
+def first_kernel(
+    where_ref, own_ref, far_ref, r1_ref, r2_ref, r3_ref, even_ref, odd_ref, faces_ref,
+    source_ref, q_ref, u_ref, coarse_ref, p_ref, f_ref, left_ref, right_ref,
+    *, depth, width, height
+):
+    slab = where_ref[0]
+    pencil = where_ref[1]
+    planes = p_ref.shape[0] - 2
+    rows = width + 2 * HALO
+    columns = p_ref.shape[2]
+    is_even = (pencil % 2) == 0
+    blank = jnp.zeros((rows, columns), jnp.float32)
+    p_ref[0] = blank
+    p_ref[planes + 1] = blank
+    for ref in (q_ref, u_ref):
+        for z in (0, 1, planes + 2, planes + 3):
+            ref[z] = blank
+    for offset, ref, index in blocks_of(own_ref, far_ref, [(1, r1_ref), (2, r2_ref), (3, r3_ref)]):
+        target = (slab ^ offset) * depth + 1
+        for z in range(depth):
+            p_ref[target + z, pl.ds(HALO, width), :] = block_rows(ref, index, z * width, width)
+
+    def edges(z, carry):
+        first = even_ref[z]
+        second = odd_ref[z]
+        p_ref[z + 1, pl.ds(0, HALO), :] = jnp.where(is_even, second, first)
+        p_ref[z + 1, pl.ds(HALO + width, HALO), :] = jnp.where(is_even, first, second)
+        return carry
+
+    lax.fori_loop(0, planes, edges, 0)
+    first = even_ref[planes][:, :LANES]
+    second = odd_ref[planes][:, :LANES]
+    f_ref[pl.ds(0, HALO), :] = jnp.where(is_even, second, first)
+    f_ref[pl.ds(HALO, width), :] = faces_ref[...]
+    f_ref[pl.ds(HALO + width, HALO), :] = jnp.where(is_even, first, second)
+
+    y = lax.broadcasted_iota(jnp.int32, (rows, columns), 0) + pencil * width - HALO
+    inside = jnp.where((y >= 0) & (y < height), 1.0, 0.0)
+    lane = lane_iota((rows, LANES))
+
+    def hessian(z, carry):
+        below = p_ref[z]
+        here = p_ref[z + 1]
+        above = p_ref[z + 2]
+        left, right = left_right(here)
+        down, up = down_up(here)
+        pxx = left + right - 2.0 * here
+        pyy = down + up - 2.0 * here
+        pzz = below + above - 2.0 * here
+        rise = above - below
+        left, right = left_right(rise)
+        pxz = right - left
+        d, u = down_up(rise)
+        pyz = u - d
+        left, right = left_right(up - down)
+        pxy = right - left
+        cross = pxy * pxy + pxz * pxz + pyz * pyz
+        source = pxx * pyy + (pxx + pyy) * pzz - 0.0625 * cross
+
+        @pl.when(z // depth == slab)
+        def _():
+            source_ref[z % depth] = source[HALO : HALO + width]
+
+        faces = f_ref[...]
+        low = jnp.where(lane == 0, pltpu.roll(faces, (LANES - z) & (LANES - 1), 1), 0.0)
+        high = jnp.where(lane == LANES - 1, pltpu.roll(faces, LANES - 1 - planes - z, 1), 0.0)
+        q_ref[z + 2] = (W * inside) * (jnp.concatenate([low, high], axis=1) - source)
+        return carry
+
+    lax.fori_loop(0, planes, hessian, 0)
+
+    def second_sweep(z, carry):
+        here = q_ref[z + 2]
+        u_ref[z + 2] = inside * swept(q_ref[z + 1], here, q_ref[z + 3], here)
+        return carry
+
+    lax.fori_loop(0, planes, second_sweep, 0)
+    restrict_window(u_ref, q_ref, coarse_ref, left_ref, right_ref, planes, width)
+
+
+def restrict_window(u_ref, q_ref, coarse_ref, left_ref, right_ref, planes, width):
+    def change(z):
+        here = u_ref[z + 2]
+        return swept(u_ref[z + 1], here, u_ref[z + 3], q_ref[z + 2]) - here
+
+    def restrict(z, carry):
+        both = (change(2 * z) + change(2 * z + 1))[HALO : HALO + width]
+        spot = pl.ds(pl.multiple_of(z * width, width), width)
+        left_ref[spot, :] = both[:, :LANES]
+        right_ref[spot, :] = both[:, LANES:]
+        return carry
+
+    lax.fori_loop(0, planes // 2, restrict, 0)
+    count = planes // 2 * width // 2
+    wide = jnp.concatenate([pair_rows(left_ref, count), pair_rows(right_ref, count)], axis=1)
+    coarse_ref[...] = mm(wide, halving_matrix(2 * LANES, LANES))
+
+
+def prolong_planes(v_ref, left_ref, right_ref, pencil, width, start, count):
+    part = width // 2
+    rows = part + 2 * HALO
+    spot = pl.ds(pl.multiple_of(pencil * part, part), rows)
+    e = v_ref[pl.ds(start, count), spot, :].reshape(count * rows, LANES)
+    wide = mm(e, doubling_matrix(LANES, 2 * LANES))
+    spread_rows(left_ref, wide[:, :LANES])
+    spread_rows(right_ref, wide[:, LANES:])
+
+
+def prolonged(left_ref, right_ref, z, width):
+    rows = width + 4 * HALO
+    spot = pl.ds(pl.multiple_of(z * rows + HALO, HALO), width + 2 * HALO)
+    return jnp.concatenate([left_ref[spot, :], right_ref[spot, :]], axis=1)
+
+
+def middle_kernel(
+    where_ref, gathered_ref, q_ref, u_ref, qwin_ref, uwin_ref, coarse_ref,
+    q1_ref, a1_ref, b1_ref, tmp_ref, left_ref, right_ref, a_ref, b_ref,
+    *, depth, width, height, shape
+):
+    slab = where_ref[0]
+    pencil = where_ref[1]
+    planes = a_ref.shape[0] - 4
+    rows = width + 2 * HALO
+    columns = a_ref.shape[2]
+    solve_level_one(gathered_ref, q1_ref, a1_ref, b1_ref, tmp_ref, shape)
+    prolong_planes(a1_ref, left_ref, right_ref, pencil, width, 1, planes // 2)
+    blank = jnp.zeros((rows, columns), jnp.float32)
+    for ref in (a_ref, b_ref):
+        for z in (0, 1, planes + 2, planes + 3):
+            ref[z] = blank
+
+    def correct(z, carry):
+        wide = prolonged(left_ref, right_ref, z, width)
+        a_ref[2 * z + 2] = u_ref[2 * z + 2] + wide
+        a_ref[2 * z + 3] = u_ref[2 * z + 3] + wide
+        return carry
+
+    lax.fori_loop(0, planes // 2, correct, 0)
+    y = lax.broadcasted_iota(jnp.int32, (rows, columns), 0) + pencil * width - HALO
+    inside = jnp.where((y >= 0) & (y < height), 1.0, 0.0)
+
+    def sweep(src, dst):
+        def body(z, carry):
+            dst[z + 2] = inside * swept(src[z + 1], src[z + 2], src[z + 3], q_ref[z + 2])
+            return carry
+
+        lax.fori_loop(0, planes, body, 0)
+
+    sweep(a_ref, b_ref)
+    sweep(b_ref, a_ref)
+    sweep(a_ref, b_ref)
+    sweep(b_ref, a_ref)
+    restrict_window(a_ref, q_ref, coarse_ref, left_ref, right_ref, planes, width)
+    for z in range(depth + 4):
+        qwin_ref[z] = q_ref[slab * depth + z]
+        uwin_ref[z] = a_ref[slab * depth + z]
+
+
+def last_kernel(
+    where_ref, gathered_ref, qwin_ref, uwin_ref, out_ref,
+    q1_ref, a1_ref, b1_ref, tmp_ref, left_ref, right_ref, a_ref, b_ref,
+    *, depth, width, height, shape
+):
+    slab = where_ref[0]
+    pencil = where_ref[1]
+    planes = shape[0] * 2
+    rows = width + 2 * HALO
+    columns = a_ref.shape[2]
+    solve_level_one(gathered_ref, q1_ref, a1_ref, b1_ref, tmp_ref, shape)
+    coarse = depth // 2 + 2
+    prolong_planes(a1_ref, left_ref, right_ref, pencil, width, slab * (depth // 2), coarse)
+    for z in range(coarse):
+        wide = prolonged(left_ref, right_ref, z, width)
+        a_ref[2 * z] = uwin_ref[2 * z] + wide
+        a_ref[2 * z + 1] = uwin_ref[2 * z + 1] + wide
+    y = lax.broadcasted_iota(jnp.int32, (rows, columns), 0) + pencil * width - HALO
+    inside = jnp.where((y >= 0) & (y < height), 1.0, 0.0)
+    for z in range(1, depth + 3):
+        at = slab * depth - 2 + z
+        live = jnp.where((at >= 0) & (at < planes), inside, 0.0)
+        b_ref[z] = live * swept(a_ref[z - 1], a_ref[z], a_ref[z + 1], qwin_ref[z])
+    for z in range(2, depth + 2):
+        new = swept(b_ref[z - 1], b_ref[z], b_ref[z + 1], qwin_ref[z])
+        out_ref[z - 2] = new[HALO : HALO + width]
+
+
+def vmem():
+    return pl.BlockSpec(memory_space=pltpu.VMEM)
+
+
+def smem():
+    return pl.BlockSpec(memory_space=pltpu.SMEM)
+
+
+def arr(*shape):
+    return jax.ShapeDtypeStruct(shape, jnp.float32)
+
+
+def buf(*shape):
+    return pltpu.VMEM(shape, jnp.float32)
+
+
+def call(kernel, name, scalars, args, outs, scratch=()):
+    return pl.pallas_call(
+        kernel,
+        out_shape=outs,
+        in_specs=[smem()] * len(scalars) + [vmem()] * len(args),
+        out_specs=jax.tree.map(lambda _: vmem(), outs),
+        scratch_shapes=list(scratch),
+        compiler_params=pltpu.CompilerParams(vmem_limit_bytes=48 << 20),
+        name=name,
+    )(*scalars, *args)
+
+
+def windowed(potential, parent_store, face_owner, face_offset):
+    depth, width, columns = potential.shape
+    slabs = lax.axis_size("slab")
+    pencils = lax.axis_size("pencil")
+    planes, height = slabs * depth, pencils * width
+    rows = width + 2 * HALO
+    where = jnp.stack([lax.axis_index("slab"), lax.axis_index("pencil")]).astype(jnp.int32)
+    own = call(
+        pack_kernel, "pack", [], [potential, parent_store], arr(depth * width + 8, columns)
+    )
+
+    def swap(x, bits):
+        return lax.ppermute(x, "slab", [(i, i ^ bits) for i in range(slabs)])
+
+    far = swap(own, 4)
+    both = jnp.stack([own, far])
+    others = [swap(both, bits) for bits in (1, 2, 3)]
+
+    even, odd, faces = call(
+        partial(edges_kernel, depth=depth, width=width),
+        "edges",
+        [where, face_owner, face_offset],
+        [own, far, *others],
+        (arr(planes + 1, HALO, columns), arr(planes + 1, HALO, columns), arr(width, LANES)),
+        [buf(slabs, 8, LANES), buf(LANES, LANES)],
+    )
+    low_pairs = [(i, i + 1) for i in range(0, pencils - 1, 2)]
+    high_pairs = [(i, i + 1) for i in range(1, pencils - 1, 2)]
+    even = lax.ppermute(even, "pencil", low_pairs + [(j, i) for i, j in low_pairs])
+    odd = lax.ppermute(odd, "pencil", high_pairs + [(j, i) for i, j in high_pairs])
+    shape = (planes // 2, height // 2, columns // 2)
+    part = arr(planes // 2 * (width // 2), columns // 2)
+    field = (planes + 4, rows, columns)
+    half_rows = planes // 2 * (width + 4 * HALO)
+    source, q, u, coarse = call(
+        partial(first_kernel, depth=depth, width=width, height=height),
+        "first",
+        [where],
+        [own, far, *others, even, odd, faces],
+        (arr(depth, width, columns), arr(*field), arr(*field), part),
+        [
+            buf(planes + 2, rows, columns),
+            buf(rows, LANES),
+            buf(planes // 2 * width, LANES),
+            buf(planes // 2 * width, LANES),
+        ],
+    )
+    level = (shape[0] + 2, shape[1] + 2 * HALO, LANES)
+    level_scratch = [
+        buf(*level),
+        buf(*level),
+        buf(*level),
+        buf(shape[0] * shape[1], LANES),
+        buf(half_rows, LANES),
+        buf(half_rows, LANES),
+    ]
+
+    def gather(x):
+        whole = lax.all_gather(x, "pencil", axis=0, tiled=False)
+        return whole.reshape(pencils, shape[0], width // 2, columns // 2)
+
+    sizes = dict(depth=depth, width=width, height=height, shape=shape)
+    slim = (depth + 4, rows, columns)
+    qwin, uwin, coarse = call(
+        partial(middle_kernel, **sizes),
+        "middle",
+        [where],
+        [gather(coarse), q, u],
+        (arr(*slim), arr(*slim), part),
+        level_scratch + [buf(*field), buf(*field)],
+    )
+    solved = call(
+        partial(last_kernel, **sizes),
+        "last",
+        [where],
+        [gather(coarse), qwin, uwin],
+        arr(depth, width, columns),
+        level_scratch + [buf(*slim), buf(*slim)],
+    )
+    return solved, source
+
+
+def fits_window(potential, parent_store):
+    depth, width, columns = potential.shape
+    slabs = lax.axis_size("slab")
+    pencils = lax.axis_size("pencil")
+    planes = slabs * depth
+    return (
+        slabs == 8
+        and pencils % 2 == 0
+        and depth == 4
+        and columns == 2 * LANES
+        and width == 32
+        and parent_store.shape[0] * width == LANES
+        and 2 * planes <= LANES
+        and pencils <= 8
+    )
 
 
 def padded(cells, sides, width):
@@ -65,10 +621,6 @@
     )
 
 
-def is_coarsest(shape):
-    return min(shape) <= 4 or any((d % 2 for d in shape))
-
-
 def vcycle(u, rhs, level):
     if is_coarsest(rhs.shape):
         for sweep_count in range(8):
@@ -122,7 +674,7 @@
     return u
 
 
-def on_device(potential, parent_store, face_owner, face_offset):
+def plain(potential, parent_store, face_owner, face_offset):
     depth, width, columns = potential.shape
     grown = widen_x(padded(potential, (("slab", 0), ("pencil", 1)), 1))
     source = hessian_source(grown)
@@ -141,6 +693,12 @@
     return (solved, source)
 
 
+def on_device(potential, parent_store, face_owner, face_offset):
+    if fits_window(potential, parent_store):
+        return windowed(potential, parent_store, face_owner, face_offset)
+    return plain(potential, parent_store, face_owner, face_offset)
+
+
 def solution(mesh):
     in_specs = (P("slab", "pencil", None), P("slab", None, None, "pencil"), P(), P())
     out_specs = (P("slab", "pencil", None), P("slab", "pencil", None))

time: 487 us -> 102 us (0.21); the launches traced: 480 us -> 101 us
  starting transfers between devices: 147 us -> 8.33 us
  waiting for transfers between devices: 121 us -> 18.7 us
  blocking collectives: 110 us -> 20.6 us
  local copies, waits for them, and re-layouts: 74.5 us -> 2.92 us
  Pallas kernels: 0 us -> 50 us
  other arithmetic: 24.2 us -> 0.1 us
    ppermute x72 -> x6, starting transfers between devices: 147 us -> 8.33 us  [the longest x4 7.6 us: swap(): return lax.ppermute(x, 'slab', [(i, i ^ bits) for i in range(slabs)])]
    ppermute x72 -> x6, waiting for transfers between devices: 121 us -> 18.7 us  [the longest x4 17.8 us: swap(): return lax.ppermute(x, 'slab', [(i, i ^ bits) for i in range(slabs)])]
    all_gather x3 -> x2, blocking collectives: 110 us -> 20.6 us  [gather(): whole = lax.all_gather(x, 'pencil', axis=0, tiled=False)]
    reshape x8 -> x0, local copies, waits for them, and re-layouts: 54.6 us -> none  [the longest x4 31 us: restrict(): return r.reshape(a // 2, 2, b // 2, 2, c // 2, 2).mean(axis=(1, 3, 5))]
    pallas_call x0 -> x5, Pallas kernels: none -> 50 us  [call(): pl.pallas_call(kernel, out_shape=outs, in_specs=[smem()] * len(scalars) +...]
    broadcast_in_dim x8 -> x0, local copies, waits for them, and re-layouts: 13.9 us -> none  [prolong(): jnp.broadcast_to(e[:, None, :, None, :, None], (a, 2, b, 2, c, 2))]
    reduce_sum x9 -> x0, other arithmetic: 13.7 us -> none  [the longest x8 13.6 us: restrict(): return r.reshape(a // 2, 2, b // 2, 2, c // 2, 2).mean(axis=(1, 3, 5))]
  transfers between devices with their start and end apart: 72 -> 6, of which waited for: 44 -> 5; matrix products, arithmetic and copies ran while one was open for 1% -> 0% of each run, Pallas kernels for 0% -> 0%
where the time goes in v1:
time: 102 us; the launch traced here: 101 us
  Pallas kernels  50 us (49%)
  blocking collectives  20.6 us (20%)
  waiting for transfers between devices  18.7 us (18%)
  starting transfers between devices  8.33 us (8%)
  local copies, waits for them, and re-layouts  2.92 us (3%)
    pallas_call x5, Pallas kernels, call(): pl.pallas_call(kernel, out_shape=outs, in_specs=[smem()] * len(scalars) +...  50 us
    all_gather x2, blocking collectives, gather(): whole = lax.all_gather(x, 'pencil', axis=0, tiled=False)  20.6 us
    ppermute x4, waiting for transfers between devices, swap(): return lax.ppermute(x, 'slab', [(i, i ^ bits) for i in range(slabs)])  17.8 us
    ppermute x4, starting transfers between devices, swap(): return lax.ppermute(x, 'slab', [(i, i ^ bits) for i in range(slabs)])  7.6 us
    unnamed x8, local copies, waits for them, and re-layouts  2.92 us
  transfers between devices with their start and end apart: 6, of which 5 were waited for; matrix products, arithmetic and copies ran while one was open for 0% of the time, Pallas kernels for 0%

profile of v1, /device:TPU:0, one launch (start us, length us, event | category | flops | bytes accessed | tf_op | source)
XLA Modules:
  0.0 101.3 jit_solution(10482514728391993148)
XLA Ops:
  0.6 0.0 copy-start
  0.6 0.9 copy-done
  1.5 0.0 copy-start.1
  1.5 0.7 copy-done.1
  2.3 0.1 pack.1.own_ref
  2.3 4.0 %collective-permute-start = (f32[136,256]{1,0:T(8,128)S(1)}, f32[136,256]{1,0:T(8,128)S(1)}, u32[]{:S(2)}, u32[]{:S(2)}) collective-permute-start(f32[136,256]{1,0:T(8,128)S(1)} %pack.1.own_ref), channel_id=1, source_target_pairs={{0,16},{4,20},{8,24},{12,28},{16,0},{20,4},{24,8},{28,12},{1,17},{... | collective-permute-start | bytes 417800 | tf_op jit(solution)/shard_map/ppermute | solution.py:481
  6.4 6.7 %collective-permute-done.far_ref = f32[136,256]{1,0:T(8,128)S(1)} collective-permute-done((f32[136,256]{1,0:T(8,128)S(1)}, f32[136,256]{1,0:T(8,128)S(1)}, u32[]{:S(2)}, u32[]{:S(2)}) %collective-permute-start) | collective-permute-done | bytes 139296 | tf_op jit(solution)/shard_map/ppermute | solution.py:481
  13.1 1.7 %collective-permute-start.3 = (f32[2,136,256]{2,1,0:T(8,128)S(1)}, f32[2,136,256]{2,1,0:T(8,128)S(1)}, u32[]{:S(2)}, u32[]{:S(2)}) collective-permute-start(f32[2,136,256]{2,1,0:T(8,128)S(1)} %pad_maximum_fusion), channel_id=1, source_target_pairs={{0,12},{4,8},{8,4},{12,0},{16,28},{20,24},{24,20},{28,16},{1,13},{... | collective-permute-start | bytes 835592 | tf_op jit(solution)/shard_map/ppermute | solution.py:481
  14.8 1.4 %collective-permute-start.2 = (f32[2,136,256]{2,1,0:T(8,128)S(1)}, f32[2,136,256]{2,1,0:T(8,128)S(1)}, u32[]{:S(2)}, u32[]{:S(2)}) collective-permute-start(f32[2,136,256]{2,1,0:T(8,128)S(1)} %pad_maximum_fusion), channel_id=1, source_target_pairs={{0,8},{4,12},{8,0},{12,4},{16,24},{20,28},{24,16},{28,20},{1,9},{5... | collective-permute-start | bytes 835592 | tf_op jit(solution)/shard_map/ppermute | solution.py:481
  16.1 0.5 collective-permute-start.1
  16.6 0.1 pad_add_fusion.where_ref
  16.7 7.0 %collective-permute-done.3.r3_ref = f32[2,136,256]{2,1,0:T(8,128)S(1)} collective-permute-done((f32[2,136,256]{2,1,0:T(8,128)S(1)}, f32[2,136,256]{2,1,0:T(8,128)S(1)}, u32[]{:S(2)}, u32[]{:S(2)}) %collective-permute-start.3) | collective-permute-done | bytes 278560 | tf_op jit(solution)/shard_map/ppermute | solution.py:481
  23.7 4.0 %collective-permute-done.2.r2_ref = f32[2,136,256]{2,1,0:T(8,128)S(1)} collective-permute-done((f32[2,136,256]{2,1,0:T(8,128)S(1)}, f32[2,136,256]{2,1,0:T(8,128)S(1)}, u32[]{:S(2)}, u32[]{:S(2)}) %collective-permute-start.2) | collective-permute-done | bytes 278560 | tf_op jit(solution)/shard_map/ppermute | solution.py:481
  27.7 0.2 collective-permute-done.1.r1_ref
  27.8 0.0 copy-start.2
  27.8 0.7 copy-done.2
  28.5 0.0 copy-start.3
  28.5 0.7 copy-done.3
  29.1 0.9 edges.1
  30.1 0.1 collective-permute-start.4
  30.1 0.7 collective-permute-start.5
  30.8 0.8 collective-permute-done.4.even_ref
  31.7 0.0 collective-permute-done.5.odd_ref
  31.7 14.3 %first.1 = (f32[4,32,256]{2,1,0:T(8,128)}, f32[36,48,256]{2,1,0:T(8,128)S(1)}, f32[36,48,256]{2,1,0:T(8,128)S(1)}, f32[256,128]{1,0:T(8,128)S(1)}) custom-call(s32[2]{0:T(128)S(1)} %pad_add_fusion.where_ref, f32[136,256]{1,0:T(8,128)S(1)} %pack.1.own_ref, f32[136,256]{1,0:T(8,128)S(1)} %collective-permute-done.far_ref, ...), custom_call_target="tpu_custom_call" | custom-call | tf_op jit(solution)/shard_map/first/pallas_call | solution.py:458
  45.9 13.3 %all-gather = f32[1024,128]{1,0:T(8,128)S(1)} all-gather(f32[256,128]{1,0:T(8,128)S(1)} %get-tuple-element.15), channel_id=2, replica_groups=mesh['slab'=8,'pencil'=4] {'pencil'}, dimensions={0}, use_global_device_ids=true | all-gather | bytes 655360 | tf_op jit(solution)/shard_map/all_gather | solution.py:527
  59.2 25.4 %middle.1 = (f32[8,48,256]{2,1,0:T(8,128)S(1)}, f32[8,48,256]{2,1,0:T(8,128)S(1)}, f32[256,128]{1,0:T(8,128)S(1)}) custom-call(s32[2]{0:T(128)S(1)} %pad_add_fusion.where_ref, f32[4,16,16,128]{3,2,1,0:T(8,128)S(1)} %bitcast.7, f32[36,48,256]{2,1,0:T(8,128)S(1)} %get-tuple-element.16.q_ref, f32[36,48,256]{2,1,0:T(8,128)S(1)} %get-tuple-element.17.u_ref), custom_call_target="tpu_custom_call" | custom-call | tf_op jit(solution)/shard_map/middle/pallas_call | solution.py:458
  84.6 7.3 %all-gather.1 = f32[1024,128]{1,0:T(8,128)S(1)} all-gather(f32[256,128]{1,0:T(8,128)S(1)} %get-tuple-element.18), channel_id=3, replica_groups=mesh['slab'=8,'pencil'=4] {'pencil'}, dimensions={0}, use_global_device_ids=true | all-gather | bytes 655360 | tf_op jit(solution)/shard_map/all_gather | solution.py:527
  91.9 9.4 %last.1 = f32[4,32,256]{2,1,0:T(8,128)} custom-call(s32[2]{0:T(128)S(1)} %pad_add_fusion.where_ref, f32[4,16,16,128]{3,2,1,0:T(8,128)S(1)} %bitcast.8, f32[8,48,256]{2,1,0:T(8,128)S(1)} %get-tuple-element.19.qwin_ref, f32[8,48,256]{2,1,0:T(8,128)S(1)} %get-tuple-element.20.uwin_ref), custom_call_target="tpu_custom_call" | custom-call | tf_op jit(solution)/shard_map/last/pallas_call | solution.py:458
  (1 shorter events, 0.0 us)
Async XLA Ops:
  0.6 0.9 copy-start
  1.5 0.7 copy-start.1
  2.3 10.7 %collective-permute-start = (f32[136,256]{1,0:T(8,128)S(1)}, f32[136,256]{1,0:T(8,128)S(1)}, u32[]{:S(2)}, u32[]{:S(2)}) collective-permute-start(f32[136,256]{1,0:T(8,128)S(1)} %pack.1.own_ref), channel_id=1, source_target_pairs={{0,16},{4,20},{8,24},{12,28},{16,0},{20,4},{24,8},{28,12},{1,17},{... | collective-permute-start | bytes 417800 | tf_op jit(solution)/shard_map/ppermute | solution.py:481
  13.1 10.6 %collective-permute-start.3 = (f32[2,136,256]{2,1,0:T(8,128)S(1)}, f32[2,136,256]{2,1,0:T(8,128)S(1)}, u32[]{:S(2)}, u32[]{:S(2)}) collective-permute-start(f32[2,136,256]{2,1,0:T(8,128)S(1)} %pad_maximum_fusion), channel_id=1, source_target_pairs={{0,12},{4,8},{8,4},{12,0},{16,28},{20,24},{24,20},{28,16},{1,13},{... | collective-permute-start | bytes 835592 | tf_op jit(solution)/shard_map/ppermute | solution.py:481
  14.8 12.9 %collective-permute-start.2 = (f32[2,136,256]{2,1,0:T(8,128)S(1)}, f32[2,136,256]{2,1,0:T(8,128)S(1)}, u32[]{:S(2)}, u32[]{:S(2)}) collective-permute-start(f32[2,136,256]{2,1,0:T(8,128)S(1)} %pad_maximum_fusion), channel_id=1, source_target_pairs={{0,8},{4,12},{8,0},{12,4},{16,24},{20,28},{24,16},{28,20},{1,9},{5... | collective-permute-start | bytes 835592 | tf_op jit(solution)/shard_map/ppermute | solution.py:481
  16.1 11.7 %collective-permute-start.1 = (f32[2,136,256]{2,1,0:T(8,128)S(1)}, f32[2,136,256]{2,1,0:T(8,128)S(1)}, u32[]{:S(2)}, u32[]{:S(2)}) collective-permute-start(f32[2,136,256]{2,1,0:T(8,128)S(1)} %pad_maximum_fusion), channel_id=1, source_target_pairs={{0,4},{4,0},{8,12},{12,8},{16,20},{20,16},{24,28},{28,24},{1,5},{5... | collective-permute-start | bytes 835592 | tf_op jit(solution)/shard_map/ppermute | solution.py:481
  27.8 0.7 copy-start.2
  28.5 0.7 copy-start.3
  30.1 1.6 %collective-permute-start.4 = (f32[33,8,256]{2,1,0:T(8,128)S(1)}, f32[33,8,256]{2,1,0:T(8,128)S(1)}, u32[]{:S(2)}, u32[]{:S(2)}) collective-permute-start(f32[33,8,256]{2,1,0:T(8,128)S(1)} %get-tuple-element.12), channel_id=1, source_target_pairs={{0,1},{2,3},{1,0},{3,2},{4,5},{6,7},{5,4},{7,6},{8,9},{10,11},{9,8... | collective-permute-start | bytes 811016 | tf_op jit(solution)/shard_map/ppermute | solution.py:497
  30.1 1.5 %collective-permute-start.5 = (f32[33,8,256]{2,1,0:T(8,128)S(1)}, f32[33,8,256]{2,1,0:T(8,128)S(1)}, u32[]{:S(2)}, u32[]{:S(2)}) collective-permute-start(f32[33,8,256]{2,1,0:T(8,128)S(1)} %get-tuple-element.13), channel_id=1, source_target_pairs={{1,2},{2,1},{5,6},{6,5},{9,10},{10,9},{13,14},{14,13},{17,18},{18,... | collective-permute-start | bytes 811016 | tf_op jit(solution)/shard_map/ppermute | solution.py:498

commit v2 on v1

v2 whole, which is shorter than its diff:
```python
from functools import partial

import jax
import jax.numpy as jnp
from jax import lax
from jax.experimental import pallas as pl
from jax.experimental.pallas import tpu as pltpu
from jax.sharding import PartitionSpec as P

CYCLES = 2
OMEGA = 0.8
W = OMEGA / 6.0
KEEP = 1.0 - OMEGA
HALO = 8
LANES = 128
UNROLL = 4


def is_coarsest(shape):
    return min(shape) <= 4 or any((d % 2 for d in shape))


def lane_iota(shape):
    return lax.broadcasted_iota(jnp.int32, shape, len(shape) - 1)


def row_iota(shape):
    return lax.broadcasted_iota(jnp.int32, shape, len(shape) - 2)


def x_other(values, odd):
    lane = lane_iota(values.shape)
    if odd:
        return jnp.where(lane == LANES - 1, 0.0, pltpu.roll(values, LANES - 1, 1))
    return jnp.where(lane == 0, 0.0, pltpu.roll(values, 1, 1))


def y_other(values, odd):
    return pltpu.roll(values, values.shape[0] - 1 if odd else 1, 0)


def swept(below, here, above, q, c):
    across, along = here[c ^ 1], here[c ^ 2]
    near = (below + above) + (across + x_other(across, c & 1))
    near = near + (along + y_other(along, c >> 1))
    return KEEP * here[c] + W * near + q


def parts(ref, z):
    return [ref[z, c] for c in range(4)]


def halo_mask(pencil, pencils):
    row = row_iota((8, LANES))
    above = jnp.where(pencil < pencils - 1, 1.0, 0.0)
    below = jnp.where(pencil > 0, 1.0, 0.0)
    return jnp.where(row < 4, above, below)


def put(ref, z, c, values, mask):
    own = values.shape[0] - 8
    ref[z, c, pl.ds(0, own), :] = values[:own]
    ref[z, c, pl.ds(own, 8), :] = values[own:] * mask


def pair_rows(ref, count):
    return ref[pl.ds(0, count, stride=2), :] + ref[pl.ds(1, count, stride=2), :]


def spread_rows(ref, values):
    count = values.shape[0]
    ref[pl.ds(0, count, stride=2), :] = values
    ref[pl.ds(1, count, stride=2), :] = values


def index_pair(rows, columns):
    return (
        lax.broadcasted_iota(jnp.int32, (rows, columns), 0),
        lax.broadcasted_iota(jnp.int32, (rows, columns), 1),
    )


def chosen(where, value):
    return jnp.where(where, value, 0.0).astype(jnp.bfloat16)


def halving_matrix():
    i, j = index_pair(LANES, LANES)
    return chosen(i // 2 == j, 0.5)


def doubling_matrix():
    i, j = index_pair(LANES, LANES)
    return chosen(i == j // 2, 1.0)


def splitting_matrix():
    i, j = index_pair(2 * LANES, 2 * LANES)
    return chosen(i == 2 * (j % LANES) + j // LANES, 1.0)


def merging_matrix():
    i, j = index_pair(2 * LANES, 2 * LANES)
    return chosen(j == 2 * (i % LANES) + i // LANES, 1.0)


def mm(a, b):
    high = a.astype(jnp.bfloat16)
    rest = a - high.astype(jnp.float32)
    middle = rest.astype(jnp.bfloat16)
    low = (rest - middle.astype(jnp.float32)).astype(jnp.bfloat16)

    def dot(x):
        return jnp.dot(x, b, preferred_element_type=jnp.float32)

    return dot(high) + (dot(middle) + dot(low))


def flat_sweep(u, q, shape):
    zs, ys, xs = shape
    rows = zs * ys
    zero = jnp.zeros((ys, LANES), jnp.float32)
    below = jnp.concatenate([zero, u[: rows - ys]], axis=0)
    above = jnp.concatenate([u[ys:], zero], axis=0)
    y = row_iota(u.shape) % ys
    lane = lane_iota(u.shape)
    down = jnp.where(y == 0, 0.0, pltpu.roll(u, 1, 0))
    up = jnp.where(y == ys - 1, 0.0, pltpu.roll(u, rows - 1, 0))
    left = pltpu.roll(u, 1, 1)
    right = pltpu.roll(u, LANES - 1, 1)
    out = KEEP * u + W * ((below + above) + (down + up) + (left + right)) + q
    return jnp.where(lane < xs, out, 0.0)


def flat_vcycle(q, shape, tmp_ref):
    if is_coarsest(shape):
        u = q
        for _ in range(7):
            u = flat_sweep(u, q, shape)
        return u
    zs, ys, xs = shape
    u = flat_sweep(q, q, shape)
    change = flat_sweep(u, q, shape) - u
    pairs = [
        change[2 * z * ys : (2 * z + 1) * ys] + change[(2 * z + 1) * ys : (2 * z + 2) * ys]
        for z in range(zs // 2)
    ]
    half = zs * ys // 2
    tmp_ref[pl.ds(0, half), :] = jnp.concatenate(pairs, axis=0)
    coarse = mm(pair_rows(tmp_ref, half // 2), halving_matrix())
    coarse_shape = (zs // 2, ys // 2, xs // 2)
    e = flat_vcycle(coarse, coarse_shape, tmp_ref)
    spread_rows(tmp_ref, mm(e, doubling_matrix()))
    wide = tmp_ref[pl.ds(0, half), :]
    planes = []
    for z in range(zs // 2):
        planes += [wide[z * ys : (z + 1) * ys]] * 2
    u = u + jnp.concatenate(planes, axis=0)
    u = flat_sweep(u, q, shape)
    return flat_sweep(u, q, shape)


def solve_level_one(gathered_ref, q_ref, a_ref, b_ref, tmp_ref, shape):
    zs, ys, xs = shape
    pencils, _, part, _ = gathered_ref.shape
    inner = pl.ds(HALO, ys)
    row = row_iota((ys, LANES))
    lane = lane_iota((ys, LANES))
    a_ref[...] = jnp.zeros_like(a_ref)
    b_ref[...] = jnp.zeros_like(b_ref)
    q_ref[pl.ds(0, 1)] = jnp.zeros((1,) + q_ref.shape[1:], jnp.float32)
    q_ref[pl.ds(zs + 1, 1)] = jnp.zeros((1,) + q_ref.shape[1:], jnp.float32)
    for part_index in range(pencils):
        q_ref[pl.ds(1, zs), pl.ds(HALO + part_index * part, part), :] = gathered_ref[part_index]

    def sweep_plane(src, z):
        here = src[z, inner, :]
        below = src[z - 1, inner, :]
        above = src[z + 1, inner, :]
        down = jnp.where(row == 0, 0.0, pltpu.roll(here, 1, 0))
        up = jnp.where(row == ys - 1, 0.0, pltpu.roll(here, ys - 1, 0))
        left = jnp.where(lane == 0, 0.0, pltpu.roll(here, 1, 1))
        right = jnp.where(lane == LANES - 1, 0.0, pltpu.roll(here, LANES - 1, 1))
        near = (below + above) + (down + up) + (left + right)
        return here, KEEP * here + W * near + q_ref[z, inner, :]

    def sweep(src, dst):
        def body(z, carry):
            dst[z, inner, :] = sweep_plane(src, z)[1]
            return carry

        lax.fori_loop(1, zs + 1, body, 0, unroll=UNROLL)

    sweep(q_ref, a_ref)

    def restrict(z, carry):
        h0, s0 = sweep_plane(a_ref, 2 * z + 1)
        h1, s1 = sweep_plane(a_ref, 2 * z + 2)
        tmp_ref[pl.ds(pl.multiple_of(z * ys, ys), ys), :] = (s0 - h0) + (s1 - h1)
        return carry

    lax.fori_loop(0, zs // 2, restrict, 0, unroll=2)
    coarse_shape = (zs // 2, ys // 2, xs // 2)
    coarse = mm(
        pair_rows(tmp_ref, coarse_shape[0] * coarse_shape[1]), halving_matrix()
    )
    e = flat_vcycle(coarse, coarse_shape, tmp_ref)
    spread_rows(tmp_ref, mm(e, doubling_matrix()))

    def correct(z, carry):
        wide = tmp_ref[pl.ds(pl.multiple_of(z * ys, ys), ys), :]
        a_ref[2 * z + 1, inner, :] = a_ref[2 * z + 1, inner, :] + wide
        a_ref[2 * z + 2, inner, :] = a_ref[2 * z + 2, inner, :] + wide
        return carry

    lax.fori_loop(0, zs // 2, correct, 0, unroll=2)
    sweep(a_ref, b_ref)
    sweep(b_ref, a_ref)


def pack_kernel(potential_ref, store_ref, out_ref, even_ref, odd_ref):
    depth, width, columns = potential_ref.shape
    slots = store_ref.shape[0]
    part = width // 2
    split = mm(potential_ref[...].reshape(depth * width, columns), splitting_matrix())
    even_ref[...] = split[:, :LANES]
    odd_ref[...] = split[:, LANES:]
    for z in range(depth):
        for c in range(4):
            ref = odd_ref if c & 1 else even_ref
            spot = pl.ds((4 * z + c) * part, part)
            out_ref[spot, :] = ref[pl.ds(z * width + (c >> 1), part, stride=2), :]
    base = depth * width * 2
    for slot in range(slots):
        for side in range(2):
            spot = pl.ds(base + side * depth, depth)
            out_ref[spot, pl.ds(slot * width, width)] = store_ref[slot, side]


def blocks_of(own_ref, far_ref, others):
    out = [(0, own_ref, None), (4, far_ref, None)]
    for offset, ref in others:
        out += [(offset, ref, 0), (offset ^ 4, ref, 1)]
    return out


def block_rows(ref, index, start, count):
    if index is None:
        return ref[pl.ds(start, count), :]
    return ref[index, pl.ds(start, count), :]


def ends(load, first, second, part, low_half):
    head = jnp.where(low_half, load(first, 8), pltpu.roll(load(second, 8), 4, 0))
    tail = jnp.where(
        low_half, pltpu.roll(load(first + part - 8, 8), 4, 0), load(second + part - 8, 8)
    )
    return head, tail


def edges_kernel(
    scalar_ref, own_ref, far_ref, r1_ref, r2_ref, r3_ref,
    even_ref, odd_ref, faces_ref, store_ref, rows_ref, *, depth, width, slabs
):
    slab = scalar_ref[0]
    pencil = scalar_ref[1]
    planes = slabs * depth
    part = width // 2
    is_even = (pencil % 2) == 0
    low_half = row_iota((8, LANES)) < 4
    blocks = blocks_of(own_ref, far_ref, [(1, r1_ref), (2, r2_ref), (3, r3_ref)])
    base = depth * width * 2
    for offset, ref, index in blocks:
        target = slab ^ offset
        store_ref[target] = block_rows(ref, index, base, 8)
        for z in range(depth):
            for t in range(2):
                head, tail = ends(
                    partial(block_rows, ref, index),
                    (4 * z + 2 * t) * part, (4 * z + 2 * t + 1) * part, part, low_half,
                )
                even_ref[2 * (target * depth + z) + t] = jnp.where(is_even, tail, head)
                odd_ref[2 * (target * depth + z) + t] = jnp.where(is_even, head, tail)
    rows_ref[...] = jnp.zeros_like(rows_ref)
    for s in range(slabs):
        tile = store_ref[scalar_ref[2 + s]]
        slot = scalar_ref[2 + slabs + s]
        picked = jnp.zeros((8, width), jnp.float32)
        for k in range(LANES // width):
            picked = jnp.where(slot == k, tile[:, k * width : (k + 1) * width], picked)
        rows_ref[pl.ds(s * depth, depth), pl.ds(0, width)] = picked[:depth]
        rows_ref[pl.ds(planes + s * depth, depth), pl.ds(0, width)] = picked[depth:]
    rows_ref[...] = rows_ref[...].T
    faces_ref[pl.ds(0, part), :] = rows_ref[pl.ds(0, part, stride=2), :]
    faces_ref[pl.ds(part, part), :] = rows_ref[pl.ds(1, part, stride=2), :]
    head, tail = ends(partial(block_rows, faces_ref, None), 0, part, part, low_half)
    even_ref[2 * planes] = jnp.where(is_even, tail, head)
    odd_ref[2 * planes] = jnp.where(is_even, head, tail)


def halo_tiles(even_ref, odd_ref, index, is_even, low_half):
    first = even_ref[index]
    second = odd_ref[index]
    above = jnp.where(is_even, first, second)
    below = jnp.where(is_even, second, first)
    return (
        jnp.where(low_half, above, pltpu.roll(below, 4, 0)),
        jnp.where(low_half, pltpu.roll(above, 4, 0), below),
    )


def join_planes(load, out_ref, left_ref, right_ref, depth, width):
    part = width // 2
    for z in range(depth):
        for c in range(4):
            ref = right_ref if c & 1 else left_ref
            ref[pl.ds(z * width + (c >> 1), part, stride=2), :] = load(z, c)
    rows = depth * width
    both = jnp.concatenate([left_ref[pl.ds(0, rows), :], right_ref[pl.ds(0, rows), :]], axis=1)
    out_ref[...] = mm(both, merging_matrix()).reshape(depth, width, 2 * LANES)


def first_kernel(
    scalar_ref, own_ref, far_ref, r1_ref, r2_ref, r3_ref, even_ref, odd_ref, faces_ref,
    source_ref, q_ref, u_ref, coarse_ref, p_ref, f_ref, s_ref, left_ref, right_ref,
    *, depth, width, pencils
):
    slab = scalar_ref[0]
    pencil = scalar_ref[1]
    planes = p_ref.shape[0] - 2
    part = width // 2
    is_even = (pencil % 2) == 0
    low_half = row_iota((8, LANES)) < 4
    mask = halo_mask(pencil, pencils)
    blank = jnp.zeros(p_ref.shape[1:], jnp.float32)
    p_ref[0] = blank
    p_ref[planes + 1] = blank
    for ref in (q_ref, u_ref):
        for z in (0, 1, planes + 2, planes + 3):
            ref[z] = blank
    for offset, ref, index in blocks_of(own_ref, far_ref, [(1, r1_ref), (2, r2_ref), (3, r3_ref)]):
        target = (slab ^ offset) * depth + 1
        for z in range(depth):
            for c in range(4):
                p_ref[target + z, c, pl.ds(0, part), :] = block_rows(
                    ref, index, (4 * z + c) * part, part
                )

    def edges(z, carry):
        for t in range(2):
            first, second = halo_tiles(even_ref, odd_ref, 2 * z + t, is_even, low_half)
            p_ref[z + 1, 2 * t, pl.ds(part, 8), :] = first
            p_ref[z + 1, 2 * t + 1, pl.ds(part, 8), :] = second
        return carry

    lax.fori_loop(0, planes, edges, 0, unroll=UNROLL)
    first, second = halo_tiles(even_ref, odd_ref, 2 * planes, is_even, low_half)
    f_ref[0, pl.ds(0, part), :] = faces_ref[pl.ds(0, part), :]
    f_ref[0, pl.ds(part, 8), :] = first
    f_ref[1, pl.ds(0, part), :] = faces_ref[pl.ds(part, part), :]
    f_ref[1, pl.ds(part, 8), :] = second
    lane = lane_iota((part + 8, LANES))

    def hessian(z, carry):
        below = parts(p_ref, z)
        here = parts(p_ref, z + 1)
        above = parts(p_ref, z + 2)
        rise = [a - b for a, b in zip(above, below)]
        y_sum, y_rise, yz_rise = [], [], []
        for c in range(4):
            odd = c >> 1
            same, other = here[c ^ 2], y_other(here[c ^ 2], odd)
            y_sum.append(same + other)
            y_rise.append(other - same if odd else same - other)
            same, other = rise[c ^ 2], y_other(rise[c ^ 2], odd)
            yz_rise.append(other - same if odd else same - other)
        for c in range(4):
            odd = c & 1
            same, other = here[c ^ 1], x_other(here[c ^ 1], odd)
            twice = 2.0 * here[c]
            pxx = same + other - twice
            pyy = y_sum[c] - twice
            pzz = below[c] + above[c] - twice
            same, other = rise[c ^ 1], x_other(rise[c ^ 1], odd)
            pxz = other - same if odd else same - other
            same, other = y_rise[c ^ 1], x_other(y_rise[c ^ 1], odd)
            pxy = other - same if odd else same - other
            pyz = yz_rise[c]
            cross = pxy * pxy + pxz * pxz + pyz * pyz
            source = pxx * pyy + (pxx + pyy) * pzz - 0.0625 * cross
            s_ref[z, c] = source[:part]
            face = f_ref[c >> 1]
            if odd:
                face = jnp.where(
                    lane == LANES - 1, pltpu.roll(face, LANES - 1 - planes - z, 1), 0.0
                )
            else:
                face = jnp.where(lane == 0, pltpu.roll(face, (LANES - z) & (LANES - 1), 1), 0.0)
            put(q_ref, z + 2, c, W * (face - source), mask)
        return carry

    lax.fori_loop(0, planes, hessian, 0, unroll=2)
    join_planes(
        lambda z, c: s_ref[slab * depth + z, c], source_ref, left_ref, right_ref, depth, width
    )

    def second_sweep(z, carry):
        here = parts(q_ref, z + 2)
        for c in range(4):
            new = swept(q_ref[z + 1, c], here, q_ref[z + 3, c], here[c], c)
            put(u_ref, z + 2, c, new, mask)
        return carry

    lax.fori_loop(0, planes, second_sweep, 0, unroll=UNROLL)
    restrict_window(u_ref, q_ref, coarse_ref, planes, part)


def restrict_window(u_ref, q_ref, coarse_ref, planes, part):
    def restrict(z, carry):
        total = None
        for at in (2 * z + 2, 2 * z + 3):
            here = parts(u_ref, at)
            for c in range(4):
                new = swept(u_ref[at - 1, c], here, u_ref[at + 1, c], q_ref[at, c], c)
                change = (new - here[c])[:part]
                total = change if total is None else total + change
        coarse_ref[pl.ds(pl.multiple_of(z * part, part), part), :] = 0.5 * total
        return carry

    lax.fori_loop(0, planes // 2, restrict, 0, unroll=2)


def coarse_window(v_ref, z, pencil, part):
    start = pl.multiple_of(pencil * part, part)
    own = v_ref[z, pl.ds(start + HALO, part), :]
    above = v_ref[z, pl.ds(start + HALO + part, 8), :]
    below = v_ref[z, pl.ds(start, 8), :]
    tile = jnp.where(row_iota((8, LANES)) < 4, above, below)
    return jnp.concatenate([own, tile], axis=0)


def middle_kernel(
    scalar_ref, gathered_ref, q_ref, u_ref, qwin_ref, uwin_ref, coarse_ref,
    q1_ref, a1_ref, b1_ref, tmp_ref, a_ref, b_ref, *, depth, width, pencils, shape
):
    slab = scalar_ref[0]
    pencil = scalar_ref[1]
    planes = a_ref.shape[0] - 4
    part = width // 2
    mask = halo_mask(pencil, pencils)
    solve_level_one(gathered_ref, q1_ref, a1_ref, b1_ref, tmp_ref, shape)
    blank = jnp.zeros(a_ref.shape[1:], jnp.float32)
    for ref in (a_ref, b_ref):
        for z in (0, 1, planes + 2, planes + 3):
            ref[z] = blank

    def correct(z, carry):
        wide = coarse_window(a1_ref, z + 1, pencil, part)
        for at in (2 * z + 2, 2 * z + 3):
            for c in range(4):
                a_ref[at, c] = u_ref[at, c] + wide
        return carry

    lax.fori_loop(0, planes // 2, correct, 0, unroll=2)

    def sweep(src, dst):
        def body(z, carry):
            here = parts(src, z + 2)
            for c in range(4):
                new = swept(src[z + 1, c], here, src[z + 3, c], q_ref[z + 2, c], c)
                put(dst, z + 2, c, new, mask)
            return carry

        lax.fori_loop(0, planes, body, 0, unroll=UNROLL)

    sweep(a_ref, b_ref)
    sweep(b_ref, a_ref)
    sweep(a_ref, b_ref)
    sweep(b_ref, a_ref)
    restrict_window(a_ref, q_ref, coarse_ref, planes, part)
    for z in range(depth + 4):
        qwin_ref[z] = q_ref[slab * depth + z]
        uwin_ref[z] = a_ref[slab * depth + z]


def last_kernel(
    scalar_ref, gathered_ref, qwin_ref, uwin_ref, out_ref,
    q1_ref, a1_ref, b1_ref, tmp_ref, a_ref, b_ref, left_ref, right_ref,
    *, depth, width, pencils, shape
):
    slab = scalar_ref[0]
    pencil = scalar_ref[1]
    planes = shape[0] * 2
    part = width // 2
    mask = halo_mask(pencil, pencils)
    solve_level_one(gathered_ref, q1_ref, a1_ref, b1_ref, tmp_ref, shape)
    for z in range(depth // 2 + 2):
        wide = coarse_window(a1_ref, slab * (depth // 2) + z, pencil, part)
        for at in (2 * z, 2 * z + 1):
            for c in range(4):
                a_ref[at, c] = uwin_ref[at, c] + wide
    for z in range(1, depth + 3):
        at = slab * depth - 2 + z
        live = jnp.where((at >= 0) & (at < planes), 1.0, 0.0)
        here = parts(a_ref, z)
        for c in range(4):
            new = swept(a_ref[z - 1, c], here, a_ref[z + 1, c], qwin_ref[z, c], c)
            put(b_ref, z, c, live * new, mask)
    done = {}
    for z in range(2, depth + 2):
        here = parts(b_ref, z)
        for c in range(4):
            new = swept(b_ref[z - 1, c], here, b_ref[z + 1, c], qwin_ref[z, c], c)
            done[z - 2, c] = new[:part]
    join_planes(lambda z, c: done[z, c], out_ref, left_ref, right_ref, depth, width)


def vmem():
    return pl.BlockSpec(memory_space=pltpu.VMEM)


def smem():
    return pl.BlockSpec(memory_space=pltpu.SMEM)


def arr(*shape):
    return jax.ShapeDtypeStruct(shape, jnp.float32)


def buf(*shape):
    return pltpu.VMEM(shape, jnp.float32)


def call(kernel, name, scalars, args, outs, scratch=()):
    return pl.pallas_call(
        kernel,
        out_shape=outs,
        in_specs=[smem()] * len(scalars) + [vmem()] * len(args),
        out_specs=jax.tree.map(lambda _: vmem(), outs),
        scratch_shapes=list(scratch),
        compiler_params=pltpu.CompilerParams(vmem_limit_bytes=48 << 20),
        name=name,
    )(*scalars, *args)


def windowed(potential, parent_store, face_owner, face_offset):
    depth, width, columns = potential.shape
    slabs = lax.axis_size("slab")
    pencils = lax.axis_size("pencil")
    planes, height = slabs * depth, pencils * width
    part = width // 2
    rows = part + 8
    where = jnp.stack([lax.axis_index("slab"), lax.axis_index("pencil")]).astype(jnp.int32)
    scalars = jnp.concatenate([where, face_owner, face_offset])
    own = call(
        pack_kernel,
        "pack",
        [],
        [potential, parent_store],
        arr(depth * width * 2 + 8, LANES),
        [buf(depth * width, LANES), buf(depth * width, LANES)],
    )

    def swap(x, bits):
        return lax.ppermute(x, "slab", [(i, i ^ bits) for i in range(slabs)])

    far = swap(own, 4)
    both = jnp.stack([own, far])
    others = [swap(both, bits) for bits in (1, 2, 3)]
    message = arr(2 * planes + 1, 8, LANES)
    even, odd, faces = call(
        partial(edges_kernel, depth=depth, width=width, slabs=slabs),
        "edges",
        [scalars],
        [own, far, *others],
        (message, message, arr(width, LANES)),
        [buf(slabs, 8, LANES), buf(LANES, LANES)],
    )
    low_pairs = [(i, i + 1) for i in range(0, pencils - 1, 2)]
    high_pairs = [(i, i + 1) for i in range(1, pencils - 1, 2)]
    even = lax.ppermute(even, "pencil", low_pairs + [(j, i) for i, j in low_pairs])
    odd = lax.ppermute(odd, "pencil", high_pairs + [(j, i) for i, j in high_pairs])
    shape = (planes // 2, height // 2, columns // 2)
    coarse_part = arr(planes // 2 * part, LANES)
    field = (planes + 4, 4, rows, LANES)
    source, q, u, coarse = call(
        partial(first_kernel, depth=depth, width=width, pencils=pencils),
        "first",
        [scalars],
        [own, far, *others, even, odd, faces],
        (arr(depth, width, columns), arr(*field), arr(*field), coarse_part),
        [
            buf(planes + 2, 4, rows, LANES),
            buf(2, rows, LANES),
            buf(planes, 4, part, LANES),
            buf(depth * width, LANES),
            buf(depth * width, LANES),
        ],
    )
    level = (shape[0] + 2, shape[1] + 2 * HALO, LANES)
    level_scratch = [buf(*level), buf(*level), buf(*level), buf(shape[0] * shape[1], LANES)]

    def gather(x):
        whole = lax.all_gather(x, "pencil", axis=0, tiled=False)
        return whole.reshape(pencils, shape[0], part, LANES)

    sizes = dict(depth=depth, width=width, pencils=pencils, shape=shape)
    slim = (depth + 4, 4, rows, LANES)
    qwin, uwin, coarse = call(
        partial(middle_kernel, **sizes),
        "middle",
        [scalars],
        [gather(coarse), q, u],
        (arr(*slim), arr(*slim), coarse_part),
        level_scratch + [buf(*field), buf(*field)],
    )
    solved = call(
        partial(last_kernel, **sizes),
        "last",
        [scalars],
        [gather(coarse), qwin, uwin],
        arr(depth, width, columns),
        level_scratch
        + [buf(*slim), buf(*slim), buf(depth * width, LANES), buf(depth * width, LANES)],
    )
    return solved, source


def fits_window(potential, parent_store):
    depth, width, columns = potential.shape
    slabs = lax.axis_size("slab")
    pencils = lax.axis_size("pencil")
    planes = slabs * depth
    return (
        slabs == 8
        and pencils % 2 == 0
        and depth == 4
        and columns == 2 * LANES
        and width == 32
        and parent_store.shape[0] * width == LANES
        and 2 * planes <= LANES
        and pencils <= 8
    )


def padded(cells, sides, width):
    for axis, dim in sides:
        count = lax.axis_size(axis)
        ends = count - 1
        head = lax.slice_in_dim(cells, 0, width, axis=dim)
        tail = lax.slice_in_dim(cells, cells.shape[dim] - width, cells.shape[dim], axis=dim)
        cells = jnp.concatenate(
            [
                lax.ppermute(tail, axis, [(i, (i + 1) % count) for i in range(ends)]),
                cells,
                lax.ppermute(head, axis, [((i + 1) % count, i) for i in range(ends)]),
            ],
            axis=dim,
        )
    return cells


def hessian_source(p):
    c = p[1:-1, 1:-1, 1:-1]
    pxx = p[1:-1, 1:-1, 2:] + p[1:-1, 1:-1, :-2] - 2.0 * c
    pyy = p[1:-1, 2:, 1:-1] + p[1:-1, :-2, 1:-1] - 2.0 * c
    pzz = p[2:, 1:-1, 1:-1] + p[:-2, 1:-1, 1:-1] - 2.0 * c
    pxy = 0.25 * (p[1:-1, 2:, 2:] - p[1:-1, :-2, 2:] - p[1:-1, 2:, :-2] + p[1:-1, :-2, :-2])
    pxz = 0.25 * (p[2:, 1:-1, 2:] - p[:-2, 1:-1, 2:] - p[2:, 1:-1, :-2] + p[:-2, 1:-1, :-2])
    pyz = 0.25 * (p[2:, 2:, 1:-1] - p[:-2, 2:, 1:-1] - p[2:, :-2, 1:-1] + p[:-2, :-2, 1:-1])
    return pxx * pyy + pxx * pzz + pyy * pzz - pxy * pxy - pxz * pxz - pyz * pyz


def apply_padded(p, level):
    c = p[1:-1, 1:-1, 1:-1]
    near = p[2:, 1:-1, 1:-1] + p[:-2, 1:-1, 1:-1]
    near = near + p[1:-1, 2:, 1:-1] + p[1:-1, :-2, 1:-1]
    near = near + p[1:-1, 1:-1, 2:] + p[1:-1, 1:-1, :-2]
    return (6.0 * c - near) * 0.25**level


def step_weight(level):
    return OMEGA / 6.0 * 4.0**level


def sweep_whole(u, rhs, level):
    return u + step_weight(level) * (rhs - apply_padded(jnp.pad(u, 1), level))


def restrict(r):
    a, b, c = r.shape
    return r.reshape(a // 2, 2, b // 2, 2, c // 2, 2).mean(axis=(1, 3, 5))


def prolong(e):
    a, b, c = e.shape
    return jnp.broadcast_to(e[:, None, :, None, :, None], (a, 2, b, 2, c, 2)).reshape(
        2 * a, 2 * b, 2 * c
    )


def vcycle(u, rhs, level):
    if is_coarsest(rhs.shape):
        for sweep_count in range(8):
            u = sweep_whole(u, rhs, level)
        return u
    u = sweep_whole(u, rhs, level)
    u = sweep_whole(u, rhs, level)
    resid = rhs - apply_padded(jnp.pad(u, 1), level)
    coarse = restrict(resid)
    correction = vcycle(jnp.zeros_like(coarse), coarse, level + 1)
    u = u + prolong(correction)
    u = sweep_whole(u, rhs, level)
    u = sweep_whole(u, rhs, level)
    return u


def widen_x(p):
    return jnp.pad(p, ((0, 0), (0, 0), (1, 1)))


def rim_one(u):
    return widen_x(padded(u, (("slab", 0), ("pencil", 1)), 1))


def coarse_solve(rhs, level):
    width = rhs.shape[1]
    columns = rhs.shape[2]
    whole = lax.all_gather(rhs, ("slab", "pencil"), axis=0, tiled=True)
    whole = whole.reshape(lax.axis_size("slab"), lax.axis_size("pencil") * width, columns)
    solved = vcycle(jnp.zeros_like(whole), whole, level)
    start_y = lax.axis_index("pencil") * width
    return lax.dynamic_slice(
        solved, (lax.axis_index("slab"), start_y, jnp.int32(0)), (1, width, columns)
    )


def split_vcycle(u, rhs, level, from_zero):
    if rhs.shape[0] == 1:
        return coarse_solve(rhs, level)
    weight = step_weight(level)
    if from_zero:
        u = weight * rhs
    else:
        u = u + weight * (rhs - apply_padded(rim_one(u), level))
    u = u + weight * (rhs - apply_padded(rim_one(u), level))
    resid = rhs - apply_padded(rim_one(u), level)
    correction = split_vcycle(None, restrict(resid), level + 1, True)
    u = u + prolong(correction)
    u = u + weight * (rhs - apply_padded(rim_one(u), level))
    u = u + weight * (rhs - apply_padded(rim_one(u), level))
    return u


def plain(potential, parent_store, face_owner, face_offset):
    depth, width, columns = potential.shape
    grown = widen_x(padded(potential, (("slab", 0), ("pencil", 1)), 1))
    source = hessian_source(grown)
    slab_index = lax.axis_index("slab")
    wanted = face_owner[slab_index] * parent_store.shape[0] + face_offset[slab_index]
    piece = lax.all_gather(parent_store, "slab", axis=0, tiled=True)
    labels = jnp.arange(piece.shape[0], dtype=jnp.int32)
    match = labels == wanted
    faces = jnp.sum(jnp.where(match[:, None, None, None], piece, 0.0), axis=0)
    rhs = -source
    rhs = rhs.at[:, :, 0].add(faces[0])
    rhs = rhs.at[:, :, columns - 1].add(faces[1])
    solved = jnp.zeros_like(rhs)
    for cycle in range(CYCLES):
        solved = split_vcycle(solved, rhs, 0, cycle == 0)
    return (solved, source)


def on_device(potential, parent_store, face_owner, face_offset):
    if fits_window(potential, parent_store):
        return windowed(potential, parent_store, face_owner, face_offset)
    return plain(potential, parent_store, face_owner, face_offset)


def solution(mesh):
    in_specs = (P("slab", "pencil", None), P("slab", None, None, "pencil"), P(), P())
    out_specs = (P("slab", "pencil", None), P("slab", "pencil", None))
    return jax.shard_map(
        on_device, mesh=mesh, in_specs=in_specs, out_specs=out_specs, check_vma=False
    )
```

time: 102 us -> 73.8 us (0.72)
  Pallas kernels: 50 us -> 23.9 us
  local copies, waits for them, and re-layouts: 2.92 us -> 1.61 us
  waiting for transfers between devices: 18.7 us -> 17.4 us
    pallas_call x5, Pallas kernels: 50 us -> 23.9 us  [call(): pl.pallas_call(kernel, out_shape=outs, in_specs=[smem()] * len(scalars) +...]
    unnamed x8 -> x4, local copies, waits for them, and re-layouts: 2.92 us -> 1.61 us
    ppermute x4, waiting for transfers between devices: 17.8 us -> 16.6 us  [swap(): return lax.ppermute(x, 'slab', [(i, i ^ bits) for i in range(slabs)])]
  transfers between devices with their start and end apart: 6 -> 6, of which waited for: 5 -> 5; matrix products, arithmetic and copies ran while one was open for 0% -> 1% of each run, Pallas kernels for 0% -> 0%
where the time goes in v2:
time: 73.8 us; the launch traced here: 73.4 us
  Pallas kernels  23.9 us (32%)
  blocking collectives  20.5 us (28%)
  waiting for transfers between devices  17.4 us (24%)
  starting transfers between devices  8.41 us (11%)
  local copies, waits for them, and re-layouts  1.61 us (2%)
  other arithmetic  0.78 us (1%)
    pallas_call x5, Pallas kernels, call(): pl.pallas_call(kernel, out_shape=outs, in_specs=[smem()] * len(scalars) +...  23.9 us
    all_gather x2, blocking collectives, gather(): whole = lax.all_gather(x, 'pencil', axis=0, tiled=False)  20.5 us
    ppermute x4, waiting for transfers between devices, swap(): return lax.ppermute(x, 'slab', [(i, i ^ bits) for i in range(slabs)])  16.6 us
    ppermute x4, starting transfers between devices, swap(): return lax.ppermute(x, 'slab', [(i, i ^ bits) for i in range(slabs)])  7.65 us
    unnamed x4, local copies, waits for them, and re-layouts  1.61 us
  transfers between devices with their start and end apart: 6, of which 5 were waited for; matrix products, arithmetic and copies ran while one was open for 1% of the time, Pallas kernels for 0%

profile of v2, /device:TPU:0, one launch (start us, length us, event | category | flops | bytes accessed | tf_op | source)
XLA Modules:
  0.0 73.4 jit_solution(13583644487892130718)
XLA Ops:
  0.6 0.0 copy-start
  0.6 0.9 %copy-done = f32[4,32,256]{2,1,0:T(8,128)S(1)} copy-done((f32[4,32,256]{2,1,0:T(8,128)S(1)}, f32[4,32,256]{2,1,0:T(8,128)}, u32[]{:S(2)}) %copy-start) | copy-done | bytes 131096
  1.5 0.0 copy-start.1
  1.5 0.7 copy-done.1
  2.3 0.2 pack.1.own_ref
  2.5 4.1 %collective-permute-start = (f32[264,128]{1,0:T(8,128)S(1)}, f32[264,128]{1,0:T(8,128)S(1)}, u32[]{:S(2)}, u32[]{:S(2)}) collective-permute-start(f32[264,128]{1,0:T(8,128)S(1)} %pack.1.own_ref), channel_id=1, source_target_pairs={{0,16},{4,20},{8,24},{12,28},{16,0},{20,4},{24,8},{28,12},{1,17},{... | collective-permute-start | bytes 405512 | tf_op jit(solution)/shard_map/ppermute | solution.py:565
  6.6 6.5 %collective-permute-done.far_ref = f32[264,128]{1,0:T(8,128)S(1)} collective-permute-done((f32[264,128]{1,0:T(8,128)S(1)}, f32[264,128]{1,0:T(8,128)S(1)}, u32[]{:S(2)}, u32[]{:S(2)}) %collective-permute-start) | collective-permute-done | bytes 135200 | tf_op jit(solution)/shard_map/ppermute | solution.py:565
  13.1 1.7 %collective-permute-start.3 = (f32[2,264,128]{2,1,0:T(8,128)S(1)}, f32[2,264,128]{2,1,0:T(8,128)S(1)}, u32[]{:S(2)}, u32[]{:S(2)}) collective-permute-start(f32[2,264,128]{2,1,0:T(8,128)S(1)} %pad_maximum_fusion), channel_id=1, source_target_pairs={{0,12},{4,8},{8,4},{12,0},{16,28},{20,24},{24,20},{28,16},{1,13},{... | collective-permute-start | bytes 811016 | tf_op jit(solution)/shard_map/ppermute | solution.py:565
  14.8 1.4 %collective-permute-start.2 = (f32[2,264,128]{2,1,0:T(8,128)S(1)}, f32[2,264,128]{2,1,0:T(8,128)S(1)}, u32[]{:S(2)}, u32[]{:S(2)}) collective-permute-start(f32[2,264,128]{2,1,0:T(8,128)S(1)} %pad_maximum_fusion), channel_id=1, source_target_pairs={{0,8},{4,12},{8,0},{12,4},{16,24},{20,28},{24,16},{28,20},{1,9},{5... | collective-permute-start | bytes 811016 | tf_op jit(solution)/shard_map/ppermute | solution.py:565
  16.2 0.5 collective-permute-start.1
  16.7 0.7 %pad_add_fusion.scalar_ref = s32[18]{0:T(128)S(1)} fusion(s32[8]{0:T(128)} %param.7, s32[8]{0:T(128)} %param.6, s32[1]{0:T(128)} %bitcast.1, s32[1]{0:T(128)} %bitcast), kind=kLoop, calls=%fused_computation.1 | loop fusion | flops 54 | bytes 144 | tf_op jit(solution)/shard_map/concatenate | solution.py:554
  17.4 6.1 %collective-permute-done.3.r3_ref = f32[2,264,128]{2,1,0:T(8,128)S(1)} collective-permute-done((f32[2,264,128]{2,1,0:T(8,128)S(1)}, f32[2,264,128]{2,1,0:T(8,128)S(1)}, u32[]{:S(2)}, u32[]{:S(2)}) %collective-permute-start.3) | collective-permute-done | bytes 270368 | tf_op jit(solution)/shard_map/ppermute | solution.py:565
  23.5 3.8 %collective-permute-done.2.r2_ref = f32[2,264,128]{2,1,0:T(8,128)S(1)} collective-permute-done((f32[2,264,128]{2,1,0:T(8,128)S(1)}, f32[2,264,128]{2,1,0:T(8,128)S(1)}, u32[]{:S(2)}, u32[]{:S(2)}) %collective-permute-start.2) | collective-permute-done | bytes 270368 | tf_op jit(solution)/shard_map/ppermute | solution.py:565
  27.4 0.2 collective-permute-done.1.r1_ref
  27.5 1.0 %edges.1 = (f32[65,8,128]{2,1,0:T(8,128)S(1)}, f32[65,8,128]{2,1,0:T(8,128)S(1)}, f32[32,128]{1,0:T(8,128)S(1)}) custom-call(s32[18]{0:T(128)S(1)} %pad_add_fusion.scalar_ref, f32[264,128]{1,0:T(8,128)S(1)} %pack.1.own_ref, f32[264,128]{1,0:T(8,128)S(1)} %collective-permute-done.far_ref, f32[2,264,128]{2,1,0:T(8,128)S(1)} %collective-permute-done.1.r1_ref, ...), custom_call_target="tpu_custom_call" | custom-call | tf_op jit(solution)/shard_map/edges/pallas_call | solution.py:535
  28.5 0.1 collective-permute-start.4
  28.6 0.7 collective-permute-start.5
  29.3 0.8 %collective-permute-done.4.even_ref = f32[65,8,128]{2,1,0:T(8,128)S(1)} collective-permute-done((f32[65,8,128]{2,1,0:T(8,128)S(1)}, f32[65,8,128]{2,1,0:T(8,128)S(1)}, u32[]{:S(2)}, u32[]{:S(2)}) %collective-permute-start.4) | collective-permute-done | bytes 266272 | tf_op jit(solution)/shard_map/ppermute | solution.py:581
  30.1 0.0 collective-permute-done.5.odd_ref
  30.1 6.3 %first.1 = (f32[4,32,256]{2,1,0:T(8,128)}, f32[36,4,24,128]{3,2,1,0:T(8,128)S(1)}, f32[36,4,24,128]{3,2,1,0:T(8,128)S(1)}, f32[256,128]{1,0:T(8,128)S(1)}) custom-call(s32[18]{0:T(128)S(1)} %pad_add_fusion.scalar_ref, f32[264,128]{1,0:T(8,128)S(1)} %pack.1.own_ref, f32[264,128]{1,0:T(8,128)S(1)} %collective-permute-done.far_ref, ...), custom_call_target="tpu_custom_call" | custom-call | tf_op jit(solution)/shard_map/first/pallas_call | solution.py:535
  36.4 13.2 %all-gather = f32[1024,128]{1,0:T(8,128)S(1)} all-gather(f32[256,128]{1,0:T(8,128)S(1)} %get-tuple-element.15), channel_id=2, replica_groups=mesh['slab'=8,'pencil'=4] {'pencil'}, dimensions={0}, use_global_device_ids=true | all-gather | bytes 655360 | tf_op jit(solution)/shard_map/all_gather | solution.py:604
  49.7 10.5 %middle.1 = (f32[8,4,24,128]{3,2,1,0:T(8,128)S(1)}, f32[8,4,24,128]{3,2,1,0:T(8,128)S(1)}, f32[256,128]{1,0:T(8,128)S(1)}) custom-call(s32[18]{0:T(128)S(1)} %pad_add_fusion.scalar_ref, f32[4,16,16,128]{3,2,1,0:T(8,128)S(1)} %bitcast.7, f32[36,4,24,128]{3,2,1,0:T(8,128)S(1)} %get-tuple-element.16.q_ref, f32[36,4,24,128]{3,2,1,0:T(8,128)S(1)} %get-tuple-element.17.u_ref), custom_call_target="tpu_custom_call" | custom-call | tf_op jit(solution)/shard_map/middle/pallas_call | solution.py:535
  60.2 7.3 %all-gather.1 = f32[1024,128]{1,0:T(8,128)S(1)} all-gather(f32[256,128]{1,0:T(8,128)S(1)} %get-tuple-element.18), channel_id=3, replica_groups=mesh['slab'=8,'pencil'=4] {'pencil'}, dimensions={0}, use_global_device_ids=true | all-gather | bytes 655360 | tf_op jit(solution)/shard_map/all_gather | solution.py:604
  67.5 5.9 %last.1 = f32[4,32,256]{2,1,0:T(8,128)} custom-call(s32[18]{0:T(128)S(1)} %pad_add_fusion.scalar_ref, f32[4,16,16,128]{3,2,1,0:T(8,128)S(1)} %bitcast.8, f32[8,4,24,128]{3,2,1,0:T(8,128)S(1)} %get-tuple-element.19.qwin_ref, f32[8,4,24,128]{3,2,1,0:T(8,128)S(1)} %get-tuple-element.20.uwin_ref), custom_call_target="tpu_custom_call" | custom-call | tf_op jit(solution)/shard_map/last/pallas_call | solution.py:535
  (1 shorter events, 0.0 us)
Async XLA Ops:
  0.6 0.9 %copy-start = (f32[4,32,256]{2,1,0:T(8,128)S(1)}, f32[4,32,256]{2,1,0:T(8,128)}, u32[]{:S(2)}) copy-start(f32[4,32,256]{2,1,0:T(8,128)} %potential_ref.1) | copy-start | bytes 393220
  1.5 0.7 copy-start.1
  2.5 10.6 %collective-permute-start = (f32[264,128]{1,0:T(8,128)S(1)}, f32[264,128]{1,0:T(8,128)S(1)}, u32[]{:S(2)}, u32[]{:S(2)}) collective-permute-start(f32[264,128]{1,0:T(8,128)S(1)} %pack.1.own_ref), channel_id=1, source_target_pairs={{0,16},{4,20},{8,24},{12,28},{16,0},{20,4},{24,8},{28,12},{1,17},{... | collective-permute-start | bytes 405512 | tf_op jit(solution)/shard_map/ppermute | solution.py:565
  13.1 10.4 %collective-permute-start.3 = (f32[2,264,128]{2,1,0:T(8,128)S(1)}, f32[2,264,128]{2,1,0:T(8,128)S(1)}, u32[]{:S(2)}, u32[]{:S(2)}) collective-permute-start(f32[2,264,128]{2,1,0:T(8,128)S(1)} %pad_maximum_fusion), channel_id=1, source_target_pairs={{0,12},{4,8},{8,4},{12,0},{16,28},{20,24},{24,20},{28,16},{1,13},{... | collective-permute-start | bytes 811016 | tf_op jit(solution)/shard_map/ppermute | solution.py:565
  14.8 12.5 %collective-permute-start.2 = (f32[2,264,128]{2,1,0:T(8,128)S(1)}, f32[2,264,128]{2,1,0:T(8,128)S(1)}, u32[]{:S(2)}, u32[]{:S(2)}) collective-permute-start(f32[2,264,128]{2,1,0:T(8,128)S(1)} %pad_maximum_fusion), channel_id=1, source_target_pairs={{0,8},{4,12},{8,0},{12,4},{16,24},{20,28},{24,16},{28,20},{1,9},{5... | collective-permute-start | bytes 811016 | tf_op jit(solution)/shard_map/ppermute | solution.py:565
  16.2 11.4 %collective-permute-start.1 = (f32[2,264,128]{2,1,0:T(8,128)S(1)}, f32[2,264,128]{2,1,0:T(8,128)S(1)}, u32[]{:S(2)}, u32[]{:S(2)}) collective-permute-start(f32[2,264,128]{2,1,0:T(8,128)S(1)} %pad_maximum_fusion), channel_id=1, source_target_pairs={{0,4},{4,0},{8,12},{12,8},{16,20},{20,16},{24,28},{28,24},{1,5},{5... | collective-permute-start | bytes 811016 | tf_op jit(solution)/shard_map/ppermute | solution.py:565
  28.5 1.6 %collective-permute-start.4 = (f32[65,8,128]{2,1,0:T(8,128)S(1)}, f32[65,8,128]{2,1,0:T(8,128)S(1)}, u32[]{:S(2)}, u32[]{:S(2)}) collective-permute-start(f32[65,8,128]{2,1,0:T(8,128)S(1)} %get-tuple-element.12), channel_id=1, source_target_pairs={{0,1},{2,3},{1,0},{3,2},{4,5},{6,7},{5,4},{7,6},{8,9},{10,11},{9,8... | collective-permute-start | bytes 798728 | tf_op jit(solution)/shard_map/ppermute | solution.py:581
  28.6 1.5 %collective-permute-start.5 = (f32[65,8,128]{2,1,0:T(8,128)S(1)}, f32[65,8,128]{2,1,0:T(8,128)S(1)}, u32[]{:S(2)}, u32[]{:S(2)}) collective-permute-start(f32[65,8,128]{2,1,0:T(8,128)S(1)} %get-tuple-element.13), channel_id=1, source_target_pairs={{1,2},{2,1},{5,6},{6,5},{9,10},{10,9},{13,14},{14,13},{17,18},{18,... | collective-permute-start | bytes 798728 | tf_op jit(solution)/shard_map/ppermute | solution.py:582

commit v3 on v2

--- a/solution.py
+++ b/solution.py
@@ -2,6 +2,7 @@
 
 import jax
 import jax.numpy as jnp
+import numpy as np
 from jax import lax
 from jax.experimental import pallas as pl
 from jax.experimental.pallas import tpu as pltpu
@@ -9,8 +10,8 @@
 
 CYCLES = 2
 OMEGA = 0.8
-W = OMEGA / 6.0
-KEEP = 1.0 - OMEGA
+W = float(np.float32(OMEGA / 6.0))
+KEEP = 1.0 - 6.0 * W
 HALO = 8
 LANES = 128
 UNROLL = 4
@@ -63,16 +64,6 @@
     ref[z, c, pl.ds(own, 8), :] = values[own:] * mask
 
 
-def pair_rows(ref, count):
-    return ref[pl.ds(0, count, stride=2), :] + ref[pl.ds(1, count, stride=2), :]
-
-
-def spread_rows(ref, values):
-    count = values.shape[0]
-    ref[pl.ds(0, count, stride=2), :] = values
-    ref[pl.ds(1, count, stride=2), :] = values
-
-
 def index_pair(rows, columns):
     return (
         lax.broadcasted_iota(jnp.int32, (rows, columns), 0),
@@ -84,24 +75,14 @@
     return jnp.where(where, value, 0.0).astype(jnp.bfloat16)
 
 
-def halving_matrix():
-    i, j = index_pair(LANES, LANES)
-    return chosen(i // 2 == j, 0.5)
-
-
-def doubling_matrix():
-    i, j = index_pair(LANES, LANES)
-    return chosen(i == j // 2, 1.0)
-
-
 def splitting_matrix():
     i, j = index_pair(2 * LANES, 2 * LANES)
-    return chosen(i == 2 * (j % LANES) + j // LANES, 1.0)
+    return chosen(i == 2 * (j & (LANES - 1)) + (j >= LANES).astype(jnp.int32), 1.0)
 
 
 def merging_matrix():
     i, j = index_pair(2 * LANES, 2 * LANES)
-    return chosen(j == 2 * (i % LANES) + i // LANES, 1.0)
+    return chosen(j == 2 * (i & (LANES - 1)) + (i >= LANES).astype(jnp.int32), 1.0)
 
 
 def mm(a, b):
@@ -116,77 +97,97 @@
     return dot(high) + (dot(middle) + dot(low))
 
 
-def flat_sweep(u, q, shape):
-    zs, ys, xs = shape
-    rows = zs * ys
-    zero = jnp.zeros((ys, LANES), jnp.float32)
-    below = jnp.concatenate([zero, u[: rows - ys]], axis=0)
-    above = jnp.concatenate([u[ys:], zero], axis=0)
-    y = row_iota(u.shape) % ys
-    lane = lane_iota(u.shape)
-    down = jnp.where(y == 0, 0.0, pltpu.roll(u, 1, 0))
-    up = jnp.where(y == ys - 1, 0.0, pltpu.roll(u, rows - 1, 0))
-    left = pltpu.roll(u, 1, 1)
-    right = pltpu.roll(u, LANES - 1, 1)
-    out = KEEP * u + W * ((below + above) + (down + up) + (left + right)) + q
-    return jnp.where(lane < xs, out, 0.0)
-
-
-def flat_vcycle(q, shape, tmp_ref):
+def pair_sum(values, distance, axis):
+    size = values.shape[axis]
+    at = lax.broadcasted_iota(jnp.int32, values.shape, axis)
+    ahead = pltpu.roll(values, size - distance, axis)
+    behind = pltpu.roll(values, distance, axis)
+    return values + jnp.where((at & distance) == 0, ahead, behind)
+
+
+def x_sides(values, distance):
+    lane = lane_iota(values.shape)
+    left = jnp.where(lane < distance, 0.0, pltpu.roll(values, distance, 1))
+    right = jnp.where(lane >= LANES - distance, 0.0, pltpu.roll(values, LANES - distance, 1))
+    return left + right
+
+
+def flat_sweep(u, q, rows, yd, xd):
+    total = u.shape[0]
+    zero = jnp.zeros((rows, LANES), jnp.float32)
+    below = jnp.concatenate([zero, u[: total - rows]], axis=0)
+    above = jnp.concatenate([u[rows:], zero], axis=0)
+    y = row_iota(u.shape) & (rows - 1)
+    down = jnp.where(y < yd, 0.0, pltpu.roll(u, yd, 0))
+    up = jnp.where(y >= rows - yd, 0.0, pltpu.roll(u, total - yd, 0))
+    return KEEP * u + W * ((below + above) + (down + up) + x_sides(u, xd)) + q
+
+
+def flat_vcycle(q, shape, rows, yd, xd):
     if is_coarsest(shape):
         u = q
         for _ in range(7):
-            u = flat_sweep(u, q, shape)
+            u = flat_sweep(u, q, rows, yd, xd)
         return u
     zs, ys, xs = shape
-    u = flat_sweep(q, q, shape)
-    change = flat_sweep(u, q, shape) - u
+    u = flat_sweep(q, q, rows, yd, xd)
+    change = flat_sweep(u, q, rows, yd, xd) - u
     pairs = [
-        change[2 * z * ys : (2 * z + 1) * ys] + change[(2 * z + 1) * ys : (2 * z + 2) * ys]
+        change[2 * z * rows : (2 * z + 1) * rows] + change[(2 * z + 1) * rows : (2 * z + 2) * rows]
         for z in range(zs // 2)
     ]
-    half = zs * ys // 2
-    tmp_ref[pl.ds(0, half), :] = jnp.concatenate(pairs, axis=0)
-    coarse = mm(pair_rows(tmp_ref, half // 2), halving_matrix())
-    coarse_shape = (zs // 2, ys // 2, xs // 2)
-    e = flat_vcycle(coarse, coarse_shape, tmp_ref)
-    spread_rows(tmp_ref, mm(e, doubling_matrix()))
-    wide = tmp_ref[pl.ds(0, half), :]
+    coarse = 0.5 * pair_sum(pair_sum(jnp.concatenate(pairs, axis=0), yd, 0), xd, 1)
+    e = flat_vcycle(coarse, (zs // 2, ys // 2, xs // 2), rows, 2 * yd, 2 * xd)
     planes = []
     for z in range(zs // 2):
-        planes += [wide[z * ys : (z + 1) * ys]] * 2
+        planes += [e[z * rows : (z + 1) * rows]] * 2
     u = u + jnp.concatenate(planes, axis=0)
-    u = flat_sweep(u, q, shape)
-    return flat_sweep(u, q, shape)
-
-
-def solve_level_one(gathered_ref, q_ref, a_ref, b_ref, tmp_ref, shape):
+    u = flat_sweep(u, q, rows, yd, xd)
+    return flat_sweep(u, q, rows, yd, xd)
+
+
+def solve_level_one(gathered_ref, v_ref, q_ref, a_ref, b_ref, tmp_ref, shape):
     zs, ys, xs = shape
-    pencils, _, part, _ = gathered_ref.shape
-    inner = pl.ds(HALO, ys)
-    row = row_iota((ys, LANES))
-    lane = lane_iota((ys, LANES))
-    a_ref[...] = jnp.zeros_like(a_ref)
-    b_ref[...] = jnp.zeros_like(b_ref)
-    q_ref[pl.ds(0, 1)] = jnp.zeros((1,) + q_ref.shape[1:], jnp.float32)
-    q_ref[pl.ds(zs + 1, 1)] = jnp.zeros((1,) + q_ref.shape[1:], jnp.float32)
-    for part_index in range(pencils):
-        q_ref[pl.ds(1, zs), pl.ds(HALO + part_index * part, part), :] = gathered_ref[part_index]
+    pencils = gathered_ref.shape[0]
+    rows = ys // 2
+    piece = rows // pencils
+    row = row_iota((rows, LANES))
+    blank = jnp.zeros((rows, LANES), jnp.float32)
+    for ref in (q_ref, a_ref, b_ref):
+        for z in (0, zs + 1):
+            for c in range(2):
+                ref[z, c] = blank
+    edge = jnp.zeros((HALO, LANES), jnp.float32)
+    for z in range(zs + 2):
+        v_ref[z, pl.ds(0, HALO), :] = edge
+        v_ref[z, pl.ds(HALO + ys, HALO), :] = edge
+    for z in (0, zs + 1):
+        for c in range(2):
+            v_ref[z, pl.ds(HALO + c * rows, rows), :] = blank
+    for z in range(zs):
+        for c in range(2):
+            for p in range(pencils):
+                spot = pl.ds(2 * piece * z + c, piece, stride=2)
+                q_ref[z + 1, c, pl.ds(p * piece, piece), :] = gathered_ref[p, spot, :]
 
     def sweep_plane(src, z):
-        here = src[z, inner, :]
-        below = src[z - 1, inner, :]
-        above = src[z + 1, inner, :]
-        down = jnp.where(row == 0, 0.0, pltpu.roll(here, 1, 0))
-        up = jnp.where(row == ys - 1, 0.0, pltpu.roll(here, ys - 1, 0))
-        left = jnp.where(lane == 0, 0.0, pltpu.roll(here, 1, 1))
-        right = jnp.where(lane == LANES - 1, 0.0, pltpu.roll(here, LANES - 1, 1))
-        near = (below + above) + (down + up) + (left + right)
-        return here, KEEP * here + W * near + q_ref[z, inner, :]
+        here = [src[z, 0], src[z, 1]]
+        new = []
+        for c in range(2):
+            other = here[1 - c]
+            if c:
+                beyond = jnp.where(row == rows - 1, 0.0, pltpu.roll(other, rows - 1, 0))
+            else:
+                beyond = jnp.where(row == 0, 0.0, pltpu.roll(other, 1, 0))
+            near = (src[z - 1, c] + src[z + 1, c]) + (other + beyond) + x_sides(here[c], 1)
+            new.append(KEEP * here[c] + W * near + q_ref[z, c])
+        return here, new
 
     def sweep(src, dst):
         def body(z, carry):
-            dst[z, inner, :] = sweep_plane(src, z)[1]
+            _, new = sweep_plane(src, z)
+            for c in range(2):
+                dst[z, c] = new[c]
             return carry
 
         lax.fori_loop(1, zs + 1, body, 0, unroll=UNROLL)
@@ -194,31 +195,47 @@
     sweep(q_ref, a_ref)
 
     def restrict(z, carry):
-        h0, s0 = sweep_plane(a_ref, 2 * z + 1)
-        h1, s1 = sweep_plane(a_ref, 2 * z + 2)
-        tmp_ref[pl.ds(pl.multiple_of(z * ys, ys), ys), :] = (s0 - h0) + (s1 - h1)
+        total = None
+        for at in (2 * z + 1, 2 * z + 2):
+            here, new = sweep_plane(a_ref, at)
+            change = (new[0] - here[0]) + (new[1] - here[1])
+            total = change if total is None else total + change
+        tmp_ref[pl.ds(pl.multiple_of(z * rows, rows), rows), :] = 0.5 * pair_sum(total, 1, 1)
         return carry
 
     lax.fori_loop(0, zs // 2, restrict, 0, unroll=2)
-    coarse_shape = (zs // 2, ys // 2, xs // 2)
-    coarse = mm(
-        pair_rows(tmp_ref, coarse_shape[0] * coarse_shape[1]), halving_matrix()
-    )
-    e = flat_vcycle(coarse, coarse_shape, tmp_ref)
-    spread_rows(tmp_ref, mm(e, doubling_matrix()))
+    tmp_ref[...] = flat_vcycle(tmp_ref[...], (zs // 2, ys // 2, xs // 2), rows, 1, 2)
 
     def correct(z, carry):
-        wide = tmp_ref[pl.ds(pl.multiple_of(z * ys, ys), ys), :]
-        a_ref[2 * z + 1, inner, :] = a_ref[2 * z + 1, inner, :] + wide
-        a_ref[2 * z + 2, inner, :] = a_ref[2 * z + 2, inner, :] + wide
+        e = tmp_ref[pl.ds(pl.multiple_of(z * rows, rows), rows), :]
+        for at in (2 * z + 1, 2 * z + 2):
+            for c in range(2):
+                a_ref[at, c] = a_ref[at, c] + e
         return carry
 
     lax.fori_loop(0, zs // 2, correct, 0, unroll=2)
     sweep(a_ref, b_ref)
-    sweep(b_ref, a_ref)
-
-
-def pack_kernel(potential_ref, store_ref, out_ref, even_ref, odd_ref):
+
+    def last_sweep(z, carry):
+        _, new = sweep_plane(b_ref, z)
+        for c in range(2):
+            v_ref[z, pl.ds(HALO + c, rows, stride=2), :] = new[c]
+        return carry
+
+    lax.fori_loop(1, zs + 1, last_sweep, 0, unroll=UNROLL)
+
+
+def pack_kernel(
+    potential_hbm, store_hbm, out_ref, even_ref, odd_ref, potential_ref, store_ref, sems
+):
+    copies = [
+        pltpu.make_async_copy(potential_hbm, potential_ref, sems.at[0]),
+        pltpu.make_async_copy(store_hbm, store_ref, sems.at[1]),
+    ]
+    for copy in copies:
+        copy.start()
+    for copy in copies:
+        copy.wait()
     depth, width, columns = potential_ref.shape
     slots = store_ref.shape[0]
     part = width // 2
@@ -237,17 +254,12 @@
             out_ref[spot, pl.ds(slot * width, width)] = store_ref[slot, side]
 
 
-def blocks_of(own_ref, far_ref, others):
-    out = [(0, own_ref, None), (4, far_ref, None)]
-    for offset, ref in others:
-        out += [(offset, ref, 0), (offset ^ 4, ref, 1)]
-    return out
-
-
-def block_rows(ref, index, start, count):
-    if index is None:
-        return ref[pl.ds(start, count), :]
-    return ref[index, pl.ds(start, count), :]
+OFFSETS = (0, 4, 3, 1, 2, 7, 5, 6)
+EARLY = 5
+
+
+def block_rows(ref, start, count):
+    return ref[pl.ds(start, count), :]
 
 
 def ends(load, first, second, part, low_half):
@@ -258,44 +270,55 @@
     return head, tail
 
 
-def edges_kernel(
-    scalar_ref, own_ref, far_ref, r1_ref, r2_ref, r3_ref,
-    even_ref, odd_ref, faces_ref, store_ref, rows_ref, *, depth, width, slabs
-):
+def store_ends(ref, pencil, out_refs, at, depth, part):
+    even_ref, odd_ref = out_refs
+    is_even = (pencil % 2) == 0
+    low_half = row_iota((8, LANES)) < 4
+    for z in range(depth):
+        for t in range(2):
+            head, tail = ends(
+                partial(block_rows, ref),
+                (4 * z + 2 * t) * part, (4 * z + 2 * t + 1) * part, part, low_half,
+            )
+            even_ref[at + 2 * z + t] = jnp.where(is_even, tail, head)
+            odd_ref[at + 2 * z + t] = jnp.where(is_even, head, tail)
+
+
+def early_edges_kernel(scalar_ref, *refs, depth, width):
+    blocks, out_refs = refs[:EARLY], refs[EARLY:]
+    for k, ref in enumerate(blocks):
+        store_ends(ref, scalar_ref[1], out_refs, 2 * depth * k, depth, width // 2)
+
+
+def late_edges_kernel(scalar_ref, *refs, depth, width):
+    slabs = len(OFFSETS)
+    even_ref, odd_ref, faces_ref, store_ref, rows_ref = refs[slabs:]
     slab = scalar_ref[0]
     pencil = scalar_ref[1]
     planes = slabs * depth
     part = width // 2
     is_even = (pencil % 2) == 0
     low_half = row_iota((8, LANES)) < 4
-    blocks = blocks_of(own_ref, far_ref, [(1, r1_ref), (2, r2_ref), (3, r3_ref)])
     base = depth * width * 2
-    for offset, ref, index in blocks:
-        target = slab ^ offset
-        store_ref[target] = block_rows(ref, index, base, 8)
-        for z in range(depth):
-            for t in range(2):
-                head, tail = ends(
-                    partial(block_rows, ref, index),
-                    (4 * z + 2 * t) * part, (4 * z + 2 * t + 1) * part, part, low_half,
-                )
-                even_ref[2 * (target * depth + z) + t] = jnp.where(is_even, tail, head)
-                odd_ref[2 * (target * depth + z) + t] = jnp.where(is_even, head, tail)
-    rows_ref[...] = jnp.zeros_like(rows_ref)
+    late = refs[EARLY:slabs]
+    for k, ref in enumerate(late):
+        store_ends(ref, pencil, (even_ref, odd_ref), 2 * depth * k, depth, part)
+    for offset, ref in zip(OFFSETS, refs):
+        store_ref[slab ^ offset] = block_rows(ref, base, 8)
+    rest = LANES - 2 * planes
+    rows_ref[pl.ds(2 * planes, rest), :] = jnp.zeros((rest, LANES), jnp.float32)
     for s in range(slabs):
         tile = store_ref[scalar_ref[2 + s]]
         slot = scalar_ref[2 + slabs + s]
-        picked = jnp.zeros((8, width), jnp.float32)
-        for k in range(LANES // width):
-            picked = jnp.where(slot == k, tile[:, k * width : (k + 1) * width], picked)
-        rows_ref[pl.ds(s * depth, depth), pl.ds(0, width)] = picked[:depth]
-        rows_ref[pl.ds(planes + s * depth, depth), pl.ds(0, width)] = picked[depth:]
+        picked = pltpu.roll(tile, (LANES - slot * width) & (LANES - 1), 1)
+        rows_ref[pl.ds(s * depth, depth), :] = picked[:depth]
+        rows_ref[pl.ds(planes + s * depth, depth), :] = picked[depth:]
     rows_ref[...] = rows_ref[...].T
     faces_ref[pl.ds(0, part), :] = rows_ref[pl.ds(0, part, stride=2), :]
     faces_ref[pl.ds(part, part), :] = rows_ref[pl.ds(1, part, stride=2), :]
-    head, tail = ends(partial(block_rows, faces_ref, None), 0, part, part, low_half)
-    even_ref[2 * planes] = jnp.where(is_even, tail, head)
-    odd_ref[2 * planes] = jnp.where(is_even, head, tail)
+    head, tail = ends(partial(block_rows, faces_ref), 0, part, part, low_half)
+    even_ref[2 * depth * len(late)] = jnp.where(is_even, tail, head)
+    odd_ref[2 * depth * len(late)] = jnp.where(is_even, head, tail)
 
 
 def halo_tiles(even_ref, odd_ref, index, is_even, low_half):
@@ -320,89 +343,161 @@
     out_ref[...] = mm(both, merging_matrix()).reshape(depth, width, 2 * LANES)
 
 
-def first_kernel(
-    scalar_ref, own_ref, far_ref, r1_ref, r2_ref, r3_ref, even_ref, odd_ref, faces_ref,
-    source_ref, q_ref, u_ref, coarse_ref, p_ref, f_ref, s_ref, left_ref, right_ref,
-    *, depth, width, pencils
-):
+def hessian_parts(below, here, above):
+    rise = [a - b for a, b in zip(above, below)]
+    y_sum, y_rise, yz_rise = [], [], []
+    for c in range(4):
+        odd = c >> 1
+        same, other = here[c ^ 2], y_other(here[c ^ 2], odd)
+        y_sum.append(same + other)
+        y_rise.append(other - same if odd else same - other)
+        same, other = rise[c ^ 2], y_other(rise[c ^ 2], odd)
+        yz_rise.append(other - same if odd else same - other)
+    out = []
+    for c in range(4):
+        odd = c & 1
+        same, other = here[c ^ 1], x_other(here[c ^ 1], odd)
+        twice = 2.0 * here[c]
+        pxx = same + other - twice
+        pyy = y_sum[c] - twice
+        pzz = below[c] + above[c] - twice
+        same, other = rise[c ^ 1], x_other(rise[c ^ 1], odd)
+        pxz = other - same if odd else same - other
+        same, other = y_rise[c ^ 1], x_other(y_rise[c ^ 1], odd)
+        pxy = other - same if odd else same - other
+        cross = pxy * pxy + pxz * pxz + yz_rise[c] * yz_rise[c]
+        out.append(pxx * pyy + (pxx + pyy) * pzz - 0.0625 * cross)
+    return out
+
+
+def face_part(face, c, z, planes):
+    lane = lane_iota(face.shape)
+    if c & 1:
+        turned = pltpu.roll(face, LANES - 1 - planes - z, 1)
+        return jnp.where(lane == LANES - 1, turned, 0.0)
+    turned = pltpu.roll(face, (LANES - z) & (LANES - 1), 1)
+    return jnp.where(lane == 0, turned, 0.0)
+
+
+def fill_block(p_ref, at, ref, edge_refs, tile, pencil, depth, part):
+    is_even = (pencil % 2) == 0
+    low_half = row_iota((8, LANES)) < 4
+    for z in range(depth):
+        for c in range(4):
+            p_ref[at + z, c, pl.ds(0, part), :] = block_rows(ref, (4 * z + c) * part, part)
+        for t in range(2):
+            first, second = halo_tiles(*edge_refs, tile + 2 * z + t, is_even, low_half)
+            p_ref[at + z, 2 * t, pl.ds(part, 8), :] = first
+            p_ref[at + z, 2 * t + 1, pl.ds(part, 8), :] = second
+
+
+def near_half_kernel(scalar_ref, *refs, depth, width, pencils):
+    near = [k for k in range(EARLY) if OFFSETS[k] < 4]
+    blocks = refs[: len(near)]
+    even_ref, odd_ref, faces_ref, p_ref, s_ref, q_ref = refs[len(near) :]
     slab = scalar_ref[0]
     pencil = scalar_ref[1]
-    planes = p_ref.shape[0] - 2
     part = width // 2
+    half = 4 * depth
+    first_plane = (slab // 4) * half
+    mask = halo_mask(pencil, pencils)
+    blank = jnp.zeros(p_ref.shape[1:], jnp.float32)
+    p_ref[0] = blank
+    p_ref[half + 1] = blank
+    for k, ref in zip(near, blocks):
+        at = ((slab ^ OFFSETS[k]) % 4) * depth + 1
+        fill_block(p_ref, at, ref, (even_ref, odd_ref), 2 * depth * k, pencil, depth, part)
+
+    def body(j, carry):
+        source = hessian_parts(parts(p_ref, j), parts(p_ref, j + 1), parts(p_ref, j + 2))
+        for c in range(4):
+            s_ref[j, c] = source[c][:part]
+            face = faces_ref[pl.ds((c >> 1) * part, part), :]
+            face = face_part(face, c, first_plane + j, 2 * half)
+            q_ref[j, c, pl.ds(0, part), :] = W * (face - source[c][:part])
+            q_ref[j, c, pl.ds(part, 8), :] = (-W * mask) * source[c][part:]
+        return carry
+
+    lax.fori_loop(0, half, body, 0, unroll=2)
+
+
+def far_half_kernel(scalar_ref, *refs, depth, width, pencils):
+    far = [k for k in range(len(OFFSETS)) if OFFSETS[k] >= 4]
+    blocks = refs[: len(far)]
+    early_refs = refs[len(far) : len(far) + 2]
+    late_refs = refs[len(far) + 2 : len(far) + 4]
+    faces_ref, pn_ref, sn_ref, qn_ref = refs[len(far) + 4 : len(far) + 8]
+    source_hbm, q_ref, u_ref, coarse_ref = refs[len(far) + 8 : len(far) + 12]
+    p_ref, f_ref, s_ref, left_ref, right_ref, source_ref, sem = refs[len(far) + 12 :]
+    slab = scalar_ref[0]
+    pencil = scalar_ref[1]
+    part = width // 2
+    half = 4 * depth
+    planes = 2 * half
+    lower = slab < 4
+    near_first = jnp.where(lower, 0, half)
+    far_first = half - near_first
     is_even = (pencil % 2) == 0
     low_half = row_iota((8, LANES)) < 4
     mask = halo_mask(pencil, pencils)
     blank = jnp.zeros(p_ref.shape[1:], jnp.float32)
-    p_ref[0] = blank
-    p_ref[planes + 1] = blank
     for ref in (q_ref, u_ref):
         for z in (0, 1, planes + 2, planes + 3):
             ref[z] = blank
-    for offset, ref, index in blocks_of(own_ref, far_ref, [(1, r1_ref), (2, r2_ref), (3, r3_ref)]):
-        target = (slab ^ offset) * depth + 1
-        for z in range(depth):
-            for c in range(4):
-                p_ref[target + z, c, pl.ds(0, part), :] = block_rows(
-                    ref, index, (4 * z + c) * part, part
-                )
-
-    def edges(z, carry):
-        for t in range(2):
-            first, second = halo_tiles(even_ref, odd_ref, 2 * z + t, is_even, low_half)
-            p_ref[z + 1, 2 * t, pl.ds(part, 8), :] = first
-            p_ref[z + 1, 2 * t + 1, pl.ds(part, 8), :] = second
-        return carry
-
-    lax.fori_loop(0, planes, edges, 0, unroll=UNROLL)
-    first, second = halo_tiles(even_ref, odd_ref, 2 * planes, is_even, low_half)
+    p_ref[jnp.where(lower, half + 1, 0)] = blank
+    p_ref[jnp.where(lower, 0, half + 1)] = pn_ref[jnp.where(lower, half, 1)]
+    for k, ref in zip(far, blocks):
+        at = ((slab ^ OFFSETS[k]) % 4) * depth + 1
+        early = k < EARLY
+        tile = 2 * depth * (k if early else k - EARLY)
+        edge_refs = early_refs if early else late_refs
+        fill_block(p_ref, at, ref, edge_refs, tile, pencil, depth, part)
+    face_tile = 2 * depth * (len(OFFSETS) - EARLY)
+    first, second = halo_tiles(*late_refs, face_tile, is_even, low_half)
     f_ref[0, pl.ds(0, part), :] = faces_ref[pl.ds(0, part), :]
     f_ref[0, pl.ds(part, 8), :] = first
     f_ref[1, pl.ds(0, part), :] = faces_ref[pl.ds(part, part), :]
     f_ref[1, pl.ds(part, 8), :] = second
-    lane = lane_iota((part + 8, LANES))
-
-    def hessian(z, carry):
-        below = parts(p_ref, z)
-        here = parts(p_ref, z + 1)
-        above = parts(p_ref, z + 2)
-        rise = [a - b for a, b in zip(above, below)]
-        y_sum, y_rise, yz_rise = [], [], []
+
+    def finish(source, z):
         for c in range(4):
-            odd = c >> 1
-            same, other = here[c ^ 2], y_other(here[c ^ 2], odd)
-            y_sum.append(same + other)
-            y_rise.append(other - same if odd else same - other)
-            same, other = rise[c ^ 2], y_other(rise[c ^ 2], odd)
-            yz_rise.append(other - same if odd else same - other)
+            face = face_part(f_ref[c >> 1], c, z, planes)
+            put(q_ref, z + 2, c, W * (face - source[c]), mask)
+
+    def copy(j, carry):
+        z = near_first + j
         for c in range(4):
-            odd = c & 1
-            same, other = here[c ^ 1], x_other(here[c ^ 1], odd)
-            twice = 2.0 * here[c]
-            pxx = same + other - twice
-            pyy = y_sum[c] - twice
-            pzz = below[c] + above[c] - twice
-            same, other = rise[c ^ 1], x_other(rise[c ^ 1], odd)
-            pxz = other - same if odd else same - other
-            same, other = y_rise[c ^ 1], x_other(y_rise[c ^ 1], odd)
-            pxy = other - same if odd else same - other
-            pyz = yz_rise[c]
-            cross = pxy * pxy + pxz * pxz + pyz * pyz
-            source = pxx * pyy + (pxx + pyy) * pzz - 0.0625 * cross
-            s_ref[z, c] = source[:part]
-            face = f_ref[c >> 1]
-            if odd:
-                face = jnp.where(
-                    lane == LANES - 1, pltpu.roll(face, LANES - 1 - planes - z, 1), 0.0
-                )
-            else:
-                face = jnp.where(lane == 0, pltpu.roll(face, (LANES - z) & (LANES - 1), 1), 0.0)
-            put(q_ref, z + 2, c, W * (face - source), mask)
+            face = face_part(f_ref[c >> 1, pl.ds(part, 8), :], c, z, planes)
+            q_ref[z + 2, c, pl.ds(0, part), :] = qn_ref[j, c, pl.ds(0, part), :]
+            q_ref[z + 2, c, pl.ds(part, 8), :] = (
+                qn_ref[j, c, pl.ds(part, 8), :] + (W * mask) * face
+            )
         return carry
 
-    lax.fori_loop(0, planes, hessian, 0, unroll=2)
-    join_planes(
-        lambda z, c: s_ref[slab * depth + z, c], source_ref, left_ref, right_ref, depth, width
-    )
+    lax.fori_loop(0, half, copy, 0, unroll=UNROLL)
+
+    def body(j, carry):
+        source = hessian_parts(parts(p_ref, j), parts(p_ref, j + 1), parts(p_ref, j + 2))
+        finish(source, far_first + j)
+        return carry
+
+    lax.fori_loop(0, half, body, 0, unroll=2)
+    seam = jnp.where(lower, half, 1)
+    here = parts(pn_ref, seam)
+    inner = parts(pn_ref, jnp.where(lower, half - 1, 2))
+    outer = parts(p_ref, jnp.where(lower, 1, half))
+    below = [jnp.where(lower, a, b) for a, b in zip(inner, outer)]
+    above = [jnp.where(lower, b, a) for a, b in zip(inner, outer)]
+    source = hessian_parts(below, here, above)
+    finish(source, near_first + seam - 1)
+    own = (slab % 4) * depth
+    for z in range(depth):
+        is_seam = own + z == seam - 1
+        for c in range(4):
+            s_ref[z, c] = jnp.where(is_seam, source[c][:part], sn_ref[own + z, c])
+    join_planes(lambda z, c: s_ref[z, c], source_ref, left_ref, right_ref, depth, width)
+    copy_out = pltpu.make_async_copy(source_ref, source_hbm, sem)
+    copy_out.start()
 
     def second_sweep(z, carry):
         here = parts(q_ref, z + 2)
@@ -413,6 +508,7 @@
 
     lax.fori_loop(0, planes, second_sweep, 0, unroll=UNROLL)
     restrict_window(u_ref, q_ref, coarse_ref, planes, part)
+    copy_out.wait()
 
 
 def restrict_window(u_ref, q_ref, coarse_ref, planes, part):
@@ -441,21 +537,21 @@
 
 def middle_kernel(
     scalar_ref, gathered_ref, q_ref, u_ref, qwin_ref, uwin_ref, coarse_ref,
-    q1_ref, a1_ref, b1_ref, tmp_ref, a_ref, b_ref, *, depth, width, pencils, shape
+    v_ref, q1_ref, a1_ref, b1_ref, tmp_ref, a_ref, b_ref, *, depth, width, pencils, shape
 ):
     slab = scalar_ref[0]
     pencil = scalar_ref[1]
     planes = a_ref.shape[0] - 4
     part = width // 2
     mask = halo_mask(pencil, pencils)
-    solve_level_one(gathered_ref, q1_ref, a1_ref, b1_ref, tmp_ref, shape)
+    solve_level_one(gathered_ref, v_ref, q1_ref, a1_ref, b1_ref, tmp_ref, shape)
     blank = jnp.zeros(a_ref.shape[1:], jnp.float32)
     for ref in (a_ref, b_ref):
         for z in (0, 1, planes + 2, planes + 3):
             ref[z] = blank
 
     def correct(z, carry):
-        wide = coarse_window(a1_ref, z + 1, pencil, part)
+        wide = coarse_window(v_ref, z + 1, pencil, part)
         for at in (2 * z + 2, 2 * z + 3):
             for c in range(4):
                 a_ref[at, c] = u_ref[at, c] + wide
@@ -485,7 +581,7 @@
 
 def last_kernel(
     scalar_ref, gathered_ref, qwin_ref, uwin_ref, out_ref,
-    q1_ref, a1_ref, b1_ref, tmp_ref, a_ref, b_ref, left_ref, right_ref,
+    v_ref, q1_ref, a1_ref, b1_ref, tmp_ref, a_ref, b_ref, left_ref, right_ref,
     *, depth, width, pencils, shape
 ):
     slab = scalar_ref[0]
@@ -493,9 +589,9 @@
     planes = shape[0] * 2
     part = width // 2
     mask = halo_mask(pencil, pencils)
-    solve_level_one(gathered_ref, q1_ref, a1_ref, b1_ref, tmp_ref, shape)
+    solve_level_one(gathered_ref, v_ref, q1_ref, a1_ref, b1_ref, tmp_ref, shape)
     for z in range(depth // 2 + 2):
-        wide = coarse_window(a1_ref, slab * (depth // 2) + z, pencil, part)
+        wide = coarse_window(v_ref, slab * (depth // 2) + z, pencil, part)
         for at in (2 * z, 2 * z + 1):
             for c in range(4):
                 a_ref[at, c] = uwin_ref[at, c] + wide
@@ -531,14 +627,17 @@
     return pltpu.VMEM(shape, jnp.float32)
 
 
-def call(kernel, name, scalars, args, outs, scratch=()):
+def call(kernel, name, scalars, args, outs, scratch=(), space=pltpu.VMEM, out_space=None):
+    out_specs = jax.tree.map(lambda _: vmem(), outs)
+    if out_space is not None:
+        out_specs = tuple(pl.BlockSpec(memory_space=one) for one in out_space)
     return pl.pallas_call(
         kernel,
         out_shape=outs,
-        in_specs=[smem()] * len(scalars) + [vmem()] * len(args),
-        out_specs=jax.tree.map(lambda _: vmem(), outs),
+        in_specs=[smem()] * len(scalars) + [pl.BlockSpec(memory_space=space)] * len(args),
+        out_specs=out_specs,
         scratch_shapes=list(scratch),
-        compiler_params=pltpu.CompilerParams(vmem_limit_bytes=48 << 20),
+        compiler_params=pltpu.CompilerParams(vmem_limit_bytes=16 << 20),
         name=name,
     )(*scalars, *args)
 
@@ -556,53 +655,90 @@
         pack_kernel,
         "pack",
         [],
-        [potential, parent_store],
+        [pltpu.with_memory_space_constraint(x, pltpu.HBM) for x in (potential, parent_store)],
         arr(depth * width * 2 + 8, LANES),
-        [buf(depth * width, LANES), buf(depth * width, LANES)],
+        [
+            buf(depth * width, LANES),
+            buf(depth * width, LANES),
+            buf(*potential.shape),
+            buf(*parent_store.shape),
+            pltpu.SemaphoreType.DMA((2,)),
+        ],
+        space=pltpu.HBM,
     )
 
     def swap(x, bits):
         return lax.ppermute(x, "slab", [(i, i ^ bits) for i in range(slabs)])
 
-    far = swap(own, 4)
-    both = jnp.stack([own, far])
-    others = [swap(both, bits) for bits in (1, 2, 3)]
-    message = arr(2 * planes + 1, 8, LANES)
+    near = [swap(own, bits) for bits in OFFSETS[1:5]]
+    blocks = [own, *near] + [swap(near[0], bits) for bits in OFFSETS[2:5]]
+    low_pairs = [(i, i + 1) for i in range(0, pencils - 1, 2)]
+    high_pairs = [(i, i + 1) for i in range(1, pencils - 1, 2)]
+
+    def beside(even, odd):
+        return (
+            lax.ppermute(even, "pencil", low_pairs + [(j, i) for i, j in low_pairs]),
+            lax.ppermute(odd, "pencil", high_pairs + [(j, i) for i, j in high_pairs]),
+        )
+
+    message = arr(2 * depth * EARLY, 8, LANES)
+    early = call(
+        partial(early_edges_kernel, depth=depth, width=width),
+        "early_edges",
+        [scalars],
+        blocks[:EARLY],
+        (message, message),
+    )
+    early = beside(*early)
+    message = arr(2 * depth * (slabs - EARLY) + 1, 8, LANES)
     even, odd, faces = call(
-        partial(edges_kernel, depth=depth, width=width, slabs=slabs),
-        "edges",
+        partial(late_edges_kernel, depth=depth, width=width),
+        "late_edges",
         [scalars],
-        [own, far, *others],
+        blocks,
         (message, message, arr(width, LANES)),
         [buf(slabs, 8, LANES), buf(LANES, LANES)],
     )
-    low_pairs = [(i, i + 1) for i in range(0, pencils - 1, 2)]
-    high_pairs = [(i, i + 1) for i in range(1, pencils - 1, 2)]
-    even = lax.ppermute(even, "pencil", low_pairs + [(j, i) for i, j in low_pairs])
-    odd = lax.ppermute(odd, "pencil", high_pairs + [(j, i) for i, j in high_pairs])
+    late = beside(even, odd)
     shape = (planes // 2, height // 2, columns // 2)
     coarse_part = arr(planes // 2 * part, LANES)
     field = (planes + 4, 4, rows, LANES)
+    half = planes // 2
+    near = call(
+        partial(near_half_kernel, depth=depth, width=width, pencils=pencils),
+        "near_half",
+        [scalars],
+        [b for b, offset in zip(blocks, OFFSETS) if offset < 4] + [*early, faces],
+        (arr(half + 2, 4, rows, LANES), arr(half, 4, part, LANES), arr(half, 4, rows, LANES)),
+    )
     source, q, u, coarse = call(
-        partial(first_kernel, depth=depth, width=width, pencils=pencils),
-        "first",
+        partial(far_half_kernel, depth=depth, width=width, pencils=pencils),
+        "far_half",
         [scalars],
-        [own, far, *others, even, odd, faces],
+        [b for b, offset in zip(blocks, OFFSETS) if offset >= 4] + [*early, *late, faces, *near],
         (arr(depth, width, columns), arr(*field), arr(*field), coarse_part),
         [
-            buf(planes + 2, 4, rows, LANES),
+            buf(half + 2, 4, rows, LANES),
             buf(2, rows, LANES),
-            buf(planes, 4, part, LANES),
+            buf(depth, 4, part, LANES),
             buf(depth * width, LANES),
             buf(depth * width, LANES),
+            buf(depth, width, columns),
+            pltpu.SemaphoreType.DMA,
         ],
-    )
-    level = (shape[0] + 2, shape[1] + 2 * HALO, LANES)
-    level_scratch = [buf(*level), buf(*level), buf(*level), buf(shape[0] * shape[1], LANES)]
+        out_space=[pl.ANY] + [pltpu.VMEM] * 3,
+    )
+    level = (shape[0] + 2, 2, shape[1] // 2, LANES)
+    level_scratch = [
+        buf(shape[0] + 2, shape[1] + 2 * HALO, LANES),
+        buf(*level),
+        buf(*level),
+        buf(*level),
+        buf(shape[0] * shape[1] // 4, LANES),
+    ]
 
     def gather(x):
-        whole = lax.all_gather(x, "pencil", axis=0, tiled=False)
-        return whole.reshape(pencils, shape[0], part, LANES)
+        return lax.all_gather(x, "pencil", axis=0, tiled=False)
 
     sizes = dict(depth=depth, width=width, pencils=pencils, shape=shape)
     slim = (depth + 4, 4, rows, LANES)
@@ -638,8 +774,8 @@
         and columns == 2 * LANES
         and width == 32
         and parent_store.shape[0] * width == LANES
-        and 2 * planes <= LANES
-        and pencils <= 8
+        and 2 * planes < LANES
+        and pencils in (2, 4, 8)
     )
 
 

time: 73.8 us -> 64.6 us (0.88)
  waiting for transfers between devices: 17.4 us -> 7.14 us
  starting transfers between devices: 8.41 us -> 12.8 us
  blocking collectives: 20.5 us -> 18 us
  local copies, waits for them, and re-layouts: 1.61 us -> 0 us
  Pallas kernels: 23.9 us -> 25 us
    ppermute x4 -> x7, waiting for transfers between devices: 16.6 us -> 7.13 us  [swap(): return lax.ppermute(x, 'slab', [(i, i ^ bits) for i in range(slabs)])]
    ppermute x4 -> x7, starting transfers between devices: 7.65 us -> 11.3 us  [swap(): return lax.ppermute(x, 'slab', [(i, i ^ bits) for i in range(slabs)])]
    all_gather x2, blocking collectives: 20.5 us -> 18 us  [gather(): return lax.all_gather(x, 'pencil', axis=0, tiled=False)]
    unnamed x4 -> x0, local copies, waits for them, and re-layouts: 1.61 us -> none
    pallas_call x5 -> x7, Pallas kernels: 23.9 us -> 25 us  [call(): pl.pallas_call(kernel, out_shape=outs, in_specs=[smem()] * len(scalars) +...]
    ppermute x2 -> x4, waiting for transfers between devices: 0.84 us -> 0.01 us  [the longest x2 0.01 us: beside(): lax.ppermute(odd, 'pencil', high_pairs + [(j, i) for i, j in high_pairs])]
    ppermute x2 -> x4, starting transfers between devices: 0.76 us -> 1.48 us  [the longest x2 1.34 us: beside(): lax.ppermute(odd, 'pencil', high_pairs + [(j, i) for i, j in high_pairs])]
  transfers between devices with their start and end apart: 6 -> 11, of which waited for: 5 -> 5; matrix products, arithmetic and copies ran while one was open for 1% -> 1% of each run, Pallas kernels for 0% -> 5%
where the time goes in v3:
time: 64.6 us; the launch traced here: 64.4 us
  Pallas kernels  25 us (39%)
  blocking collectives  18 us (28%)
  starting transfers between devices  12.8 us (20%)
  waiting for transfers between devices  7.14 us (11%)
  other arithmetic  0.75 us (1%)
  between operations  0.75 us (1%)
    pallas_call x7, Pallas kernels, call(): pl.pallas_call(kernel, out_shape=outs, in_specs=[smem()] * len(scalars) +...  25 us
    all_gather x2, blocking collectives, gather(): return lax.all_gather(x, 'pencil', axis=0, tiled=False)  18 us
    ppermute x7, starting transfers between devices, swap(): return lax.ppermute(x, 'slab', [(i, i ^ bits) for i in range(slabs)])  11.3 us
    ppermute x7, waiting for transfers between devices, swap(): return lax.ppermute(x, 'slab', [(i, i ^ bits) for i in range(slabs)])  7.13 us
    ppermute x2, starting transfers between devices, beside(): lax.ppermute(odd, 'pencil', high_pairs + [(j, i) for i, j in high_pairs])  1.34 us
  transfers between devices with their start and end apart: 11, of which 5 were waited for; matrix products, arithmetic and copies ran while one was open for 1% of the time, Pallas kernels for 5%

profile of v3, /device:TPU:0, one launch (start us, length us, event | category | flops | bytes accessed | tf_op | source)
XLA Modules:
  0.0 64.4 jit_solution(10747595622573224480)
XLA Ops:
  0.6 1.2 %pack.1.refs_0_ = f32[264,128]{1,0:T(8,128)S(1)} custom-call(f32[4,32,256]{2,1,0:T(8,128)} %potential_hbm.1, f32[4,2,4,32]{3,2,1,0:T(4,128)} %store_hbm.1), custom_call_target="tpu_custom_call" | custom-call | tf_op jit(solution)/shard_map/pack/pallas_call | solution.py:634
  1.8 4.1 %collective-permute-start = (f32[264,128]{1,0:T(8,128)S(1)}, f32[264,128]{1,0:T(8,128)S(1)}, u32[]{:S(2)}, u32[]{:S(2)}) collective-permute-start(f32[264,128]{1,0:T(8,128)S(1)} %pack.1.refs_0_), channel_id=1, source_target_pairs={{0,16},{4,20},{8,24},{12,28},{16,0},{20,4},{24,8},{28,12},{1,17},{... | collective-permute-start | bytes 405512 | tf_op jit(solution)/shard_map/ppermute | solution.py:671
  5.9 1.6 %collective-permute-start.6 = (f32[264,128]{1,0:T(8,128)S(1)}, f32[264,128]{1,0:T(8,128)S(1)}, u32[]{:S(2)}, u32[]{:S(2)}) collective-permute-start(f32[264,128]{1,0:T(8,128)S(1)} %pack.1.refs_0_), channel_id=1, source_target_pairs={{0,8},{4,12},{8,0},{12,4},{16,24},{20,28},{24,16},{28,20},{1,9},{5... | collective-permute-start | bytes 405512 | tf_op jit(solution)/shard_map/ppermute | solution.py:671
  7.5 1.5 %collective-permute-start.5 = (f32[264,128]{1,0:T(8,128)S(1)}, f32[264,128]{1,0:T(8,128)S(1)}, u32[]{:S(2)}, u32[]{:S(2)}) collective-permute-start(f32[264,128]{1,0:T(8,128)S(1)} %pack.1.refs_0_), channel_id=1, source_target_pairs={{0,4},{4,0},{8,12},{12,8},{16,20},{20,16},{24,28},{28,24},{1,5},{5... | collective-permute-start | bytes 405512 | tf_op jit(solution)/shard_map/ppermute | solution.py:671
  9.0 0.4 collective-permute-start.4
  9.4 3.1 %collective-permute-done.refs_1_.refs_0_ = f32[264,128]{1,0:T(8,128)S(1)} collective-permute-done((f32[264,128]{1,0:T(8,128)S(1)}, f32[264,128]{1,0:T(8,128)S(1)}, u32[]{:S(2)}, u32[]{:S(2)}) %collective-permute-start) | collective-permute-done | bytes 135200 | tf_op jit(solution)/shard_map/ppermute | solution.py:671
  12.5 0.7 %collective-permute-start.3 = (f32[264,128]{1,0:T(8,128)S(1)}, f32[264,128]{1,0:T(8,128)S(1)}, u32[]{:S(2)}, u32[]{:S(2)}) collective-permute-start(f32[264,128]{1,0:T(8,128)S(1)} %collective-permute-done.refs_1_.refs_0_), channel_id=1, source_target_pairs={{0,8},{4,12},{8,0},{12,4},{16,24},{20,28},{24,16},{28,20},{1,9},{5... | collective-permute-start | bytes 405512 | tf_op jit(solution)/shard_map/ppermute | solution.py:671
  13.2 1.5 %collective-permute-start.2 = (f32[264,128]{1,0:T(8,128)S(1)}, f32[264,128]{1,0:T(8,128)S(1)}, u32[]{:S(2)}, u32[]{:S(2)}) collective-permute-start(f32[264,128]{1,0:T(8,128)S(1)} %collective-permute-done.refs_1_.refs_0_), channel_id=1, source_target_pairs={{0,4},{4,0},{8,12},{12,8},{16,20},{20,16},{24,28},{28,24},{1,5},{5... | collective-permute-start | bytes 405512 | tf_op jit(solution)/shard_map/ppermute | solution.py:671
  14.6 0.0 collective-permute-done.6.refs_4_.refs_3_
  14.6 1.6 %collective-permute-start.1 = (f32[264,128]{1,0:T(8,128)S(1)}, f32[264,128]{1,0:T(8,128)S(1)}, u32[]{:S(2)}, u32[]{:S(2)}) collective-permute-start(f32[264,128]{1,0:T(8,128)S(1)} %collective-permute-done.refs_1_.refs_0_), channel_id=1, source_target_pairs={{0,12},{4,8},{8,4},{12,0},{16,28},{20,24},{24,20},{28,16},{1,13},{... | collective-permute-start | bytes 405512 | tf_op jit(solution)/shard_map/ppermute | solution.py:671
  16.2 0.7 %pad_add_fusion.scalar_ref = s32[18]{0:T(128)S(1)} fusion(s32[8]{0:T(128)} %param.7, s32[8]{0:T(128)} %param.6, s32[1]{0:T(128)} %bitcast.1, s32[1]{0:T(128)} %bitcast), kind=kLoop, calls=%fused_computation | loop fusion | flops 54 | bytes 144 | tf_op jit(solution)/shard_map/concatenate | solution.py:653
  17.0 0.0 collective-permute-done.5.refs_3_.refs_2_
  17.0 0.5 collective-permute-done.4.refs_2_.refs_1_
  17.4 0.6 early_edges.1
  18.0 0.1 collective-permute-start.7
  18.1 0.7 %collective-permute-start.8 = (f32[40,8,128]{2,1,0:T(8,128)S(1)}, f32[40,8,128]{2,1,0:T(8,128)S(1)}, u32[]{:S(2)}, u32[]{:S(2)}) collective-permute-start(f32[40,8,128]{2,1,0:T(8,128)S(1)} %get-tuple-element.18), channel_id=1, source_target_pairs={{1,2},{2,1},{5,6},{6,5},{9,10},{10,9},{13,14},{14,13},{17,18},{18,... | collective-permute-start | bytes 491528 | tf_op jit(solution)/shard_map/ppermute | solution.py:681
  18.8 0.6 collective-permute-done.3.refs_7_.refs_3_
  19.3 1.4 %collective-permute-done.2.refs_6_.refs_2_ = f32[264,128]{1,0:T(8,128)S(1)} collective-permute-done((f32[264,128]{1,0:T(8,128)S(1)}, f32[264,128]{1,0:T(8,128)S(1)}, u32[]{:S(2)}, u32[]{:S(2)}) %collective-permute-start.2) | collective-permute-done | bytes 135200 | tf_op jit(solution)/shard_map/ppermute | solution.py:671
  20.8 1.6 %collective-permute-done.1.refs_5_.refs_1_ = f32[264,128]{1,0:T(8,128)S(1)} collective-permute-done((f32[264,128]{1,0:T(8,128)S(1)}, f32[264,128]{1,0:T(8,128)S(1)}, u32[]{:S(2)}, u32[]{:S(2)}) %collective-permute-start.1) | collective-permute-done | bytes 135200 | tf_op jit(solution)/shard_map/ppermute | solution.py:671
  22.3 0.7 %late_edges.1 = (f32[25,8,128]{2,1,0:T(8,128)S(1)}, f32[25,8,128]{2,1,0:T(8,128)S(1)}, f32[32,128]{1,0:T(8,128)S(1)}) custom-call(s32[18]{0:T(128)S(1)} %pad_add_fusion.scalar_ref, f32[264,128]{1,0:T(8,128)S(1)} %pack.1.refs_0_, f32[264,128]{1,0:T(8,128)S(1)} %collective-permute-done.refs_1_.refs_0_, f32[264,128]{1,0:T(8,128)S(1)} %collective-permute-done.4.refs_2_.refs_1_, ...), custom_call_target="tpu_custom_call" | custom-call | tf_op jit(solution)/shard_map/late_edges/pallas_call | solution.py:634
  23.1 0.1 collective-permute-start.9
  23.2 0.7 %collective-permute-start.10 = (f32[25,8,128]{2,1,0:T(8,128)S(1)}, f32[25,8,128]{2,1,0:T(8,128)S(1)}, u32[]{:S(2)}, u32[]{:S(2)}) collective-permute-start(f32[25,8,128]{2,1,0:T(8,128)S(1)} %get-tuple-element.20), channel_id=1, source_target_pairs={{1,2},{2,1},{5,6},{6,5},{9,10},{10,9},{13,14},{14,13},{17,18},{18,... | collective-permute-start | bytes 307208 | tf_op jit(solution)/shard_map/ppermute | solution.py:681
  23.8 0.0 collective-permute-done.7.refs_4_
  23.8 0.0 collective-permute-done.8.refs_5_
  23.8 1.9 %near_half.1 = (f32[18,4,24,128]{3,2,1,0:T(8,128)S(1)}, f32[16,4,16,128]{3,2,1,0:T(8,128)S(1)}, f32[16,4,24,128]{3,2,1,0:T(8,128)S(1)}) custom-call(s32[18]{0:T(128)S(1)} %pad_add_fusion.scalar_ref, f32[264,128]{1,0:T(8,128)S(1)} %pack.1.refs_0_, f32[264,128]{1,0:T(8,128)S(1)} %collective-permute-done.4.refs_2_.refs_1_, ...), custom_call_target="tpu_custom_call" | custom-call | tf_op jit(solution)/shard_map/near_half/pallas_call | solution.py:634
  25.8 0.0 collective-permute-done.9.refs_6_
  25.8 0.0 collective-permute-done.10.refs_7_
  25.8 4.8 %far_half.1 = (f32[4,32,256]{2,1,0:T(8,128)}, f32[36,4,24,128]{3,2,1,0:T(8,128)S(1)}, f32[36,4,24,128]{3,2,1,0:T(8,128)S(1)}, f32[256,128]{1,0:T(8,128)S(1)}) custom-call(s32[18]{0:T(128)S(1)} %pad_add_fusion.scalar_ref, f32[264,128]{1,0:T(8,128)S(1)} %collective-permute-done.refs_1_.refs_0_, f32[264,128]{1,0:T(8,128)S(1)} %collective-permute-done.1.refs_5_.refs_1_, ...), custom_call_target="tpu_custom_call" | custom-call | tf_op jit(solution)/shard_map/far_half/pallas_call | solution.py:634
  30.7 10.7 %all-gather = f32[1024,128]{1,0:T(8,128)S(1)} all-gather(f32[256,128]{1,0:T(8,128)S(1)} %get-tuple-element.25), channel_id=2, replica_groups=mesh['slab'=8,'pencil'=4] {'pencil'}, dimensions={0}, use_global_device_ids=true | all-gather | bytes 655360 | tf_op jit(solution)/shard_map/all_gather | solution.py:741
  41.4 10.2 %middle.1 = (f32[8,4,24,128]{3,2,1,0:T(8,128)S(1)}, f32[8,4,24,128]{3,2,1,0:T(8,128)S(1)}, f32[256,128]{1,0:T(8,128)S(1)}) custom-call(s32[18]{0:T(128)S(1)} %pad_add_fusion.scalar_ref, f32[4,256,128]{2,1,0:T(8,128)S(1)} %bitcast.4, f32[36,4,24,128]{3,2,1,0:T(8,128)S(1)} %get-tuple-element.26.q_ref, f32[36,4,24,128]{3,2,1,0:T(8,128)S(1)} %get-tuple-element.27.u_ref), custom_call_target="tpu_custom_call" | custom-call | tf_op jit(solution)/shard_map/middle/pallas_call | solution.py:634
  51.5 7.3 %all-gather.1 = f32[1024,128]{1,0:T(8,128)S(1)} all-gather(f32[256,128]{1,0:T(8,128)S(1)} %get-tuple-element.28), channel_id=3, replica_groups=mesh['slab'=8,'pencil'=4] {'pencil'}, dimensions={0}, use_global_device_ids=true | all-gather | bytes 655360 | tf_op jit(solution)/shard_map/all_gather | solution.py:741
  58.8 5.6 %last.1 = f32[4,32,256]{2,1,0:T(8,128)} custom-call(s32[18]{0:T(128)S(1)} %pad_add_fusion.scalar_ref, f32[4,256,128]{2,1,0:T(8,128)S(1)} %bitcast.5, f32[8,4,24,128]{3,2,1,0:T(8,128)S(1)} %get-tuple-element.29.qwin_ref, f32[8,4,24,128]{3,2,1,0:T(8,128)S(1)} %get-tuple-element.30.uwin_ref), custom_call_target="tpu_custom_call" | custom-call | tf_op jit(solution)/shard_map/last/pallas_call | solution.py:634
Async XLA Ops:
  1.8 10.7 %collective-permute-start = (f32[264,128]{1,0:T(8,128)S(1)}, f32[264,128]{1,0:T(8,128)S(1)}, u32[]{:S(2)}, u32[]{:S(2)}) collective-permute-start(f32[264,128]{1,0:T(8,128)S(1)} %pack.1.refs_0_), channel_id=1, source_target_pairs={{0,16},{4,20},{8,24},{12,28},{16,0},{20,4},{24,8},{28,12},{1,17},{... | collective-permute-start | bytes 405512 | tf_op jit(solution)/shard_map/ppermute | solution.py:671
  5.9 8.7 %collective-permute-start.6 = (f32[264,128]{1,0:T(8,128)S(1)}, f32[264,128]{1,0:T(8,128)S(1)}, u32[]{:S(2)}, u32[]{:S(2)}) collective-permute-start(f32[264,128]{1,0:T(8,128)S(1)} %pack.1.refs_0_), channel_id=1, source_target_pairs={{0,8},{4,12},{8,0},{12,4},{16,24},{20,28},{24,16},{28,20},{1,9},{5... | collective-permute-start | bytes 405512 | tf_op jit(solution)/shard_map/ppermute | solution.py:671
  7.5 9.5 %collective-permute-start.5 = (f32[264,128]{1,0:T(8,128)S(1)}, f32[264,128]{1,0:T(8,128)S(1)}, u32[]{:S(2)}, u32[]{:S(2)}) collective-permute-start(f32[264,128]{1,0:T(8,128)S(1)} %pack.1.refs_0_), channel_id=1, source_target_pairs={{0,4},{4,0},{8,12},{12,8},{16,20},{20,16},{24,28},{28,24},{1,5},{5... | collective-permute-start | bytes 405512 | tf_op jit(solution)/shard_map/ppermute | solution.py:671
  9.0 8.5 %collective-permute-start.4 = (f32[264,128]{1,0:T(8,128)S(1)}, f32[264,128]{1,0:T(8,128)S(1)}, u32[]{:S(2)}, u32[]{:S(2)}) collective-permute-start(f32[264,128]{1,0:T(8,128)S(1)} %pack.1.refs_0_), channel_id=1, source_target_pairs={{0,12},{4,8},{8,4},{12,0},{16,28},{20,24},{24,20},{28,16},{1,13},{... | collective-permute-start | bytes 405512 | tf_op jit(solution)/shard_map/ppermute | solution.py:671
  12.5 6.9 %collective-permute-start.3 = (f32[264,128]{1,0:T(8,128)S(1)}, f32[264,128]{1,0:T(8,128)S(1)}, u32[]{:S(2)}, u32[]{:S(2)}) collective-permute-start(f32[264,128]{1,0:T(8,128)S(1)} %collective-permute-done.refs_1_.refs_0_), channel_id=1, source_target_pairs={{0,8},{4,12},{8,0},{12,4},{16,24},{20,28},{24,16},{28,20},{1,9},{5... | collective-permute-start | bytes 405512 | tf_op jit(solution)/shard_map/ppermute | solution.py:671
  13.2 7.6 %collective-permute-start.2 = (f32[264,128]{1,0:T(8,128)S(1)}, f32[264,128]{1,0:T(8,128)S(1)}, u32[]{:S(2)}, u32[]{:S(2)}) collective-permute-start(f32[264,128]{1,0:T(8,128)S(1)} %collective-permute-done.refs_1_.refs_0_), channel_id=1, source_target_pairs={{0,4},{4,0},{8,12},{12,8},{16,20},{20,16},{24,28},{28,24},{1,5},{5... | collective-permute-start | bytes 405512 | tf_op jit(solution)/shard_map/ppermute | solution.py:671
  14.6 7.7 %collective-permute-start.1 = (f32[264,128]{1,0:T(8,128)S(1)}, f32[264,128]{1,0:T(8,128)S(1)}, u32[]{:S(2)}, u32[]{:S(2)}) collective-permute-start(f32[264,128]{1,0:T(8,128)S(1)} %collective-permute-done.refs_1_.refs_0_), channel_id=1, source_target_pairs={{0,12},{4,8},{8,4},{12,0},{16,28},{20,24},{24,20},{28,16},{1,13},{... | collective-permute-start | bytes 405512 | tf_op jit(solution)/shard_map/ppermute | solution.py:671
  18.0 5.8 %collective-permute-start.7 = (f32[40,8,128]{2,1,0:T(8,128)S(1)}, f32[40,8,128]{2,1,0:T(8,128)S(1)}, u32[]{:S(2)}, u32[]{:S(2)}) collective-permute-start(f32[40,8,128]{2,1,0:T(8,128)S(1)} %get-tuple-element.17), channel_id=1, source_target_pairs={{0,1},{2,3},{1,0},{3,2},{4,5},{6,7},{5,4},{7,6},{8,9},{10,11},{9,8... | collective-permute-start | bytes 491528 | tf_op jit(solution)/shard_map/ppermute | solution.py:680
  18.1 5.7 %collective-permute-start.8 = (f32[40,8,128]{2,1,0:T(8,128)S(1)}, f32[40,8,128]{2,1,0:T(8,128)S(1)}, u32[]{:S(2)}, u32[]{:S(2)}) collective-permute-start(f32[40,8,128]{2,1,0:T(8,128)S(1)} %get-tuple-element.18), channel_id=1, source_target_pairs={{1,2},{2,1},{5,6},{6,5},{9,10},{10,9},{13,14},{14,13},{17,18},{18,... | collective-permute-start | bytes 491528 | tf_op jit(solution)/shard_map/ppermute | solution.py:681
  23.1 2.7 %collective-permute-start.9 = (f32[25,8,128]{2,1,0:T(8,128)S(1)}, f32[25,8,128]{2,1,0:T(8,128)S(1)}, u32[]{:S(2)}, u32[]{:S(2)}) collective-permute-start(f32[25,8,128]{2,1,0:T(8,128)S(1)} %get-tuple-element.19), channel_id=1, source_target_pairs={{0,1},{2,3},{1,0},{3,2},{4,5},{6,7},{5,4},{7,6},{8,9},{10,11},{9,8... | collective-permute-start | bytes 307208 | tf_op jit(solution)/shard_map/ppermute | solution.py:680
  23.2 2.7 %collective-permute-start.10 = (f32[25,8,128]{2,1,0:T(8,128)S(1)}, f32[25,8,128]{2,1,0:T(8,128)S(1)}, u32[]{:S(2)}, u32[]{:S(2)}) collective-permute-start(f32[25,8,128]{2,1,0:T(8,128)S(1)} %get-tuple-element.20), channel_id=1, source_target_pairs={{1,2},{2,1},{5,6},{6,5},{9,10},{10,9},{13,14},{14,13},{17,18},{18,... | collective-permute-start | bytes 307208 | tf_op jit(solution)/shard_map/ppermute | solution.py:681

commit v4 on v3

--- a/solution.py
+++ b/solution.py
@@ -14,7 +14,11 @@
 KEEP = 1.0 - 6.0 * W
 HALO = 8
 LANES = 128
-UNROLL = 4
+UNROLL = 16
+PAIRS = 8
+HESS = 8
+LEVEL = 16
+LPAIRS = 4
 
 
 def is_coarsest(shape):
@@ -190,7 +194,7 @@
                 dst[z, c] = new[c]
             return carry
 
-        lax.fori_loop(1, zs + 1, body, 0, unroll=UNROLL)
+        lax.fori_loop(1, zs + 1, body, 0, unroll=LEVEL)
 
     sweep(q_ref, a_ref)
 
@@ -203,7 +207,7 @@
         tmp_ref[pl.ds(pl.multiple_of(z * rows, rows), rows), :] = 0.5 * pair_sum(total, 1, 1)
         return carry
 
-    lax.fori_loop(0, zs // 2, restrict, 0, unroll=2)
+    lax.fori_loop(0, zs // 2, restrict, 0, unroll=LPAIRS)
     tmp_ref[...] = flat_vcycle(tmp_ref[...], (zs // 2, ys // 2, xs // 2), rows, 1, 2)
 
     def correct(z, carry):
@@ -213,7 +217,7 @@
                 a_ref[at, c] = a_ref[at, c] + e
         return carry
 
-    lax.fori_loop(0, zs // 2, correct, 0, unroll=2)
+    lax.fori_loop(0, zs // 2, correct, 0, unroll=LPAIRS)
     sweep(a_ref, b_ref)
 
     def last_sweep(z, carry):
@@ -222,7 +226,7 @@
             v_ref[z, pl.ds(HALO + c, rows, stride=2), :] = new[c]
         return carry
 
-    lax.fori_loop(1, zs + 1, last_sweep, 0, unroll=UNROLL)
+    lax.fori_loop(1, zs + 1, last_sweep, 0, unroll=LEVEL)
 
 
 def pack_kernel(
@@ -418,7 +422,7 @@
             q_ref[j, c, pl.ds(part, 8), :] = (-W * mask) * source[c][part:]
         return carry
 
-    lax.fori_loop(0, half, body, 0, unroll=2)
+    lax.fori_loop(0, half, body, 0, unroll=HESS)
 
 
 def far_half_kernel(scalar_ref, *refs, depth, width, pencils):
@@ -481,7 +485,7 @@
         finish(source, far_first + j)
         return carry
 
-    lax.fori_loop(0, half, body, 0, unroll=2)
+    lax.fori_loop(0, half, body, 0, unroll=HESS)
     seam = jnp.where(lower, half, 1)
     here = parts(pn_ref, seam)
     inner = parts(pn_ref, jnp.where(lower, half - 1, 2))
@@ -523,7 +527,7 @@
         coarse_ref[pl.ds(pl.multiple_of(z * part, part), part), :] = 0.5 * total
         return carry
 
-    lax.fori_loop(0, planes // 2, restrict, 0, unroll=2)
+    lax.fori_loop(0, planes // 2, restrict, 0, unroll=PAIRS)
 
 
 def coarse_window(v_ref, z, pencil, part):
@@ -557,7 +561,7 @@
                 a_ref[at, c] = u_ref[at, c] + wide
         return carry
 
-    lax.fori_loop(0, planes // 2, correct, 0, unroll=2)
+    lax.fori_loop(0, planes // 2, correct, 0, unroll=PAIRS)
 
     def sweep(src, dst):
         def body(z, carry):

time: 64.6 us -> 59.6 us (0.923)
  Pallas kernels: 25 us -> 19.7 us
    pallas_call x7, Pallas kernels: 25 us -> 19.7 us  [call(): pl.pallas_call(kernel, out_shape=outs, in_specs=[smem()] * len(scalars) +...]
where the time goes in v4:
time: 59.6 us; the launch traced here: 59.4 us
  Pallas kernels  19.7 us (33%)
  blocking collectives  18.3 us (31%)
  starting transfers between devices  12.8 us (21%)
  waiting for transfers between devices  7.14 us (12%)
  other arithmetic  0.75 us (1%)
  between operations  0.75 us (1%)
    pallas_call x7, Pallas kernels, call(): pl.pallas_call(kernel, out_shape=outs, in_specs=[smem()] * len(scalars) +...  19.7 us
    all_gather x2, blocking collectives, gather(): return lax.all_gather(x, 'pencil', axis=0, tiled=False)  18.3 us
    ppermute x7, starting transfers between devices, swap(): return lax.ppermute(x, 'slab', [(i, i ^ bits) for i in range(slabs)])  11.3 us
    ppermute x7, waiting for transfers between devices, swap(): return lax.ppermute(x, 'slab', [(i, i ^ bits) for i in range(slabs)])  7.13 us
    ppermute x2, starting transfers between devices, beside(): lax.ppermute(odd, 'pencil', high_pairs + [(j, i) for i, j in high_pairs])  1.34 us
  transfers between devices with their start and end apart: 11, of which 5 were waited for; matrix products, arithmetic and copies ran while one was open for 1% of the time, Pallas kernels for 5%

profile of v4, /device:TPU:0, one launch (start us, length us, event | category | flops | bytes accessed | tf_op | source)
XLA Modules:
  0.0 59.4 jit_solution(6955830764998154979)
XLA Ops:
  0.6 1.2 %pack.1.refs_0_ = f32[264,128]{1,0:T(8,128)S(1)} custom-call(f32[4,32,256]{2,1,0:T(8,128)} %potential_hbm.1, f32[4,2,4,32]{3,2,1,0:T(4,128)} %store_hbm.1), custom_call_target="tpu_custom_call" | custom-call | tf_op jit(solution)/shard_map/pack/pallas_call | solution.py:638
  1.8 4.1 %collective-permute-start = (f32[264,128]{1,0:T(8,128)S(1)}, f32[264,128]{1,0:T(8,128)S(1)}, u32[]{:S(2)}, u32[]{:S(2)}) collective-permute-start(f32[264,128]{1,0:T(8,128)S(1)} %pack.1.refs_0_), channel_id=1, source_target_pairs={{0,16},{4,20},{8,24},{12,28},{16,0},{20,4},{24,8},{28,12},{1,17},{... | collective-permute-start | bytes 405512 | tf_op jit(solution)/shard_map/ppermute | solution.py:675
  5.9 1.6 %collective-permute-start.6 = (f32[264,128]{1,0:T(8,128)S(1)}, f32[264,128]{1,0:T(8,128)S(1)}, u32[]{:S(2)}, u32[]{:S(2)}) collective-permute-start(f32[264,128]{1,0:T(8,128)S(1)} %pack.1.refs_0_), channel_id=1, source_target_pairs={{0,8},{4,12},{8,0},{12,4},{16,24},{20,28},{24,16},{28,20},{1,9},{5... | collective-permute-start | bytes 405512 | tf_op jit(solution)/shard_map/ppermute | solution.py:675
  7.5 1.5 %collective-permute-start.5 = (f32[264,128]{1,0:T(8,128)S(1)}, f32[264,128]{1,0:T(8,128)S(1)}, u32[]{:S(2)}, u32[]{:S(2)}) collective-permute-start(f32[264,128]{1,0:T(8,128)S(1)} %pack.1.refs_0_), channel_id=1, source_target_pairs={{0,4},{4,0},{8,12},{12,8},{16,20},{20,16},{24,28},{28,24},{1,5},{5... | collective-permute-start | bytes 405512 | tf_op jit(solution)/shard_map/ppermute | solution.py:675
  9.0 0.4 collective-permute-start.4
  9.4 3.1 %collective-permute-done.refs_1_.refs_0_ = f32[264,128]{1,0:T(8,128)S(1)} collective-permute-done((f32[264,128]{1,0:T(8,128)S(1)}, f32[264,128]{1,0:T(8,128)S(1)}, u32[]{:S(2)}, u32[]{:S(2)}) %collective-permute-start) | collective-permute-done | bytes 135200 | tf_op jit(solution)/shard_map/ppermute | solution.py:675
  12.5 0.7 %collective-permute-start.3 = (f32[264,128]{1,0:T(8,128)S(1)}, f32[264,128]{1,0:T(8,128)S(1)}, u32[]{:S(2)}, u32[]{:S(2)}) collective-permute-start(f32[264,128]{1,0:T(8,128)S(1)} %collective-permute-done.refs_1_.refs_0_), channel_id=1, source_target_pairs={{0,8},{4,12},{8,0},{12,4},{16,24},{20,28},{24,16},{28,20},{1,9},{5... | collective-permute-start | bytes 405512 | tf_op jit(solution)/shard_map/ppermute | solution.py:675
  13.2 1.5 %collective-permute-start.2 = (f32[264,128]{1,0:T(8,128)S(1)}, f32[264,128]{1,0:T(8,128)S(1)}, u32[]{:S(2)}, u32[]{:S(2)}) collective-permute-start(f32[264,128]{1,0:T(8,128)S(1)} %collective-permute-done.refs_1_.refs_0_), channel_id=1, source_target_pairs={{0,4},{4,0},{8,12},{12,8},{16,20},{20,16},{24,28},{28,24},{1,5},{5... | collective-permute-start | bytes 405512 | tf_op jit(solution)/shard_map/ppermute | solution.py:675
  14.6 0.0 collective-permute-done.6.refs_4_.refs_3_
  14.6 1.6 %collective-permute-start.1 = (f32[264,128]{1,0:T(8,128)S(1)}, f32[264,128]{1,0:T(8,128)S(1)}, u32[]{:S(2)}, u32[]{:S(2)}) collective-permute-start(f32[264,128]{1,0:T(8,128)S(1)} %collective-permute-done.refs_1_.refs_0_), channel_id=1, source_target_pairs={{0,12},{4,8},{8,4},{12,0},{16,28},{20,24},{24,20},{28,16},{1,13},{... | collective-permute-start | bytes 405512 | tf_op jit(solution)/shard_map/ppermute | solution.py:675
  16.2 0.7 %pad_add_fusion.scalar_ref = s32[18]{0:T(128)S(1)} fusion(s32[8]{0:T(128)} %param.7, s32[8]{0:T(128)} %param.6, s32[1]{0:T(128)} %bitcast.1, s32[1]{0:T(128)} %bitcast), kind=kLoop, calls=%fused_computation | loop fusion | flops 54 | bytes 144 | tf_op jit(solution)/shard_map/concatenate | solution.py:657
  17.0 0.0 collective-permute-done.5.refs_3_.refs_2_
  17.0 0.5 collective-permute-done.4.refs_2_.refs_1_
  17.4 0.6 early_edges.1
  18.0 0.1 collective-permute-start.7
  18.1 0.7 %collective-permute-start.8 = (f32[40,8,128]{2,1,0:T(8,128)S(1)}, f32[40,8,128]{2,1,0:T(8,128)S(1)}, u32[]{:S(2)}, u32[]{:S(2)}) collective-permute-start(f32[40,8,128]{2,1,0:T(8,128)S(1)} %get-tuple-element.18), channel_id=1, source_target_pairs={{1,2},{2,1},{5,6},{6,5},{9,10},{10,9},{13,14},{14,13},{17,18},{18,... | collective-permute-start | bytes 491528 | tf_op jit(solution)/shard_map/ppermute | solution.py:685
  18.8 0.6 collective-permute-done.3.refs_7_.refs_3_
  19.3 1.4 %collective-permute-done.2.refs_6_.refs_2_ = f32[264,128]{1,0:T(8,128)S(1)} collective-permute-done((f32[264,128]{1,0:T(8,128)S(1)}, f32[264,128]{1,0:T(8,128)S(1)}, u32[]{:S(2)}, u32[]{:S(2)}) %collective-permute-start.2) | collective-permute-done | bytes 135200 | tf_op jit(solution)/shard_map/ppermute | solution.py:675
  20.8 1.6 %collective-permute-done.1.refs_5_.refs_1_ = f32[264,128]{1,0:T(8,128)S(1)} collective-permute-done((f32[264,128]{1,0:T(8,128)S(1)}, f32[264,128]{1,0:T(8,128)S(1)}, u32[]{:S(2)}, u32[]{:S(2)}) %collective-permute-start.1) | collective-permute-done | bytes 135200 | tf_op jit(solution)/shard_map/ppermute | solution.py:675
  22.3 0.7 %late_edges.1 = (f32[25,8,128]{2,1,0:T(8,128)S(1)}, f32[25,8,128]{2,1,0:T(8,128)S(1)}, f32[32,128]{1,0:T(8,128)S(1)}) custom-call(s32[18]{0:T(128)S(1)} %pad_add_fusion.scalar_ref, f32[264,128]{1,0:T(8,128)S(1)} %pack.1.refs_0_, f32[264,128]{1,0:T(8,128)S(1)} %collective-permute-done.refs_1_.refs_0_, f32[264,128]{1,0:T(8,128)S(1)} %collective-permute-done.4.refs_2_.refs_1_, ...), custom_call_target="tpu_custom_call" | custom-call | tf_op jit(solution)/shard_map/late_edges/pallas_call | solution.py:638
  23.1 0.1 collective-permute-start.9
  23.2 0.7 %collective-permute-start.10 = (f32[25,8,128]{2,1,0:T(8,128)S(1)}, f32[25,8,128]{2,1,0:T(8,128)S(1)}, u32[]{:S(2)}, u32[]{:S(2)}) collective-permute-start(f32[25,8,128]{2,1,0:T(8,128)S(1)} %get-tuple-element.20), channel_id=1, source_target_pairs={{1,2},{2,1},{5,6},{6,5},{9,10},{10,9},{13,14},{14,13},{17,18},{18,... | collective-permute-start | bytes 307208 | tf_op jit(solution)/shard_map/ppermute | solution.py:685
  23.8 0.0 collective-permute-done.7.refs_4_
  23.8 0.0 collective-permute-done.8.refs_5_
  23.8 1.6 %near_half.1 = (f32[18,4,24,128]{3,2,1,0:T(8,128)S(1)}, f32[16,4,16,128]{3,2,1,0:T(8,128)S(1)}, f32[16,4,24,128]{3,2,1,0:T(8,128)S(1)}) custom-call(s32[18]{0:T(128)S(1)} %pad_add_fusion.scalar_ref, f32[264,128]{1,0:T(8,128)S(1)} %pack.1.refs_0_, f32[264,128]{1,0:T(8,128)S(1)} %collective-permute-done.4.refs_2_.refs_1_, ...), custom_call_target="tpu_custom_call" | custom-call | tf_op jit(solution)/shard_map/near_half/pallas_call | solution.py:638
  25.5 0.0 collective-permute-done.9.refs_6_
  25.5 0.0 collective-permute-done.10.refs_7_
  25.5 3.5 %far_half.1 = (f32[4,32,256]{2,1,0:T(8,128)}, f32[36,4,24,128]{3,2,1,0:T(8,128)S(1)}, f32[36,4,24,128]{3,2,1,0:T(8,128)S(1)}, f32[256,128]{1,0:T(8,128)S(1)}) custom-call(s32[18]{0:T(128)S(1)} %pad_add_fusion.scalar_ref, f32[264,128]{1,0:T(8,128)S(1)} %collective-permute-done.refs_1_.refs_0_, f32[264,128]{1,0:T(8,128)S(1)} %collective-permute-done.1.refs_5_.refs_1_, ...), custom_call_target="tpu_custom_call" | custom-call | tf_op jit(solution)/shard_map/far_half/pallas_call | solution.py:638
  29.0 11.0 %all-gather = f32[1024,128]{1,0:T(8,128)S(1)} all-gather(f32[256,128]{1,0:T(8,128)S(1)} %get-tuple-element.25), channel_id=2, replica_groups=mesh['slab'=8,'pencil'=4] {'pencil'}, dimensions={0}, use_global_device_ids=true | all-gather | bytes 655360 | tf_op jit(solution)/shard_map/all_gather | solution.py:745
  40.0 7.4 %middle.1 = (f32[8,4,24,128]{3,2,1,0:T(8,128)S(1)}, f32[8,4,24,128]{3,2,1,0:T(8,128)S(1)}, f32[256,128]{1,0:T(8,128)S(1)}) custom-call(s32[18]{0:T(128)S(1)} %pad_add_fusion.scalar_ref, f32[4,256,128]{2,1,0:T(8,128)S(1)} %bitcast.4, f32[36,4,24,128]{3,2,1,0:T(8,128)S(1)} %get-tuple-element.26.q_ref, f32[36,4,24,128]{3,2,1,0:T(8,128)S(1)} %get-tuple-element.27.u_ref), custom_call_target="tpu_custom_call" | custom-call | tf_op jit(solution)/shard_map/middle/pallas_call | solution.py:638
  47.5 7.3 %all-gather.1 = f32[1024,128]{1,0:T(8,128)S(1)} all-gather(f32[256,128]{1,0:T(8,128)S(1)} %get-tuple-element.28), channel_id=3, replica_groups=mesh['slab'=8,'pencil'=4] {'pencil'}, dimensions={0}, use_global_device_ids=true | all-gather | bytes 655360 | tf_op jit(solution)/shard_map/all_gather | solution.py:745
  54.8 4.6 %last.1 = f32[4,32,256]{2,1,0:T(8,128)} custom-call(s32[18]{0:T(128)S(1)} %pad_add_fusion.scalar_ref, f32[4,256,128]{2,1,0:T(8,128)S(1)} %bitcast.5, f32[8,4,24,128]{3,2,1,0:T(8,128)S(1)} %get-tuple-element.29.qwin_ref, f32[8,4,24,128]{3,2,1,0:T(8,128)S(1)} %get-tuple-element.30.uwin_ref), custom_call_target="tpu_custom_call" | custom-call | tf_op jit(solution)/shard_map/last/pallas_call | solution.py:638
Async XLA Ops:
  1.8 10.7 %collective-permute-start = (f32[264,128]{1,0:T(8,128)S(1)}, f32[264,128]{1,0:T(8,128)S(1)}, u32[]{:S(2)}, u32[]{:S(2)}) collective-permute-start(f32[264,128]{1,0:T(8,128)S(1)} %pack.1.refs_0_), channel_id=1, source_target_pairs={{0,16},{4,20},{8,24},{12,28},{16,0},{20,4},{24,8},{28,12},{1,17},{... | collective-permute-start | bytes 405512 | tf_op jit(solution)/shard_map/ppermute | solution.py:675
  5.9 8.7 %collective-permute-start.6 = (f32[264,128]{1,0:T(8,128)S(1)}, f32[264,128]{1,0:T(8,128)S(1)}, u32[]{:S(2)}, u32[]{:S(2)}) collective-permute-start(f32[264,128]{1,0:T(8,128)S(1)} %pack.1.refs_0_), channel_id=1, source_target_pairs={{0,8},{4,12},{8,0},{12,4},{16,24},{20,28},{24,16},{28,20},{1,9},{5... | collective-permute-start | bytes 405512 | tf_op jit(solution)/shard_map/ppermute | solution.py:675
  7.5 9.5 %collective-permute-start.5 = (f32[264,128]{1,0:T(8,128)S(1)}, f32[264,128]{1,0:T(8,128)S(1)}, u32[]{:S(2)}, u32[]{:S(2)}) collective-permute-start(f32[264,128]{1,0:T(8,128)S(1)} %pack.1.refs_0_), channel_id=1, source_target_pairs={{0,4},{4,0},{8,12},{12,8},{16,20},{20,16},{24,28},{28,24},{1,5},{5... | collective-permute-start | bytes 405512 | tf_op jit(solution)/shard_map/ppermute | solution.py:675
  9.0 8.5 %collective-permute-start.4 = (f32[264,128]{1,0:T(8,128)S(1)}, f32[264,128]{1,0:T(8,128)S(1)}, u32[]{:S(2)}, u32[]{:S(2)}) collective-permute-start(f32[264,128]{1,0:T(8,128)S(1)} %pack.1.refs_0_), channel_id=1, source_target_pairs={{0,12},{4,8},{8,4},{12,0},{16,28},{20,24},{24,20},{28,16},{1,13},{... | collective-permute-start | bytes 405512 | tf_op jit(solution)/shard_map/ppermute | solution.py:675
  12.5 6.9 %collective-permute-start.3 = (f32[264,128]{1,0:T(8,128)S(1)}, f32[264,128]{1,0:T(8,128)S(1)}, u32[]{:S(2)}, u32[]{:S(2)}) collective-permute-start(f32[264,128]{1,0:T(8,128)S(1)} %collective-permute-done.refs_1_.refs_0_), channel_id=1, source_target_pairs={{0,8},{4,12},{8,0},{12,4},{16,24},{20,28},{24,16},{28,20},{1,9},{5... | collective-permute-start | bytes 405512 | tf_op jit(solution)/shard_map/ppermute | solution.py:675
  13.2 7.6 %collective-permute-start.2 = (f32[264,128]{1,0:T(8,128)S(1)}, f32[264,128]{1,0:T(8,128)S(1)}, u32[]{:S(2)}, u32[]{:S(2)}) collective-permute-start(f32[264,128]{1,0:T(8,128)S(1)} %collective-permute-done.refs_1_.refs_0_), channel_id=1, source_target_pairs={{0,4},{4,0},{8,12},{12,8},{16,20},{20,16},{24,28},{28,24},{1,5},{5... | collective-permute-start | bytes 405512 | tf_op jit(solution)/shard_map/ppermute | solution.py:675
  14.6 7.7 %collective-permute-start.1 = (f32[264,128]{1,0:T(8,128)S(1)}, f32[264,128]{1,0:T(8,128)S(1)}, u32[]{:S(2)}, u32[]{:S(2)}) collective-permute-start(f32[264,128]{1,0:T(8,128)S(1)} %collective-permute-done.refs_1_.refs_0_), channel_id=1, source_target_pairs={{0,12},{4,8},{8,4},{12,0},{16,28},{20,24},{24,20},{28,16},{1,13},{... | collective-permute-start | bytes 405512 | tf_op jit(solution)/shard_map/ppermute | solution.py:675
  18.0 5.8 %collective-permute-start.7 = (f32[40,8,128]{2,1,0:T(8,128)S(1)}, f32[40,8,128]{2,1,0:T(8,128)S(1)}, u32[]{:S(2)}, u32[]{:S(2)}) collective-permute-start(f32[40,8,128]{2,1,0:T(8,128)S(1)} %get-tuple-element.17), channel_id=1, source_target_pairs={{0,1},{2,3},{1,0},{3,2},{4,5},{6,7},{5,4},{7,6},{8,9},{10,11},{9,8... | collective-permute-start | bytes 491528 | tf_op jit(solution)/shard_map/ppermute | solution.py:684
  18.1 5.7 %collective-permute-start.8 = (f32[40,8,128]{2,1,0:T(8,128)S(1)}, f32[40,8,128]{2,1,0:T(8,128)S(1)}, u32[]{:S(2)}, u32[]{:S(2)}) collective-permute-start(f32[40,8,128]{2,1,0:T(8,128)S(1)} %get-tuple-element.18), channel_id=1, source_target_pairs={{1,2},{2,1},{5,6},{6,5},{9,10},{10,9},{13,14},{14,13},{17,18},{18,... | collective-permute-start | bytes 491528 | tf_op jit(solution)/shard_map/ppermute | solution.py:685
  23.1 2.4 %collective-permute-start.9 = (f32[25,8,128]{2,1,0:T(8,128)S(1)}, f32[25,8,128]{2,1,0:T(8,128)S(1)}, u32[]{:S(2)}, u32[]{:S(2)}) collective-permute-start(f32[25,8,128]{2,1,0:T(8,128)S(1)} %get-tuple-element.19), channel_id=1, source_target_pairs={{0,1},{2,3},{1,0},{3,2},{4,5},{6,7},{5,4},{7,6},{8,9},{10,11},{9,8... | collective-permute-start | bytes 307208 | tf_op jit(solution)/shard_map/ppermute | solution.py:684
  23.2 2.3 %collective-permute-start.10 = (f32[25,8,128]{2,1,0:T(8,128)S(1)}, f32[25,8,128]{2,1,0:T(8,128)S(1)}, u32[]{:S(2)}, u32[]{:S(2)}) collective-permute-start(f32[25,8,128]{2,1,0:T(8,128)S(1)} %get-tuple-element.20), channel_id=1, source_target_pairs={{1,2},{2,1},{5,6},{6,5},{9,10},{10,9},{13,14},{14,13},{17,18},{18,... | collective-permute-start | bytes 307208 | tf_op jit(solution)/shard_map/ppermute | solution.py:685

commit v5 on v4

--- a/solution.py
+++ b/solution.py
@@ -44,11 +44,24 @@
     return pltpu.roll(values, values.shape[0] - 1 if odd else 1, 0)
 
 
-def swept(below, here, above, q, c):
+def neighbours(below, here, above, c):
     across, along = here[c ^ 1], here[c ^ 2]
     near = (below + above) + (across + x_other(across, c & 1))
-    near = near + (along + y_other(along, c >> 1))
-    return KEEP * here[c] + W * near + q
+    return near + (along + y_other(along, c >> 1))
+
+
+def swept(below, here, above, q, c):
+    return KEEP * here[c] + W * neighbours(below, here, above, c) + q
+
+
+def swept_children(below, here, above):
+    here = W * here
+    base = ((1.0 - 3.0 * W) / W) * here
+    beyond = [W * below, W * above]
+    across = [base + x_other(here, odd) for odd in range(2)]
+    along = [y_other(here, odd) for odd in range(2)]
+    flat = [across[c & 1] + along[c >> 1] for c in range(4)]
+    return [[one + beyond[k] for one in flat] for k in range(2)]
 
 
 def parts(ref, z):
@@ -150,83 +163,108 @@
     return flat_sweep(u, q, rows, yd, xd)
 
 
-def solve_level_one(gathered_ref, v_ref, q_ref, a_ref, b_ref, tmp_ref, shape):
+def solve_level_one(gathered_ref, v_ref, q_ref, a_ref, b_ref, tmp_ref, shape, near=None):
     zs, ys, xs = shape
     pencils = gathered_ref.shape[0]
     rows = ys // 2
+    half = zs // 2
     piece = rows // pencils
     row = row_iota((rows, LANES))
     blank = jnp.zeros((rows, LANES), jnp.float32)
     for ref in (q_ref, a_ref, b_ref):
-        for z in (0, zs + 1):
+        for z in (0, 1, zs + 2, zs + 3):
             for c in range(2):
                 ref[z, c] = blank
+    for z in (0, 1, half + 2, half + 3):
+        tmp_ref[pl.ds(z * rows, rows), :] = blank
     edge = jnp.zeros((HALO, LANES), jnp.float32)
     for z in range(zs + 2):
         v_ref[z, pl.ds(0, HALO), :] = edge
         v_ref[z, pl.ds(HALO + ys, HALO), :] = edge
-    for z in (0, zs + 1):
-        for c in range(2):
-            v_ref[z, pl.ds(HALO + c * rows, rows), :] = blank
+    if near is None:
+        for z in (0, zs + 1):
+            for c in range(2):
+                v_ref[z, pl.ds(HALO + c * rows, rows), :] = blank
     for z in range(zs):
         for c in range(2):
             for p in range(pencils):
                 spot = pl.ds(2 * piece * z + c, piece, stride=2)
-                q_ref[z + 1, c, pl.ds(p * piece, piece), :] = gathered_ref[p, spot, :]
-
-    def sweep_plane(src, z):
+                q_ref[z + 2, c, pl.ds(p * piece, piece), :] = gathered_ref[p, spot, :]
+
+    def y_beyond(other, c):
+        if c:
+            return jnp.where(row == rows - 1, 0.0, pltpu.roll(other, rows - 1, 0))
+        return jnp.where(row == 0, 0.0, pltpu.roll(other, 1, 0))
+
+    def around(src, z):
         here = [src[z, 0], src[z, 1]]
-        new = []
+        near = []
         for c in range(2):
             other = here[1 - c]
-            if c:
-                beyond = jnp.where(row == rows - 1, 0.0, pltpu.roll(other, rows - 1, 0))
-            else:
-                beyond = jnp.where(row == 0, 0.0, pltpu.roll(other, 1, 0))
-            near = (src[z - 1, c] + src[z + 1, c]) + (other + beyond) + x_sides(here[c], 1)
-            new.append(KEEP * here[c] + W * near + q_ref[z, c])
-        return here, new
-
-    def sweep(src, dst):
-        def body(z, carry):
-            _, new = sweep_plane(src, z)
-            for c in range(2):
-                dst[z, c] = new[c]
-            return carry
-
-        lax.fori_loop(1, zs + 1, body, 0, unroll=LEVEL)
-
-    sweep(q_ref, a_ref)
+            sides = (other + y_beyond(other, c)) + x_sides(here[c], 1)
+            near.append((src[z - 1, c] + src[z + 1, c]) + sides)
+        return here, near
+
+    def second(z, carry):
+        here, sides = around(q_ref, z)
+        for c in range(2):
+            a_ref[z, c] = (1.0 + KEEP) * here[c] + W * sides[c]
+        return carry
+
+    lax.fori_loop(2, zs + 2, second, 0, unroll=LEVEL)
 
     def restrict(z, carry):
         total = None
-        for at in (2 * z + 1, 2 * z + 2):
-            here, new = sweep_plane(a_ref, at)
-            change = (new[0] - here[0]) + (new[1] - here[1])
-            total = change if total is None else total + change
-        tmp_ref[pl.ds(pl.multiple_of(z * rows, rows), rows), :] = 0.5 * pair_sum(total, 1, 1)
+        for at in (2 * z + 2, 2 * z + 3):
+            here, sides = around(a_ref, at)
+            for c in range(2):
+                new = KEEP * here[c] + W * sides[c] + q_ref[at, c]
+                b_ref[at, c] = new
+                change = new - here[c]
+                total = change if total is None else total + change
+        spot = pl.ds(pl.multiple_of((z + 2) * rows, rows), rows)
+        tmp_ref[spot, :] = 0.5 * pair_sum(total, 1, 1)
         return carry
 
-    lax.fori_loop(0, zs // 2, restrict, 0, unroll=LPAIRS)
-    tmp_ref[...] = flat_vcycle(tmp_ref[...], (zs // 2, ys // 2, xs // 2), rows, 1, 2)
-
-    def correct(z, carry):
-        e = tmp_ref[pl.ds(pl.multiple_of(z * rows, rows), rows), :]
-        for at in (2 * z + 1, 2 * z + 2):
-            for c in range(2):
-                a_ref[at, c] = a_ref[at, c] + e
-        return carry
-
-    lax.fori_loop(0, zs // 2, correct, 0, unroll=LPAIRS)
-    sweep(a_ref, b_ref)
-
-    def last_sweep(z, carry):
-        _, new = sweep_plane(b_ref, z)
+    pairs_unroll = LPAIRS if near is None else half
+    lax.fori_loop(0, half, restrict, 0, unroll=pairs_unroll)
+    inner = pl.ds(2 * rows, half * rows)
+    tmp_ref[inner, :] = flat_vcycle(tmp_ref[inner, :], (half, ys // 2, xs // 2), rows, 1, 2)
+
+    def live(at, count):
+        return jnp.where((at >= 0) & (at < count), 1.0, 0.0)
+
+    def third(z):
+        e = [tmp_ref[pl.ds(pl.multiple_of((z + k) * rows, rows), rows), :] for k in (1, 2, 3)]
+        here = W * e[1]
+        base = ((1.0 - 4.0 * W) / W) * here + x_sides(here, 1)
         for c in range(2):
-            v_ref[z, pl.ds(HALO + c, rows, stride=2), :] = new[c]
-        return carry
-
-    lax.fori_loop(1, zs + 1, last_sweep, 0, unroll=LEVEL)
+            flat = base + y_beyond(here, c)
+            for k in range(2):
+                new = b_ref[2 * z + 2 + k, c] + (flat + W * e[2 * k])
+                a_ref[2 * z + 2 + k, c] = new if near is None else live(z, half) * new
+
+    def fourth(z):
+        here, sides = around(a_ref, z + 2)
+        for c in range(2):
+            new = KEEP * here[c] + W * sides[c] + q_ref[z + 2, c]
+            if near is not None:
+                new = live(z, zs) * new
+            v_ref[z + 1, pl.ds(HALO + c, rows, stride=2), :] = new
+
+    def loop(step, start, count, unroll):
+        def body(i, carry):
+            step(start + i)
+            return carry
+
+        lax.fori_loop(0, count, body, 0, unroll=unroll)
+
+    if near is None:
+        loop(third, 0, half, LPAIRS)
+        loop(fourth, 0, zs, LEVEL)
+    else:
+        loop(third, near - 1, 3, 3)
+        loop(fourth, 2 * near - 1, 4, 4)
 
 
 def pack_kernel(
@@ -431,8 +469,8 @@
     early_refs = refs[len(far) : len(far) + 2]
     late_refs = refs[len(far) + 2 : len(far) + 4]
     faces_ref, pn_ref, sn_ref, qn_ref = refs[len(far) + 4 : len(far) + 8]
-    source_hbm, q_ref, u_ref, coarse_ref = refs[len(far) + 8 : len(far) + 12]
-    p_ref, f_ref, s_ref, left_ref, right_ref, source_ref, sem = refs[len(far) + 12 :]
+    source_hbm, q_ref, swept_ref, coarse_ref = refs[len(far) + 8 : len(far) + 12]
+    p_ref, f_ref, s_ref, u_ref, left_ref, right_ref, source_ref, sem = refs[len(far) + 12 :]
     slab = scalar_ref[0]
     pencil = scalar_ref[1]
     part = width // 2
@@ -446,7 +484,7 @@
     mask = halo_mask(pencil, pencils)
     blank = jnp.zeros(p_ref.shape[1:], jnp.float32)
     for ref in (q_ref, u_ref):
-        for z in (0, 1, planes + 2, planes + 3):
+        for z in (1, planes + 2):
             ref[z] = blank
     p_ref[jnp.where(lower, half + 1, 0)] = blank
     p_ref[jnp.where(lower, 0, half + 1)] = pn_ref[jnp.where(lower, half, 1)]
@@ -506,23 +544,24 @@
     def second_sweep(z, carry):
         here = parts(q_ref, z + 2)
         for c in range(4):
-            new = swept(q_ref[z + 1, c], here, q_ref[z + 3, c], here[c], c)
-            put(u_ref, z + 2, c, new, mask)
+            sides = neighbours(q_ref[z + 1, c], here, q_ref[z + 3, c], c)
+            put(u_ref, z + 2, c, (1.0 + KEEP) * here[c] + W * sides, mask)
         return carry
 
     lax.fori_loop(0, planes, second_sweep, 0, unroll=UNROLL)
-    restrict_window(u_ref, q_ref, coarse_ref, planes, part)
+    restrict_window(u_ref, q_ref, coarse_ref, swept_ref, mask, planes, part)
     copy_out.wait()
 
 
-def restrict_window(u_ref, q_ref, coarse_ref, planes, part):
+def restrict_window(u_ref, q_ref, coarse_ref, swept_ref, mask, planes, part):
     def restrict(z, carry):
         total = None
         for at in (2 * z + 2, 2 * z + 3):
             here = parts(u_ref, at)
             for c in range(4):
                 new = swept(u_ref[at - 1, c], here, u_ref[at + 1, c], q_ref[at, c], c)
-                change = (new - here[c])[:part]
+                put(swept_ref, at, c, new, mask)
+                change = new[:part] - here[c][:part]
                 total = change if total is None else total + change
         coarse_ref[pl.ds(pl.multiple_of(z * part, part), part), :] = 0.5 * total
         return carry
@@ -540,7 +579,7 @@
 
 
 def middle_kernel(
-    scalar_ref, gathered_ref, q_ref, u_ref, qwin_ref, uwin_ref, coarse_ref,
+    scalar_ref, gathered_ref, q_ref, swept_ref, qwin_ref, win_ref, coarse_ref,
     v_ref, q1_ref, a1_ref, b1_ref, tmp_ref, a_ref, b_ref, *, depth, width, pencils, shape
 ):
     slab = scalar_ref[0]
@@ -551,17 +590,18 @@
     solve_level_one(gathered_ref, v_ref, q1_ref, a1_ref, b1_ref, tmp_ref, shape)
     blank = jnp.zeros(a_ref.shape[1:], jnp.float32)
     for ref in (a_ref, b_ref):
-        for z in (0, 1, planes + 2, planes + 3):
+        for z in (1, planes + 2):
             ref[z] = blank
 
-    def correct(z, carry):
-        wide = coarse_window(v_ref, z + 1, pencil, part)
-        for at in (2 * z + 2, 2 * z + 3):
+    def third_sweep(z, carry):
+        v = [coarse_window(v_ref, z + k, pencil, part) for k in range(3)]
+        for k, children in enumerate(swept_children(*v)):
+            at = 2 * z + 2 + k
             for c in range(4):
-                a_ref[at, c] = u_ref[at, c] + wide
+                put(a_ref, at, c, swept_ref[at, c] + children[c], mask)
         return carry
 
-    lax.fori_loop(0, planes // 2, correct, 0, unroll=PAIRS)
+    lax.fori_loop(0, planes // 2, third_sweep, 0, unroll=PAIRS)
 
     def sweep(src, dst):
         def body(z, carry):
@@ -576,16 +616,16 @@
     sweep(a_ref, b_ref)
     sweep(b_ref, a_ref)
     sweep(a_ref, b_ref)
-    sweep(b_ref, a_ref)
-    restrict_window(a_ref, q_ref, coarse_ref, planes, part)
-    for z in range(depth + 4):
-        qwin_ref[z] = q_ref[slab * depth + z]
-        uwin_ref[z] = a_ref[slab * depth + z]
+    restrict_window(b_ref, q_ref, coarse_ref, a_ref, mask, planes, part)
+    for z in range(depth):
+        qwin_ref[z] = q_ref[slab * depth + z + 2]
+    for z in range(depth + 2):
+        win_ref[z] = a_ref[slab * depth + z + 1]
 
 
 def last_kernel(
-    scalar_ref, gathered_ref, qwin_ref, uwin_ref, out_ref,
-    v_ref, q1_ref, a1_ref, b1_ref, tmp_ref, a_ref, b_ref, left_ref, right_ref,
+    scalar_ref, gathered_ref, qwin_ref, win_ref, out_hbm,
+    v_ref, q1_ref, a1_ref, b1_ref, tmp_ref, a_ref, left_ref, right_ref, out_ref, sems,
     *, depth, width, pencils, shape
 ):
     slab = scalar_ref[0]
@@ -593,26 +633,31 @@
     planes = shape[0] * 2
     part = width // 2
     mask = halo_mask(pencil, pencils)
-    solve_level_one(gathered_ref, v_ref, q1_ref, a1_ref, b1_ref, tmp_ref, shape)
-    for z in range(depth // 2 + 2):
-        wide = coarse_window(v_ref, slab * (depth // 2) + z, pencil, part)
-        for at in (2 * z, 2 * z + 1):
-            for c in range(4):
-                a_ref[at, c] = uwin_ref[at, c] + wide
-    for z in range(1, depth + 3):
-        at = slab * depth - 2 + z
-        live = jnp.where((at >= 0) & (at < planes), 1.0, 0.0)
-        here = parts(a_ref, z)
+    solve_level_one(gathered_ref, v_ref, q1_ref, a1_ref, b1_ref, tmp_ref, shape, slab)
+    blank = jnp.zeros((part + 8, LANES), jnp.float32)
+    v = [coarse_window(v_ref, slab * (depth // 2) + k, pencil, part) for k in range(4)]
+    v = [blank] + v + [blank]
+    for k in range(4):
+        for side, children in enumerate(swept_children(*v[k : k + 3])):
+            z = 2 * k + side - 1
+            if 0 <= z < depth + 2:
+                at = slab * depth - 1 + z
+                live = jnp.where((at >= 0) & (at < planes), 1.0, 0.0)
+                for c in range(4):
+                    put(a_ref, z, c, live * (win_ref[z, c] + children[c]), mask)
+    matrix = merging_matrix()
+    copies = []
+    for z in range(depth):
+        here = parts(a_ref, z + 1)
         for c in range(4):
-            new = swept(a_ref[z - 1, c], here, a_ref[z + 1, c], qwin_ref[z, c], c)
-            put(b_ref, z, c, live * new, mask)
-    done = {}
-    for z in range(2, depth + 2):
-        here = parts(b_ref, z)
-        for c in range(4):
-            new = swept(b_ref[z - 1, c], here, b_ref[z + 1, c], qwin_ref[z, c], c)
-            done[z - 2, c] = new[:part]
-    join_planes(lambda z, c: done[z, c], out_ref, left_ref, right_ref, depth, width)
+            new = swept(a_ref[z, c], here, a_ref[z + 2, c], qwin_ref[z, c], c)
+            ref = right_ref if c & 1 else left_ref
+            ref[z, pl.ds(c >> 1, part, stride=2), :] = new[:part]
+        out_ref[z] = mm(jnp.concatenate([left_ref[z], right_ref[z]], axis=1), matrix)
+        copies.append(pltpu.make_async_copy(out_ref.at[z], out_hbm.at[z], sems.at[z]))
+        copies[-1].start()
+    for copy in copies:
+        copy.wait()
 
 
 def vmem():
@@ -715,7 +760,7 @@
         [b for b, offset in zip(blocks, OFFSETS) if offset < 4] + [*early, faces],
         (arr(half + 2, 4, rows, LANES), arr(half, 4, part, LANES), arr(half, 4, rows, LANES)),
     )
-    source, q, u, coarse = call(
+    source, q, swept_once, coarse = call(
         partial(far_half_kernel, depth=depth, width=width, pencils=pencils),
         "far_half",
         [scalars],
@@ -725,6 +770,7 @@
             buf(half + 2, 4, rows, LANES),
             buf(2, rows, LANES),
             buf(depth, 4, part, LANES),
+            buf(*field),
             buf(depth * width, LANES),
             buf(depth * width, LANES),
             buf(depth, width, columns),
@@ -732,36 +778,42 @@
         ],
         out_space=[pl.ANY] + [pltpu.VMEM] * 3,
     )
-    level = (shape[0] + 2, 2, shape[1] // 2, LANES)
+    level = (shape[0] + 4, 2, shape[1] // 2, LANES)
     level_scratch = [
         buf(shape[0] + 2, shape[1] + 2 * HALO, LANES),
         buf(*level),
         buf(*level),
         buf(*level),
-        buf(shape[0] * shape[1] // 4, LANES),
+        buf((shape[0] // 2 + 4) * shape[1] // 2, LANES),
     ]
 
     def gather(x):
         return lax.all_gather(x, "pencil", axis=0, tiled=False)
 
     sizes = dict(depth=depth, width=width, pencils=pencils, shape=shape)
-    slim = (depth + 4, 4, rows, LANES)
-    qwin, uwin, coarse = call(
+    qwin, win, coarse = call(
         partial(middle_kernel, **sizes),
         "middle",
         [scalars],
-        [gather(coarse), q, u],
-        (arr(*slim), arr(*slim), coarse_part),
+        [gather(coarse), q, swept_once],
+        (arr(depth, 4, rows, LANES), arr(depth + 2, 4, rows, LANES), coarse_part),
         level_scratch + [buf(*field), buf(*field)],
     )
-    solved = call(
+    (solved,) = call(
         partial(last_kernel, **sizes),
         "last",
         [scalars],
-        [gather(coarse), qwin, uwin],
-        arr(depth, width, columns),
+        [gather(coarse), qwin, win],
+        (arr(depth, width, columns),),
         level_scratch
-        + [buf(*slim), buf(*slim), buf(depth * width, LANES), buf(depth * width, LANES)],
+        + [
+            buf(depth + 2, 4, rows, LANES),
+            buf(depth, width, LANES),
+            buf(depth, width, LANES),
+            buf(depth, width, columns),
+            pltpu.SemaphoreType.DMA((depth,)),
+        ],
+        out_space=[pl.ANY],
     )
     return solved, source
 

time: 59.6 us -> 58.7 us (0.985)
  Pallas kernels: 19.7 us -> 18.7 us
    pallas_call x7, Pallas kernels: 19.7 us -> 18.7 us  [call(): pl.pallas_call(kernel, out_shape=outs, in_specs=[smem()] * len(scalars) +...]
where the time goes in v5:
time: 58.7 us; the launch traced here: 58.5 us
  Pallas kernels  18.7 us (32%)
  blocking collectives  18.3 us (31%)
  starting transfers between devices  12.8 us (22%)
  waiting for transfers between devices  7.14 us (12%)
  other arithmetic  0.75 us (1%)
  between operations  0.75 us (1%)
    pallas_call x7, Pallas kernels, call(): pl.pallas_call(kernel, out_shape=outs, in_specs=[smem()] * len(scalars) +...  18.7 us
    all_gather x2, blocking collectives, gather(): return lax.all_gather(x, 'pencil', axis=0, tiled=False)  18.3 us
    ppermute x7, starting transfers between devices, swap(): return lax.ppermute(x, 'slab', [(i, i ^ bits) for i in range(slabs)])  11.3 us
    ppermute x7, waiting for transfers between devices, swap(): return lax.ppermute(x, 'slab', [(i, i ^ bits) for i in range(slabs)])  7.13 us
    ppermute x2, starting transfers between devices, beside(): lax.ppermute(odd, 'pencil', high_pairs + [(j, i) for i, j in high_pairs])  1.34 us
  transfers between devices with their start and end apart: 11, of which 5 were waited for; matrix products, arithmetic and copies ran while one was open for 1% of the time, Pallas kernels for 5%

profile of v5, /device:TPU:0, one launch (start us, length us, event | category | flops | bytes accessed | tf_op | source)
XLA Modules:
  0.0 58.5 jit_solution(10347085345768493541)
XLA Ops:
  0.6 1.2 %pack.1.refs_0_ = f32[264,128]{1,0:T(8,128)S(1)} custom-call(f32[4,32,256]{2,1,0:T(8,128)} %potential_hbm.1, f32[4,2,4,32]{3,2,1,0:T(4,128)} %store_hbm.1), custom_call_target="tpu_custom_call" | custom-call | tf_op jit(solution)/shard_map/pack/pallas_call | solution.py:683
  1.8 4.1 %collective-permute-start = (f32[264,128]{1,0:T(8,128)S(1)}, f32[264,128]{1,0:T(8,128)S(1)}, u32[]{:S(2)}, u32[]{:S(2)}) collective-permute-start(f32[264,128]{1,0:T(8,128)S(1)} %pack.1.refs_0_), channel_id=1, source_target_pairs={{0,16},{4,20},{8,24},{12,28},{16,0},{20,4},{24,8},{28,12},{1,17},{... | collective-permute-start | bytes 405512 | tf_op jit(solution)/shard_map/ppermute | solution.py:720
  5.9 1.6 %collective-permute-start.6 = (f32[264,128]{1,0:T(8,128)S(1)}, f32[264,128]{1,0:T(8,128)S(1)}, u32[]{:S(2)}, u32[]{:S(2)}) collective-permute-start(f32[264,128]{1,0:T(8,128)S(1)} %pack.1.refs_0_), channel_id=1, source_target_pairs={{0,8},{4,12},{8,0},{12,4},{16,24},{20,28},{24,16},{28,20},{1,9},{5... | collective-permute-start | bytes 405512 | tf_op jit(solution)/shard_map/ppermute | solution.py:720
  7.5 1.5 %collective-permute-start.5 = (f32[264,128]{1,0:T(8,128)S(1)}, f32[264,128]{1,0:T(8,128)S(1)}, u32[]{:S(2)}, u32[]{:S(2)}) collective-permute-start(f32[264,128]{1,0:T(8,128)S(1)} %pack.1.refs_0_), channel_id=1, source_target_pairs={{0,4},{4,0},{8,12},{12,8},{16,20},{20,16},{24,28},{28,24},{1,5},{5... | collective-permute-start | bytes 405512 | tf_op jit(solution)/shard_map/ppermute | solution.py:720
  9.0 0.4 collective-permute-start.4
  9.4 3.1 %collective-permute-done.refs_1_.refs_0_ = f32[264,128]{1,0:T(8,128)S(1)} collective-permute-done((f32[264,128]{1,0:T(8,128)S(1)}, f32[264,128]{1,0:T(8,128)S(1)}, u32[]{:S(2)}, u32[]{:S(2)}) %collective-permute-start) | collective-permute-done | bytes 135200 | tf_op jit(solution)/shard_map/ppermute | solution.py:720
  12.5 0.7 %collective-permute-start.3 = (f32[264,128]{1,0:T(8,128)S(1)}, f32[264,128]{1,0:T(8,128)S(1)}, u32[]{:S(2)}, u32[]{:S(2)}) collective-permute-start(f32[264,128]{1,0:T(8,128)S(1)} %collective-permute-done.refs_1_.refs_0_), channel_id=1, source_target_pairs={{0,8},{4,12},{8,0},{12,4},{16,24},{20,28},{24,16},{28,20},{1,9},{5... | collective-permute-start | bytes 405512 | tf_op jit(solution)/shard_map/ppermute | solution.py:720
  13.2 1.5 %collective-permute-start.2 = (f32[264,128]{1,0:T(8,128)S(1)}, f32[264,128]{1,0:T(8,128)S(1)}, u32[]{:S(2)}, u32[]{:S(2)}) collective-permute-start(f32[264,128]{1,0:T(8,128)S(1)} %collective-permute-done.refs_1_.refs_0_), channel_id=1, source_target_pairs={{0,4},{4,0},{8,12},{12,8},{16,20},{20,16},{24,28},{28,24},{1,5},{5... | collective-permute-start | bytes 405512 | tf_op jit(solution)/shard_map/ppermute | solution.py:720
  14.6 0.0 collective-permute-done.6.refs_4_.refs_3_
  14.6 1.6 %collective-permute-start.1 = (f32[264,128]{1,0:T(8,128)S(1)}, f32[264,128]{1,0:T(8,128)S(1)}, u32[]{:S(2)}, u32[]{:S(2)}) collective-permute-start(f32[264,128]{1,0:T(8,128)S(1)} %collective-permute-done.refs_1_.refs_0_), channel_id=1, source_target_pairs={{0,12},{4,8},{8,4},{12,0},{16,28},{20,24},{24,20},{28,16},{1,13},{... | collective-permute-start | bytes 405512 | tf_op jit(solution)/shard_map/ppermute | solution.py:720
  16.2 0.7 %pad_add_fusion.scalar_ref = s32[18]{0:T(128)S(1)} fusion(s32[8]{0:T(128)} %param.7, s32[8]{0:T(128)} %param.6, s32[1]{0:T(128)} %bitcast.1, s32[1]{0:T(128)} %bitcast), kind=kLoop, calls=%fused_computation | loop fusion | flops 54 | bytes 144 | tf_op jit(solution)/shard_map/concatenate | solution.py:702
  17.0 0.0 collective-permute-done.5.refs_3_.refs_2_
  17.0 0.5 collective-permute-done.4.refs_2_.refs_1_
  17.4 0.6 early_edges.1
  18.0 0.1 collective-permute-start.7
  18.1 0.7 %collective-permute-start.8 = (f32[40,8,128]{2,1,0:T(8,128)S(1)}, f32[40,8,128]{2,1,0:T(8,128)S(1)}, u32[]{:S(2)}, u32[]{:S(2)}) collective-permute-start(f32[40,8,128]{2,1,0:T(8,128)S(1)} %get-tuple-element.18), channel_id=1, source_target_pairs={{1,2},{2,1},{5,6},{6,5},{9,10},{10,9},{13,14},{14,13},{17,18},{18,... | collective-permute-start | bytes 491528 | tf_op jit(solution)/shard_map/ppermute | solution.py:730
  18.8 0.6 collective-permute-done.3.refs_7_.refs_3_
  19.3 1.4 %collective-permute-done.2.refs_6_.refs_2_ = f32[264,128]{1,0:T(8,128)S(1)} collective-permute-done((f32[264,128]{1,0:T(8,128)S(1)}, f32[264,128]{1,0:T(8,128)S(1)}, u32[]{:S(2)}, u32[]{:S(2)}) %collective-permute-start.2) | collective-permute-done | bytes 135200 | tf_op jit(solution)/shard_map/ppermute | solution.py:720
  20.8 1.6 %collective-permute-done.1.refs_5_.refs_1_ = f32[264,128]{1,0:T(8,128)S(1)} collective-permute-done((f32[264,128]{1,0:T(8,128)S(1)}, f32[264,128]{1,0:T(8,128)S(1)}, u32[]{:S(2)}, u32[]{:S(2)}) %collective-permute-start.1) | collective-permute-done | bytes 135200 | tf_op jit(solution)/shard_map/ppermute | solution.py:720
  22.3 0.7 %late_edges.1 = (f32[25,8,128]{2,1,0:T(8,128)S(1)}, f32[25,8,128]{2,1,0:T(8,128)S(1)}, f32[32,128]{1,0:T(8,128)S(1)}) custom-call(s32[18]{0:T(128)S(1)} %pad_add_fusion.scalar_ref, f32[264,128]{1,0:T(8,128)S(1)} %pack.1.refs_0_, f32[264,128]{1,0:T(8,128)S(1)} %collective-permute-done.refs_1_.refs_0_, f32[264,128]{1,0:T(8,128)S(1)} %collective-permute-done.4.refs_2_.refs_1_, ...), custom_call_target="tpu_custom_call" | custom-call | tf_op jit(solution)/shard_map/late_edges/pallas_call | solution.py:683
  23.1 0.1 collective-permute-start.9
  23.2 0.7 %collective-permute-start.10 = (f32[25,8,128]{2,1,0:T(8,128)S(1)}, f32[25,8,128]{2,1,0:T(8,128)S(1)}, u32[]{:S(2)}, u32[]{:S(2)}) collective-permute-start(f32[25,8,128]{2,1,0:T(8,128)S(1)} %get-tuple-element.20), channel_id=1, source_target_pairs={{1,2},{2,1},{5,6},{6,5},{9,10},{10,9},{13,14},{14,13},{17,18},{18,... | collective-permute-start | bytes 307208 | tf_op jit(solution)/shard_map/ppermute | solution.py:730
  23.8 0.0 collective-permute-done.7.refs_4_
  23.8 0.0 collective-permute-done.8.refs_5_
  23.8 1.6 %near_half.1 = (f32[18,4,24,128]{3,2,1,0:T(8,128)S(1)}, f32[16,4,16,128]{3,2,1,0:T(8,128)S(1)}, f32[16,4,24,128]{3,2,1,0:T(8,128)S(1)}) custom-call(s32[18]{0:T(128)S(1)} %pad_add_fusion.scalar_ref, f32[264,128]{1,0:T(8,128)S(1)} %pack.1.refs_0_, f32[264,128]{1,0:T(8,128)S(1)} %collective-permute-done.4.refs_2_.refs_1_, ...), custom_call_target="tpu_custom_call" | custom-call | tf_op jit(solution)/shard_map/near_half/pallas_call | solution.py:683
  25.5 0.0 collective-permute-done.9.refs_6_
  25.5 0.0 collective-permute-done.10.refs_7_
  25.5 3.7 %far_half.1 = (f32[4,32,256]{2,1,0:T(8,128)}, f32[36,4,24,128]{3,2,1,0:T(8,128)S(1)}, f32[36,4,24,128]{3,2,1,0:T(8,128)S(1)}, f32[256,128]{1,0:T(8,128)S(1)}) custom-call(s32[18]{0:T(128)S(1)} %pad_add_fusion.scalar_ref, f32[264,128]{1,0:T(8,128)S(1)} %collective-permute-done.refs_1_.refs_0_, f32[264,128]{1,0:T(8,128)S(1)} %collective-permute-done.1.refs_5_.refs_1_, ...), custom_call_target="tpu_custom_call" | custom-call | tf_op jit(solution)/shard_map/far_half/pallas_call | solution.py:683
  29.2 11.0 %all-gather = f32[1024,128]{1,0:T(8,128)S(1)} all-gather(f32[256,128]{1,0:T(8,128)S(1)} %get-tuple-element.25), channel_id=2, replica_groups=mesh['slab'=8,'pencil'=4] {'pencil'}, dimensions={0}, use_global_device_ids=true | all-gather | bytes 655360 | tf_op jit(solution)/shard_map/all_gather | solution.py:791
  40.2 7.0 %middle.1 = (f32[4,4,24,128]{3,2,1,0:T(8,128)S(1)}, f32[6,4,24,128]{3,2,1,0:T(8,128)S(1)}, f32[256,128]{1,0:T(8,128)S(1)}) custom-call(s32[18]{0:T(128)S(1)} %pad_add_fusion.scalar_ref, f32[4,256,128]{2,1,0:T(8,128)S(1)} %bitcast.4, f32[36,4,24,128]{3,2,1,0:T(8,128)S(1)} %get-tuple-element.26.q_ref, f32[36,4,24,128]{3,2,1,0:T(8,128)S(1)} %get-tuple-element.27.swept_ref), custom_call_target="tpu_custom_call" | custom-call | tf_op jit(solution)/shard_map/middle/pallas_call | solution.py:683
  47.3 7.3 %all-gather.1 = f32[1024,128]{1,0:T(8,128)S(1)} all-gather(f32[256,128]{1,0:T(8,128)S(1)} %get-tuple-element.28), channel_id=3, replica_groups=mesh['slab'=8,'pencil'=4] {'pencil'}, dimensions={0}, use_global_device_ids=true | all-gather | bytes 655360 | tf_op jit(solution)/shard_map/all_gather | solution.py:791
  54.6 3.9 %last.1 = f32[4,32,256]{2,1,0:T(8,128)} custom-call(s32[18]{0:T(128)S(1)} %pad_add_fusion.scalar_ref, f32[4,256,128]{2,1,0:T(8,128)S(1)} %bitcast.5, f32[4,4,24,128]{3,2,1,0:T(8,128)S(1)} %get-tuple-element.29.qwin_ref, f32[6,4,24,128]{3,2,1,0:T(8,128)S(1)} %get-tuple-element.30.win_ref), custom_call_target="tpu_custom_call" | custom-call | tf_op jit(solution)/shard_map/last/pallas_call | solution.py:683
Async XLA Ops:
  1.8 10.7 %collective-permute-start = (f32[264,128]{1,0:T(8,128)S(1)}, f32[264,128]{1,0:T(8,128)S(1)}, u32[]{:S(2)}, u32[]{:S(2)}) collective-permute-start(f32[264,128]{1,0:T(8,128)S(1)} %pack.1.refs_0_), channel_id=1, source_target_pairs={{0,16},{4,20},{8,24},{12,28},{16,0},{20,4},{24,8},{28,12},{1,17},{... | collective-permute-start | bytes 405512 | tf_op jit(solution)/shard_map/ppermute | solution.py:720
  5.9 8.7 %collective-permute-start.6 = (f32[264,128]{1,0:T(8,128)S(1)}, f32[264,128]{1,0:T(8,128)S(1)}, u32[]{:S(2)}, u32[]{:S(2)}) collective-permute-start(f32[264,128]{1,0:T(8,128)S(1)} %pack.1.refs_0_), channel_id=1, source_target_pairs={{0,8},{4,12},{8,0},{12,4},{16,24},{20,28},{24,16},{28,20},{1,9},{5... | collective-permute-start | bytes 405512 | tf_op jit(solution)/shard_map/ppermute | solution.py:720
  7.5 9.5 %collective-permute-start.5 = (f32[264,128]{1,0:T(8,128)S(1)}, f32[264,128]{1,0:T(8,128)S(1)}, u32[]{:S(2)}, u32[]{:S(2)}) collective-permute-start(f32[264,128]{1,0:T(8,128)S(1)} %pack.1.refs_0_), channel_id=1, source_target_pairs={{0,4},{4,0},{8,12},{12,8},{16,20},{20,16},{24,28},{28,24},{1,5},{5... | collective-permute-start | bytes 405512 | tf_op jit(solution)/shard_map/ppermute | solution.py:720
  9.0 8.5 %collective-permute-start.4 = (f32[264,128]{1,0:T(8,128)S(1)}, f32[264,128]{1,0:T(8,128)S(1)}, u32[]{:S(2)}, u32[]{:S(2)}) collective-permute-start(f32[264,128]{1,0:T(8,128)S(1)} %pack.1.refs_0_), channel_id=1, source_target_pairs={{0,12},{4,8},{8,4},{12,0},{16,28},{20,24},{24,20},{28,16},{1,13},{... | collective-permute-start | bytes 405512 | tf_op jit(solution)/shard_map/ppermute | solution.py:720
  12.5 6.9 %collective-permute-start.3 = (f32[264,128]{1,0:T(8,128)S(1)}, f32[264,128]{1,0:T(8,128)S(1)}, u32[]{:S(2)}, u32[]{:S(2)}) collective-permute-start(f32[264,128]{1,0:T(8,128)S(1)} %collective-permute-done.refs_1_.refs_0_), channel_id=1, source_target_pairs={{0,8},{4,12},{8,0},{12,4},{16,24},{20,28},{24,16},{28,20},{1,9},{5... | collective-permute-start | bytes 405512 | tf_op jit(solution)/shard_map/ppermute | solution.py:720
  13.2 7.6 %collective-permute-start.2 = (f32[264,128]{1,0:T(8,128)S(1)}, f32[264,128]{1,0:T(8,128)S(1)}, u32[]{:S(2)}, u32[]{:S(2)}) collective-permute-start(f32[264,128]{1,0:T(8,128)S(1)} %collective-permute-done.refs_1_.refs_0_), channel_id=1, source_target_pairs={{0,4},{4,0},{8,12},{12,8},{16,20},{20,16},{24,28},{28,24},{1,5},{5... | collective-permute-start | bytes 405512 | tf_op jit(solution)/shard_map/ppermute | solution.py:720
  14.6 7.7 %collective-permute-start.1 = (f32[264,128]{1,0:T(8,128)S(1)}, f32[264,128]{1,0:T(8,128)S(1)}, u32[]{:S(2)}, u32[]{:S(2)}) collective-permute-start(f32[264,128]{1,0:T(8,128)S(1)} %collective-permute-done.refs_1_.refs_0_), channel_id=1, source_target_pairs={{0,12},{4,8},{8,4},{12,0},{16,28},{20,24},{24,20},{28,16},{1,13},{... | collective-permute-start | bytes 405512 | tf_op jit(solution)/shard_map/ppermute | solution.py:720
  18.0 5.8 %collective-permute-start.7 = (f32[40,8,128]{2,1,0:T(8,128)S(1)}, f32[40,8,128]{2,1,0:T(8,128)S(1)}, u32[]{:S(2)}, u32[]{:S(2)}) collective-permute-start(f32[40,8,128]{2,1,0:T(8,128)S(1)} %get-tuple-element.17), channel_id=1, source_target_pairs={{0,1},{2,3},{1,0},{3,2},{4,5},{6,7},{5,4},{7,6},{8,9},{10,11},{9,8... | collective-permute-start | bytes 491528 | tf_op jit(solution)/shard_map/ppermute | solution.py:729
  18.1 5.7 %collective-permute-start.8 = (f32[40,8,128]{2,1,0:T(8,128)S(1)}, f32[40,8,128]{2,1,0:T(8,128)S(1)}, u32[]{:S(2)}, u32[]{:S(2)}) collective-permute-start(f32[40,8,128]{2,1,0:T(8,128)S(1)} %get-tuple-element.18), channel_id=1, source_target_pairs={{1,2},{2,1},{5,6},{6,5},{9,10},{10,9},{13,14},{14,13},{17,18},{18,... | collective-permute-start | bytes 491528 | tf_op jit(solution)/shard_map/ppermute | solution.py:730
  23.1 2.4 %collective-permute-start.9 = (f32[25,8,128]{2,1,0:T(8,128)S(1)}, f32[25,8,128]{2,1,0:T(8,128)S(1)}, u32[]{:S(2)}, u32[]{:S(2)}) collective-permute-start(f32[25,8,128]{2,1,0:T(8,128)S(1)} %get-tuple-element.19), channel_id=1, source_target_pairs={{0,1},{2,3},{1,0},{3,2},{4,5},{6,7},{5,4},{7,6},{8,9},{10,11},{9,8... | collective-permute-start | bytes 307208 | tf_op jit(solution)/shard_map/ppermute | solution.py:729
  23.2 2.3 %collective-permute-start.10 = (f32[25,8,128]{2,1,0:T(8,128)S(1)}, f32[25,8,128]{2,1,0:T(8,128)S(1)}, u32[]{:S(2)}, u32[]{:S(2)}) collective-permute-start(f32[25,8,128]{2,1,0:T(8,128)S(1)} %get-tuple-element.20), channel_id=1, source_target_pairs={{1,2},{2,1},{5,6},{6,5},{9,10},{10,9},{13,14},{14,13},{17,18},{18,... | collective-permute-start | bytes 307208 | tf_op jit(solution)/shard_map/ppermute | solution.py:730

commit v6 on v5

--- a/solution.py
+++ b/solution.py
@@ -163,12 +163,11 @@
     return flat_sweep(u, q, rows, yd, xd)
 
 
-def solve_level_one(gathered_ref, v_ref, q_ref, a_ref, b_ref, tmp_ref, shape, near=None):
+def solve_level_one(piece_refs, pencil, v_ref, q_ref, a_ref, b_ref, tmp_ref, shape, near=None):
     zs, ys, xs = shape
-    pencils = gathered_ref.shape[0]
     rows = ys // 2
     half = zs // 2
-    piece = rows // pencils
+    piece = rows // len(piece_refs)
     row = row_iota((rows, LANES))
     blank = jnp.zeros((rows, LANES), jnp.float32)
     for ref in (q_ref, a_ref, b_ref):
@@ -187,9 +186,10 @@
                 v_ref[z, pl.ds(HALO + c * rows, rows), :] = blank
     for z in range(zs):
         for c in range(2):
-            for p in range(pencils):
+            for k, ref in enumerate(piece_refs):
                 spot = pl.ds(2 * piece * z + c, piece, stride=2)
-                q_ref[z + 2, c, pl.ds(p * piece, piece), :] = gathered_ref[p, spot, :]
+                to = pl.ds(pl.multiple_of((pencil ^ k) * piece, piece), piece)
+                q_ref[z + 2, c, to, :] = ref[spot, :]
 
     def y_beyond(other, c):
         if c:
@@ -276,12 +276,13 @@
     ]
     for copy in copies:
         copy.start()
+    matrix = splitting_matrix()
     for copy in copies:
         copy.wait()
     depth, width, columns = potential_ref.shape
     slots = store_ref.shape[0]
     part = width // 2
-    split = mm(potential_ref[...].reshape(depth * width, columns), splitting_matrix())
+    split = mm(potential_ref[...].reshape(depth * width, columns), matrix)
     even_ref[...] = split[:, :LANES]
     odd_ref[...] = split[:, LANES:]
     for z in range(depth):
@@ -469,8 +470,8 @@
     early_refs = refs[len(far) : len(far) + 2]
     late_refs = refs[len(far) + 2 : len(far) + 4]
     faces_ref, pn_ref, sn_ref, qn_ref = refs[len(far) + 4 : len(far) + 8]
-    source_hbm, q_ref, swept_ref, coarse_ref = refs[len(far) + 8 : len(far) + 12]
-    p_ref, f_ref, s_ref, u_ref, left_ref, right_ref, source_ref, sem = refs[len(far) + 12 :]
+    s_ref, q_ref, u_ref, coarse_ref = refs[len(far) + 8 : len(far) + 12]
+    p_ref, f_ref = refs[len(far) + 12 :]
     slab = scalar_ref[0]
     pencil = scalar_ref[1]
     part = width // 2
@@ -484,7 +485,7 @@
     mask = halo_mask(pencil, pencils)
     blank = jnp.zeros(p_ref.shape[1:], jnp.float32)
     for ref in (q_ref, u_ref):
-        for z in (1, planes + 2):
+        for z in (0, 1, planes + 2, planes + 3):
             ref[z] = blank
     p_ref[jnp.where(lower, half + 1, 0)] = blank
     p_ref[jnp.where(lower, 0, half + 1)] = pn_ref[jnp.where(lower, half, 1)]
@@ -537,10 +538,6 @@
         is_seam = own + z == seam - 1
         for c in range(4):
             s_ref[z, c] = jnp.where(is_seam, source[c][:part], sn_ref[own + z, c])
-    join_planes(lambda z, c: s_ref[z, c], source_ref, left_ref, right_ref, depth, width)
-    copy_out = pltpu.make_async_copy(source_ref, source_hbm, sem)
-    copy_out.start()
-
     def second_sweep(z, carry):
         here = parts(q_ref, z + 2)
         for c in range(4):
@@ -549,24 +546,51 @@
         return carry
 
     lax.fori_loop(0, planes, second_sweep, 0, unroll=UNROLL)
-    restrict_window(u_ref, q_ref, coarse_ref, swept_ref, mask, planes, part)
-    copy_out.wait()
-
-
-def restrict_window(u_ref, q_ref, coarse_ref, swept_ref, mask, planes, part):
+    restrict_window(u_ref, q_ref, coarse_ref, planes, part)
+
+
+def restrict_window(u_ref, q_ref, coarse_ref, planes, part):
     def restrict(z, carry):
         total = None
         for at in (2 * z + 2, 2 * z + 3):
             here = parts(u_ref, at)
             for c in range(4):
                 new = swept(u_ref[at - 1, c], here, u_ref[at + 1, c], q_ref[at, c], c)
-                put(swept_ref, at, c, new, mask)
                 change = new[:part] - here[c][:part]
                 total = change if total is None else total + change
         coarse_ref[pl.ds(pl.multiple_of(z * part, part), part), :] = 0.5 * total
         return carry
 
     lax.fori_loop(0, planes // 2, restrict, 0, unroll=PAIRS)
+
+
+def between_kernel(scalar_ref, q_ref, u_ref, s_ref, source_hbm, swept_ref, *refs, pencils):
+    left_ref, right_ref, source_ref, sem = refs
+    depth, width, _ = source_ref.shape
+    planes = q_ref.shape[0] - 4
+    mask = halo_mask(scalar_ref[1], pencils)
+    join_planes(lambda z, c: s_ref[z, c], source_ref, left_ref, right_ref, depth, width)
+    copy_out = pltpu.make_async_copy(source_ref, source_hbm, sem)
+    copy_out.start()
+
+    def sweep(z, carry):
+        here = parts(u_ref, z + 2)
+        for c in range(4):
+            new = swept(u_ref[z + 1, c], here, u_ref[z + 3, c], q_ref[z + 2, c], c)
+            put(swept_ref, z + 2, c, new, mask)
+        return carry
+
+    lax.fori_loop(0, planes, sweep, 0, unroll=UNROLL)
+    copy_out.wait()
+
+
+def window_kernel(scalar_ref, qwin_ref, uwin_ref, win_ref, *, pencils):
+    mask = halo_mask(scalar_ref[1], pencils)
+    for z in range(win_ref.shape[0]):
+        here = parts(uwin_ref, z + 1)
+        for c in range(4):
+            new = swept(uwin_ref[z, c], here, uwin_ref[z + 2, c], qwin_ref[z, c], c)
+            put(win_ref, z, c, new, mask)
 
 
 def coarse_window(v_ref, z, pencil, part):
@@ -579,7 +603,8 @@
 
 
 def middle_kernel(
-    scalar_ref, gathered_ref, q_ref, swept_ref, qwin_ref, win_ref, coarse_ref,
+    scalar_ref, c0_ref, c1_ref, c2_ref, c3_ref, q_ref, swept_ref,
+    qwin_ref, uwin_ref, coarse_ref,
     v_ref, q1_ref, a1_ref, b1_ref, tmp_ref, a_ref, b_ref, *, depth, width, pencils, shape
 ):
     slab = scalar_ref[0]
@@ -587,10 +612,11 @@
     planes = a_ref.shape[0] - 4
     part = width // 2
     mask = halo_mask(pencil, pencils)
-    solve_level_one(gathered_ref, v_ref, q1_ref, a1_ref, b1_ref, tmp_ref, shape)
+    piece_refs = (c0_ref, c1_ref, c2_ref, c3_ref)
+    solve_level_one(piece_refs, pencil, v_ref, q1_ref, a1_ref, b1_ref, tmp_ref, shape)
     blank = jnp.zeros(a_ref.shape[1:], jnp.float32)
     for ref in (a_ref, b_ref):
-        for z in (1, planes + 2):
+        for z in (0, 1, planes + 2, planes + 3):
             ref[z] = blank
 
     def third_sweep(z, carry):
@@ -616,15 +642,15 @@
     sweep(a_ref, b_ref)
     sweep(b_ref, a_ref)
     sweep(a_ref, b_ref)
-    restrict_window(b_ref, q_ref, coarse_ref, a_ref, mask, planes, part)
-    for z in range(depth):
-        qwin_ref[z] = q_ref[slab * depth + z + 2]
+    restrict_window(b_ref, q_ref, coarse_ref, planes, part)
     for z in range(depth + 2):
-        win_ref[z] = a_ref[slab * depth + z + 1]
+        qwin_ref[z] = q_ref[slab * depth + z + 1]
+    for z in range(depth + 4):
+        uwin_ref[z] = b_ref[slab * depth + z]
 
 
 def last_kernel(
-    scalar_ref, gathered_ref, qwin_ref, win_ref, out_hbm,
+    scalar_ref, c0_ref, c1_ref, c2_ref, c3_ref, qwin_ref, win_ref, out_hbm,
     v_ref, q1_ref, a1_ref, b1_ref, tmp_ref, a_ref, left_ref, right_ref, out_ref, sems,
     *, depth, width, pencils, shape
 ):
@@ -633,7 +659,8 @@
     planes = shape[0] * 2
     part = width // 2
     mask = halo_mask(pencil, pencils)
-    solve_level_one(gathered_ref, v_ref, q1_ref, a1_ref, b1_ref, tmp_ref, shape, slab)
+    piece_refs = (c0_ref, c1_ref, c2_ref, c3_ref)
+    solve_level_one(piece_refs, pencil, v_ref, q1_ref, a1_ref, b1_ref, tmp_ref, shape, slab)
     blank = jnp.zeros((part + 8, LANES), jnp.float32)
     v = [coarse_window(v_ref, slab * (depth // 2) + k, pencil, part) for k in range(4)]
     v = [blank] + v + [blank]
@@ -650,7 +677,7 @@
     for z in range(depth):
         here = parts(a_ref, z + 1)
         for c in range(4):
-            new = swept(a_ref[z, c], here, a_ref[z + 2, c], qwin_ref[z, c], c)
+            new = swept(a_ref[z, c], here, a_ref[z + 2, c], qwin_ref[z + 1, c], c)
             ref = right_ref if c & 1 else left_ref
             ref[z, pl.ds(c >> 1, part, stride=2), :] = new[:part]
         out_ref[z] = mm(jnp.concatenate([left_ref[z], right_ref[z]], axis=1), matrix)
@@ -760,24 +787,39 @@
         [b for b, offset in zip(blocks, OFFSETS) if offset < 4] + [*early, faces],
         (arr(half + 2, 4, rows, LANES), arr(half, 4, part, LANES), arr(half, 4, rows, LANES)),
     )
-    source, q, swept_once, coarse = call(
+    own_source, q, u, coarse = call(
         partial(far_half_kernel, depth=depth, width=width, pencils=pencils),
         "far_half",
         [scalars],
         [b for b, offset in zip(blocks, OFFSETS) if offset >= 4] + [*early, *late, faces, *near],
-        (arr(depth, width, columns), arr(*field), arr(*field), coarse_part),
+        (arr(depth, 4, part, LANES), arr(*field), arr(*field), coarse_part),
+        [buf(half + 2, 4, rows, LANES), buf(2, rows, LANES)],
+    )
+
+    def pair(x, bits):
+        return lax.ppermute(x, "pencil", [(i, i ^ bits) for i in range(pencils)])
+
+    def gather(x, meanwhile):
+        beside, across = pair(x, 1), pair(x, 2)
+        made = meanwhile()
+        across, made = lax.optimization_barrier((across, made))
+        return [x, beside, across, pair(across, 1)], made
+
+    between = lambda: call(
+        partial(between_kernel, pencils=pencils),
+        "between",
+        [scalars],
+        [q, u, own_source],
+        (arr(depth, width, columns), arr(*field)),
         [
-            buf(half + 2, 4, rows, LANES),
-            buf(2, rows, LANES),
-            buf(depth, 4, part, LANES),
-            buf(*field),
             buf(depth * width, LANES),
             buf(depth * width, LANES),
             buf(depth, width, columns),
             pltpu.SemaphoreType.DMA,
         ],
-        out_space=[pl.ANY] + [pltpu.VMEM] * 3,
-    )
+        out_space=[pl.ANY, pltpu.VMEM],
+    )
+    pieces, (source, swept_once) = gather(coarse, between)
     level = (shape[0] + 4, 2, shape[1] // 2, LANES)
     level_scratch = [
         buf(shape[0] + 2, shape[1] + 2 * HALO, LANES),
@@ -786,24 +828,28 @@
         buf(*level),
         buf((shape[0] // 2 + 4) * shape[1] // 2, LANES),
     ]
-
-    def gather(x):
-        return lax.all_gather(x, "pencil", axis=0, tiled=False)
-
     sizes = dict(depth=depth, width=width, pencils=pencils, shape=shape)
-    qwin, win, coarse = call(
+    qwin, uwin, coarse = call(
         partial(middle_kernel, **sizes),
         "middle",
         [scalars],
-        [gather(coarse), q, swept_once],
-        (arr(depth, 4, rows, LANES), arr(depth + 2, 4, rows, LANES), coarse_part),
+        [*pieces, q, swept_once],
+        (arr(depth + 2, 4, rows, LANES), arr(depth + 4, 4, rows, LANES), coarse_part),
         level_scratch + [buf(*field), buf(*field)],
     )
+    window = lambda: call(
+        partial(window_kernel, pencils=pencils),
+        "window",
+        [scalars],
+        [qwin, uwin],
+        arr(depth + 2, 4, rows, LANES),
+    )
+    pieces, win = gather(coarse, window)
     (solved,) = call(
         partial(last_kernel, **sizes),
         "last",
         [scalars],
-        [gather(coarse), qwin, win],
+        [*pieces, qwin, win],
         (arr(depth, width, columns),),
         level_scratch
         + [
@@ -825,13 +871,12 @@
     planes = slabs * depth
     return (
         slabs == 8
-        and pencils % 2 == 0
         and depth == 4
         and columns == 2 * LANES
         and width == 32
         and parent_store.shape[0] * width == LANES
         and 2 * planes < LANES
-        and pencils in (2, 4, 8)
+        and pencils == 4
     )
 
 

time: 58.7 us -> 57.7 us (0.983)
  blocking collectives: 18.3 us -> 0 us
  waiting for transfers between devices: 7.14 us -> 16.6 us
  starting transfers between devices: 12.8 us -> 18.8 us
  Pallas kernels: 18.7 us -> 20.6 us
    all_gather x2 -> x0, blocking collectives: 18.3 us -> none  [gather(): return lax.all_gather(x, 'pencil', axis=0, tiled=False)]
    ppermute x0 -> x6, waiting for transfers between devices: none -> 9.42 us  [pair(): return lax.ppermute(x, 'pencil', [(i, i ^ bits) for i in range(pencils)])]
    ppermute x0 -> x6, starting transfers between devices: none -> 6.02 us  [pair(): return lax.ppermute(x, 'pencil', [(i, i ^ bits) for i in range(pencils)])]
    pallas_call x7 -> x9, Pallas kernels: 18.7 us -> 20.6 us  [call(): pl.pallas_call(kernel, out_shape=outs, in_specs=[smem()] * len(scalars) +...]
  transfers between devices with their start and end apart: 11 -> 17, of which waited for: 5 -> 9; matrix products, arithmetic and copies ran while one was open for 1% -> 1% of each run, Pallas kernels for 5% -> 9%
where the time goes in v6:
time: 57.7 us; the launch traced here: 57.5 us
  Pallas kernels  20.6 us (36%)
  starting transfers between devices  18.8 us (33%)
  waiting for transfers between devices  16.6 us (29%)
  between operations  0.77 us (1%)
  other arithmetic  0.75 us (1%)
    pallas_call x9, Pallas kernels, call(): pl.pallas_call(kernel, out_shape=outs, in_specs=[smem()] * len(scalars) +...  20.6 us
    ppermute x7, starting transfers between devices, swap(): return lax.ppermute(x, 'slab', [(i, i ^ bits) for i in range(slabs)])  11.3 us
    ppermute x6, waiting for transfers between devices, pair(): return lax.ppermute(x, 'pencil', [(i, i ^ bits) for i in range(pencils)])  9.42 us
    ppermute x7, waiting for transfers between devices, swap(): return lax.ppermute(x, 'slab', [(i, i ^ bits) for i in range(slabs)])  7.13 us
    ppermute x6, starting transfers between devices, pair(): return lax.ppermute(x, 'pencil', [(i, i ^ bits) for i in range(pencils)])  6.02 us
    ppermute x2, starting transfers between devices, beside(): lax.ppermute(odd, 'pencil', high_pairs + [(j, i) for i, j in high_pairs])  1.34 us
  transfers between devices with their start and end apart: 17, of which 9 were waited for; matrix products, arithmetic and copies ran while one was open for 1% of the time, Pallas kernels for 9%

profile of v6, /device:TPU:0, one launch (start us, length us, event | category | flops | bytes accessed | tf_op | source)
XLA Modules:
  0.0 57.5 jit_solution(18145161784700866720)
XLA Ops:
  0.6 1.2 %pack.1.refs_0_ = f32[264,128]{1,0:T(8,128)S(1)} custom-call(f32[4,32,256]{2,1,0:T(8,128)} %potential_hbm.1, f32[4,2,4,32]{3,2,1,0:T(4,128)} %store_hbm.1), custom_call_target="tpu_custom_call" | custom-call | tf_op jit(solution)/shard_map/pack/pallas_call | solution.py:710
  1.8 4.1 %collective-permute-start = (f32[264,128]{1,0:T(8,128)S(1)}, f32[264,128]{1,0:T(8,128)S(1)}, u32[]{:S(2)}, u32[]{:S(2)}) collective-permute-start(f32[264,128]{1,0:T(8,128)S(1)} %pack.1.refs_0_), channel_id=1, source_target_pairs={{0,16},{4,20},{8,24},{12,28},{16,0},{20,4},{24,8},{28,12},{1,17},{... | collective-permute-start | bytes 405512 | tf_op jit(solution)/shard_map/ppermute | solution.py:747
  5.9 1.6 %collective-permute-start.6 = (f32[264,128]{1,0:T(8,128)S(1)}, f32[264,128]{1,0:T(8,128)S(1)}, u32[]{:S(2)}, u32[]{:S(2)}) collective-permute-start(f32[264,128]{1,0:T(8,128)S(1)} %pack.1.refs_0_), channel_id=1, source_target_pairs={{0,8},{4,12},{8,0},{12,4},{16,24},{20,28},{24,16},{28,20},{1,9},{5... | collective-permute-start | bytes 405512 | tf_op jit(solution)/shard_map/ppermute | solution.py:747
  7.5 1.5 %collective-permute-start.5 = (f32[264,128]{1,0:T(8,128)S(1)}, f32[264,128]{1,0:T(8,128)S(1)}, u32[]{:S(2)}, u32[]{:S(2)}) collective-permute-start(f32[264,128]{1,0:T(8,128)S(1)} %pack.1.refs_0_), channel_id=1, source_target_pairs={{0,4},{4,0},{8,12},{12,8},{16,20},{20,16},{24,28},{28,24},{1,5},{5... | collective-permute-start | bytes 405512 | tf_op jit(solution)/shard_map/ppermute | solution.py:747
  9.0 0.4 collective-permute-start.4
  9.4 3.1 %collective-permute-done.refs_1_.refs_0_ = f32[264,128]{1,0:T(8,128)S(1)} collective-permute-done((f32[264,128]{1,0:T(8,128)S(1)}, f32[264,128]{1,0:T(8,128)S(1)}, u32[]{:S(2)}, u32[]{:S(2)}) %collective-permute-start) | collective-permute-done | bytes 135200 | tf_op jit(solution)/shard_map/ppermute | solution.py:747
  12.5 0.7 %collective-permute-start.3 = (f32[264,128]{1,0:T(8,128)S(1)}, f32[264,128]{1,0:T(8,128)S(1)}, u32[]{:S(2)}, u32[]{:S(2)}) collective-permute-start(f32[264,128]{1,0:T(8,128)S(1)} %collective-permute-done.refs_1_.refs_0_), channel_id=1, source_target_pairs={{0,8},{4,12},{8,0},{12,4},{16,24},{20,28},{24,16},{28,20},{1,9},{5... | collective-permute-start | bytes 405512 | tf_op jit(solution)/shard_map/ppermute | solution.py:747
  13.1 1.5 %collective-permute-start.2 = (f32[264,128]{1,0:T(8,128)S(1)}, f32[264,128]{1,0:T(8,128)S(1)}, u32[]{:S(2)}, u32[]{:S(2)}) collective-permute-start(f32[264,128]{1,0:T(8,128)S(1)} %collective-permute-done.refs_1_.refs_0_), channel_id=1, source_target_pairs={{0,4},{4,0},{8,12},{12,8},{16,20},{20,16},{24,28},{28,24},{1,5},{5... | collective-permute-start | bytes 405512 | tf_op jit(solution)/shard_map/ppermute | solution.py:747
  14.6 1.6 %collective-permute-start.1 = (f32[264,128]{1,0:T(8,128)S(1)}, f32[264,128]{1,0:T(8,128)S(1)}, u32[]{:S(2)}, u32[]{:S(2)}) collective-permute-start(f32[264,128]{1,0:T(8,128)S(1)} %collective-permute-done.refs_1_.refs_0_), channel_id=1, source_target_pairs={{0,12},{4,8},{8,4},{12,0},{16,28},{20,24},{24,20},{28,16},{1,13},{... | collective-permute-start | bytes 405512 | tf_op jit(solution)/shard_map/ppermute | solution.py:747
  16.2 0.7 %pad_add_fusion.scalar_ref = s32[18]{0:T(128)S(1)} fusion(s32[8]{0:T(128)} %param.7, s32[8]{0:T(128)} %param.6, s32[1]{0:T(128)} %bitcast.1, s32[1]{0:T(128)} %bitcast), kind=kLoop, calls=%fused_computation | loop fusion | flops 54 | bytes 144 | tf_op jit(solution)/shard_map/concatenate | solution.py:729
  17.0 0.5 collective-permute-done.4.refs_2_.refs_1_
  17.4 0.6 %early_edges.1 = (f32[40,8,128]{2,1,0:T(8,128)S(1)}, f32[40,8,128]{2,1,0:T(8,128)S(1)}) custom-call(s32[18]{0:T(128)S(1)} %pad_add_fusion.scalar_ref, f32[264,128]{1,0:T(8,128)S(1)} %pack.1.refs_0_, f32[264,128]{1,0:T(8,128)S(1)} %collective-permute-done.refs_1_.refs_0_, f32[264,128]{1,0:T(8,128)S(1)} %collective-permute-done.4.refs_2_.refs_1_, ...), custom_call_target="tpu_custom_call" | custom-call | tf_op jit(solution)/shard_map/early_edges/pallas_call | solution.py:710
  18.0 0.1 collective-permute-start.7
  18.1 0.7 %collective-permute-start.8 = (f32[40,8,128]{2,1,0:T(8,128)S(1)}, f32[40,8,128]{2,1,0:T(8,128)S(1)}, u32[]{:S(2)}, u32[]{:S(2)}) collective-permute-start(f32[40,8,128]{2,1,0:T(8,128)S(1)} %get-tuple-element.25), channel_id=1, source_target_pairs={{1,2},{2,1},{5,6},{6,5},{9,10},{10,9},{13,14},{14,13},{17,18},{18,... | collective-permute-start | bytes 491528 | tf_op jit(solution)/shard_map/ppermute | solution.py:757
  18.8 0.6 %collective-permute-done.3.refs_7_.refs_3_ = f32[264,128]{1,0:T(8,128)S(1)} collective-permute-done((f32[264,128]{1,0:T(8,128)S(1)}, f32[264,128]{1,0:T(8,128)S(1)}, u32[]{:S(2)}, u32[]{:S(2)}) %collective-permute-start.3) | collective-permute-done | bytes 135200 | tf_op jit(solution)/shard_map/ppermute | solution.py:747
  19.3 1.4 %collective-permute-done.2.refs_6_.refs_2_ = f32[264,128]{1,0:T(8,128)S(1)} collective-permute-done((f32[264,128]{1,0:T(8,128)S(1)}, f32[264,128]{1,0:T(8,128)S(1)}, u32[]{:S(2)}, u32[]{:S(2)}) %collective-permute-start.2) | collective-permute-done | bytes 135200 | tf_op jit(solution)/shard_map/ppermute | solution.py:747
  20.8 1.6 %collective-permute-done.1.refs_5_.refs_1_ = f32[264,128]{1,0:T(8,128)S(1)} collective-permute-done((f32[264,128]{1,0:T(8,128)S(1)}, f32[264,128]{1,0:T(8,128)S(1)}, u32[]{:S(2)}, u32[]{:S(2)}) %collective-permute-start.1) | collective-permute-done | bytes 135200 | tf_op jit(solution)/shard_map/ppermute | solution.py:747
  22.3 0.7 %late_edges.1 = (f32[25,8,128]{2,1,0:T(8,128)S(1)}, f32[25,8,128]{2,1,0:T(8,128)S(1)}, f32[32,128]{1,0:T(8,128)S(1)}) custom-call(s32[18]{0:T(128)S(1)} %pad_add_fusion.scalar_ref, f32[264,128]{1,0:T(8,128)S(1)} %pack.1.refs_0_, f32[264,128]{1,0:T(8,128)S(1)} %collective-permute-done.refs_1_.refs_0_, f32[264,128]{1,0:T(8,128)S(1)} %collective-permute-done.4.refs_2_.refs_1_, ...), custom_call_target="tpu_custom_call" | custom-call | tf_op jit(solution)/shard_map/late_edges/pallas_call | solution.py:710
  23.1 0.7 %collective-permute-start.10 = (f32[25,8,128]{2,1,0:T(8,128)S(1)}, f32[25,8,128]{2,1,0:T(8,128)S(1)}, u32[]{:S(2)}, u32[]{:S(2)}) collective-permute-start(f32[25,8,128]{2,1,0:T(8,128)S(1)} %get-tuple-element.27), channel_id=1, source_target_pairs={{1,2},{2,1},{5,6},{6,5},{9,10},{10,9},{13,14},{14,13},{17,18},{18,... | collective-permute-start | bytes 307208 | tf_op jit(solution)/shard_map/ppermute | solution.py:757
  23.8 1.6 %near_half.1 = (f32[18,4,24,128]{3,2,1,0:T(8,128)S(1)}, f32[16,4,16,128]{3,2,1,0:T(8,128)S(1)}, f32[16,4,24,128]{3,2,1,0:T(8,128)S(1)}) custom-call(s32[18]{0:T(128)S(1)} %pad_add_fusion.scalar_ref, f32[264,128]{1,0:T(8,128)S(1)} %pack.1.refs_0_, f32[264,128]{1,0:T(8,128)S(1)} %collective-permute-done.4.refs_2_.refs_1_, ...), custom_call_target="tpu_custom_call" | custom-call | tf_op jit(solution)/shard_map/near_half/pallas_call | solution.py:710
  25.5 3.2 %far_half.1 = (f32[4,4,16,128]{3,2,1,0:T(8,128)S(1)}, f32[36,4,24,128]{3,2,1,0:T(8,128)S(1)}, f32[36,4,24,128]{3,2,1,0:T(8,128)S(1)}, f32[256,128]{1,0:T(8,128)S(1)}) custom-call(s32[18]{0:T(128)S(1)} %pad_add_fusion.scalar_ref, f32[264,128]{1,0:T(8,128)S(1)} %collective-permute-done.refs_1_.refs_0_, f32[264,128]{1,0:T(8,128)S(1)} %collective-permute-done.1.refs_5_.refs_1_, ...), custom_call_target="tpu_custom_call" | custom-call | tf_op jit(solution)/shard_map/far_half/pallas_call | solution.py:710
  28.8 5.2 %collective-permute-start.12 = (f32[256,128]{1,0:T(8,128)S(1)}, f32[256,128]{1,0:T(8,128)S(1)}, u32[]{:S(2)}, u32[]{:S(2)}) collective-permute-start(f32[256,128]{1,0:T(8,128)S(1)} %get-tuple-element.32.c0_ref), channel_id=1, source_target_pairs={{0,2},{1,3},{2,0},{3,1},{4,6},{5,7},{6,4},{7,5},{8,10},{9,11},{10,... | collective-permute-start | bytes 393224 | tf_op jit(solution)/shard_map/ppermute | solution.py:800
  34.0 1.7 %between.1 = (f32[4,32,256]{2,1,0:T(8,128)}, f32[36,4,24,128]{3,2,1,0:T(8,128)S(1)}) custom-call(s32[18]{0:T(128)S(1)} %pad_add_fusion.scalar_ref, f32[36,4,24,128]{3,2,1,0:T(8,128)S(1)} %get-tuple-element.33.q_ref, f32[36,4,24,128]{3,2,1,0:T(8,128)S(1)} %get-tuple-element.34.u_ref, f32[4,4,16,128]{3,2,1,0:T(8,128)S(1)} %get-tuple-element.35.s_ref), custom_call_target="tpu_custom_call" | custom-call | tf_op jit(solution)/shard_map/between/pallas_call | solution.py:710
  35.6 2.7 %collective-permute-done.12.c2_ref = f32[256,128]{1,0:T(8,128)S(1)} collective-permute-done((f32[256,128]{1,0:T(8,128)S(1)}, f32[256,128]{1,0:T(8,128)S(1)}, u32[]{:S(2)}, u32[]{:S(2)}) %collective-permute-start.12) | collective-permute-done | bytes 131104 | tf_op jit(solution)/shard_map/ppermute | solution.py:800
  38.3 0.1 collective-permute-start.13
  38.4 1.2 %collective-permute-done.13.c3_ref = f32[256,128]{1,0:T(8,128)S(1)} collective-permute-done((f32[256,128]{1,0:T(8,128)S(1)}, f32[256,128]{1,0:T(8,128)S(1)}, u32[]{:S(2)}, u32[]{:S(2)}) %collective-permute-start.13) | collective-permute-done | bytes 131104 | tf_op jit(solution)/shard_map/ppermute | solution.py:800
  39.6 6.9 %middle.1 = (f32[6,4,24,128]{3,2,1,0:T(8,128)S(1)}, f32[8,4,24,128]{3,2,1,0:T(8,128)S(1)}, f32[256,128]{1,0:T(8,128)S(1)}) custom-call(s32[18]{0:T(128)S(1)} %pad_add_fusion.scalar_ref, f32[256,128]{1,0:T(8,128)S(1)} %get-tuple-element.32.c0_ref, f32[256,128]{1,0:T(8,128)S(1)} %collective-permute-done.11.c1_ref, ...), custom_call_target="tpu_custom_call" | custom-call | tf_op jit(solution)/shard_map/middle/pallas_call | solution.py:710
  46.6 0.7 %collective-permute-start.15 = (f32[256,128]{1,0:T(8,128)S(1)}, f32[256,128]{1,0:T(8,128)S(1)}, u32[]{:S(2)}, u32[]{:S(2)}) collective-permute-start(f32[256,128]{1,0:T(8,128)S(1)} %get-tuple-element.40.c0_ref), channel_id=1, source_target_pairs={{0,2},{1,3},{2,0},{3,1},{4,6},{5,7},{6,4},{7,5},{8,10},{9,11},{10,... | collective-permute-start | bytes 393224 | tf_op jit(solution)/shard_map/ppermute | solution.py:800
  47.3 0.7 %window.1.win_ref = f32[6,4,24,128]{3,2,1,0:T(8,128)S(1)} custom-call(s32[18]{0:T(128)S(1)} %pad_add_fusion.scalar_ref, f32[6,4,24,128]{3,2,1,0:T(8,128)S(1)} %get-tuple-element.41.qwin_ref, f32[8,4,24,128]{3,2,1,0:T(8,128)S(1)} %get-tuple-element.42.uwin_ref), custom_call_target="tpu_custom_call" | custom-call | tf_op jit(solution)/shard_map/window/pallas_call | solution.py:710
  48.0 4.2 %collective-permute-done.15.c2_ref = f32[256,128]{1,0:T(8,128)S(1)} collective-permute-done((f32[256,128]{1,0:T(8,128)S(1)}, f32[256,128]{1,0:T(8,128)S(1)}, u32[]{:S(2)}, u32[]{:S(2)}) %collective-permute-start.15) | collective-permute-done | bytes 131104 | tf_op jit(solution)/shard_map/ppermute | solution.py:800
  52.2 1.3 %collective-permute-done.16.c3_ref = f32[256,128]{1,0:T(8,128)S(1)} collective-permute-done((f32[256,128]{1,0:T(8,128)S(1)}, f32[256,128]{1,0:T(8,128)S(1)}, u32[]{:S(2)}, u32[]{:S(2)}) %collective-permute-start.16) | collective-permute-done | bytes 131104 | tf_op jit(solution)/shard_map/ppermute | solution.py:800
  53.5 4.0 %last.1 = f32[4,32,256]{2,1,0:T(8,128)} custom-call(s32[18]{0:T(128)S(1)} %pad_add_fusion.scalar_ref, f32[256,128]{1,0:T(8,128)S(1)} %get-tuple-element.40.c0_ref, f32[256,128]{1,0:T(8,128)S(1)} %collective-permute-done.14.c1_ref, f32[256,128]{1,0:T(8,128)S(1)} %collective-permute-done.15.c2_ref, f32[256,128]{1,0:T(8,128)S(1)} %collective-permute-done.16.c3_ref, ...), custom_call_target="tpu_custom_call" | custom-call | tf_op jit(solution)/shard_map/last/pallas_call | solution.py:710
  (12 shorter events, 0.1 us)
Async XLA Ops:
  1.8 10.7 %collective-permute-start = (f32[264,128]{1,0:T(8,128)S(1)}, f32[264,128]{1,0:T(8,128)S(1)}, u32[]{:S(2)}, u32[]{:S(2)}) collective-permute-start(f32[264,128]{1,0:T(8,128)S(1)} %pack.1.refs_0_), channel_id=1, source_target_pairs={{0,16},{4,20},{8,24},{12,28},{16,0},{20,4},{24,8},{28,12},{1,17},{... | collective-permute-start | bytes 405512 | tf_op jit(solution)/shard_map/ppermute | solution.py:747
  5.9 8.7 %collective-permute-start.6 = (f32[264,128]{1,0:T(8,128)S(1)}, f32[264,128]{1,0:T(8,128)S(1)}, u32[]{:S(2)}, u32[]{:S(2)}) collective-permute-start(f32[264,128]{1,0:T(8,128)S(1)} %pack.1.refs_0_), channel_id=1, source_target_pairs={{0,8},{4,12},{8,0},{12,4},{16,24},{20,28},{24,16},{28,20},{1,9},{5... | collective-permute-start | bytes 405512 | tf_op jit(solution)/shard_map/ppermute | solution.py:747
  7.5 9.5 %collective-permute-start.5 = (f32[264,128]{1,0:T(8,128)S(1)}, f32[264,128]{1,0:T(8,128)S(1)}, u32[]{:S(2)}, u32[]{:S(2)}) collective-permute-start(f32[264,128]{1,0:T(8,128)S(1)} %pack.1.refs_0_), channel_id=1, source_target_pairs={{0,4},{4,0},{8,12},{12,8},{16,20},{20,16},{24,28},{28,24},{1,5},{5... | collective-permute-start | bytes 405512 | tf_op jit(solution)/shard_map/ppermute | solution.py:747
  9.0 8.5 %collective-permute-start.4 = (f32[264,128]{1,0:T(8,128)S(1)}, f32[264,128]{1,0:T(8,128)S(1)}, u32[]{:S(2)}, u32[]{:S(2)}) collective-permute-start(f32[264,128]{1,0:T(8,128)S(1)} %pack.1.refs_0_), channel_id=1, source_target_pairs={{0,12},{4,8},{8,4},{12,0},{16,28},{20,24},{24,20},{28,16},{1,13},{... | collective-permute-start | bytes 405512 | tf_op jit(solution)/shard_map/ppermute | solution.py:747
  12.5 6.9 %collective-permute-start.3 = (f32[264,128]{1,0:T(8,128)S(1)}, f32[264,128]{1,0:T(8,128)S(1)}, u32[]{:S(2)}, u32[]{:S(2)}) collective-permute-start(f32[264,128]{1,0:T(8,128)S(1)} %collective-permute-done.refs_1_.refs_0_), channel_id=1, source_target_pairs={{0,8},{4,12},{8,0},{12,4},{16,24},{20,28},{24,16},{28,20},{1,9},{5... | collective-permute-start | bytes 405512 | tf_op jit(solution)/shard_map/ppermute | solution.py:747
  13.1 7.6 %collective-permute-start.2 = (f32[264,128]{1,0:T(8,128)S(1)}, f32[264,128]{1,0:T(8,128)S(1)}, u32[]{:S(2)}, u32[]{:S(2)}) collective-permute-start(f32[264,128]{1,0:T(8,128)S(1)} %collective-permute-done.refs_1_.refs_0_), channel_id=1, source_target_pairs={{0,4},{4,0},{8,12},{12,8},{16,20},{20,16},{24,28},{28,24},{1,5},{5... | collective-permute-start | bytes 405512 | tf_op jit(solution)/shard_map/ppermute | solution.py:747
  14.6 7.7 %collective-permute-start.1 = (f32[264,128]{1,0:T(8,128)S(1)}, f32[264,128]{1,0:T(8,128)S(1)}, u32[]{:S(2)}, u32[]{:S(2)}) collective-permute-start(f32[264,128]{1,0:T(8,128)S(1)} %collective-permute-done.refs_1_.refs_0_), channel_id=1, source_target_pairs={{0,12},{4,8},{8,4},{12,0},{16,28},{20,24},{24,20},{28,16},{1,13},{... | collective-permute-start | bytes 405512 | tf_op jit(solution)/shard_map/ppermute | solution.py:747
  18.0 5.8 %collective-permute-start.7 = (f32[40,8,128]{2,1,0:T(8,128)S(1)}, f32[40,8,128]{2,1,0:T(8,128)S(1)}, u32[]{:S(2)}, u32[]{:S(2)}) collective-permute-start(f32[40,8,128]{2,1,0:T(8,128)S(1)} %get-tuple-element.24), channel_id=1, source_target_pairs={{0,1},{2,3},{1,0},{3,2},{4,5},{6,7},{5,4},{7,6},{8,9},{10,11},{9,8... | collective-permute-start | bytes 491528 | tf_op jit(solution)/shard_map/ppermute | solution.py:756
  18.1 5.7 %collective-permute-start.8 = (f32[40,8,128]{2,1,0:T(8,128)S(1)}, f32[40,8,128]{2,1,0:T(8,128)S(1)}, u32[]{:S(2)}, u32[]{:S(2)}) collective-permute-start(f32[40,8,128]{2,1,0:T(8,128)S(1)} %get-tuple-element.25), channel_id=1, source_target_pairs={{1,2},{2,1},{5,6},{6,5},{9,10},{10,9},{13,14},{14,13},{17,18},{18,... | collective-permute-start | bytes 491528 | tf_op jit(solution)/shard_map/ppermute | solution.py:757
  23.1 2.4 %collective-permute-start.9 = (f32[25,8,128]{2,1,0:T(8,128)S(1)}, f32[25,8,128]{2,1,0:T(8,128)S(1)}, u32[]{:S(2)}, u32[]{:S(2)}) collective-permute-start(f32[25,8,128]{2,1,0:T(8,128)S(1)} %get-tuple-element.26), channel_id=1, source_target_pairs={{0,1},{2,3},{1,0},{3,2},{4,5},{6,7},{5,4},{7,6},{8,9},{10,11},{9,8... | collective-permute-start | bytes 307208 | tf_op jit(solution)/shard_map/ppermute | solution.py:756
  23.1 2.3 %collective-permute-start.10 = (f32[25,8,128]{2,1,0:T(8,128)S(1)}, f32[25,8,128]{2,1,0:T(8,128)S(1)}, u32[]{:S(2)}, u32[]{:S(2)}) collective-permute-start(f32[25,8,128]{2,1,0:T(8,128)S(1)} %get-tuple-element.27), channel_id=1, source_target_pairs={{1,2},{2,1},{5,6},{6,5},{9,10},{10,9},{13,14},{14,13},{17,18},{18,... | collective-permute-start | bytes 307208 | tf_op jit(solution)/shard_map/ppermute | solution.py:757
  28.8 9.5 %collective-permute-start.12 = (f32[256,128]{1,0:T(8,128)S(1)}, f32[256,128]{1,0:T(8,128)S(1)}, u32[]{:S(2)}, u32[]{:S(2)}) collective-permute-start(f32[256,128]{1,0:T(8,128)S(1)} %get-tuple-element.32.c0_ref), channel_id=1, source_target_pairs={{0,2},{1,3},{2,0},{3,1},{4,6},{5,7},{6,4},{7,5},{8,10},{9,11},{10,... | collective-permute-start | bytes 393224 | tf_op jit(solution)/shard_map/ppermute | solution.py:800
  34.0 4.5 %collective-permute-start.11 = (f32[256,128]{1,0:T(8,128)S(1)}, f32[256,128]{1,0:T(8,128)S(1)}, u32[]{:S(2)}, u32[]{:S(2)}) collective-permute-start(f32[256,128]{1,0:T(8,128)S(1)} %get-tuple-element.32.c0_ref), channel_id=1, source_target_pairs={{0,1},{1,0},{2,3},{3,2},{4,5},{5,4},{6,7},{7,6},{8,9},{9,8},{10,11... | collective-permute-start | bytes 393224 | tf_op jit(solution)/shard_map/ppermute | solution.py:800
  38.3 1.3 %collective-permute-start.13 = (f32[256,128]{1,0:T(8,128)S(1)}, f32[256,128]{1,0:T(8,128)S(1)}, u32[]{:S(2)}, u32[]{:S(2)}) collective-permute-start(f32[256,128]{1,0:T(8,128)S(1)} %collective-permute-done.12.c2_ref), channel_id=1, source_target_pairs={{0,1},{1,0},{2,3},{3,2},{4,5},{5,4},{6,7},{7,6},{8,9},{9,8},{10,11... | collective-permute-start | bytes 393224 | tf_op jit(solution)/shard_map/ppermute | solution.py:800
  46.6 5.6 %collective-permute-start.15 = (f32[256,128]{1,0:T(8,128)S(1)}, f32[256,128]{1,0:T(8,128)S(1)}, u32[]{:S(2)}, u32[]{:S(2)}) collective-permute-start(f32[256,128]{1,0:T(8,128)S(1)} %get-tuple-element.40.c0_ref), channel_id=1, source_target_pairs={{0,2},{1,3},{2,0},{3,1},{4,6},{5,7},{6,4},{7,5},{8,10},{9,11},{10,... | collective-permute-start | bytes 393224 | tf_op jit(solution)/shard_map/ppermute | solution.py:800
  47.3 4.9 %collective-permute-start.14 = (f32[256,128]{1,0:T(8,128)S(1)}, f32[256,128]{1,0:T(8,128)S(1)}, u32[]{:S(2)}, u32[]{:S(2)}) collective-permute-start(f32[256,128]{1,0:T(8,128)S(1)} %get-tuple-element.40.c0_ref), channel_id=1, source_target_pairs={{0,1},{1,0},{2,3},{3,2},{4,5},{5,4},{6,7},{7,6},{8,9},{9,8},{10,11... | collective-permute-start | bytes 393224 | tf_op jit(solution)/shard_map/ppermute | solution.py:800
  52.2 1.3 %collective-permute-start.16 = (f32[256,128]{1,0:T(8,128)S(1)}, f32[256,128]{1,0:T(8,128)S(1)}, u32[]{:S(2)}, u32[]{:S(2)}) collective-permute-start(f32[256,128]{1,0:T(8,128)S(1)} %collective-permute-done.15.c2_ref), channel_id=1, source_target_pairs={{0,1},{1,0},{2,3},{3,2},{4,5},{5,4},{6,7},{7,6},{8,9},{9,8},{10,11... | collective-permute-start | bytes 393224 | tf_op jit(solution)/shard_map/ppermute | solution.py:800

commit v7 on v6

--- a/solution.py
+++ b/solution.py
@@ -15,8 +15,8 @@
 HALO = 8
 LANES = 128
 UNROLL = 16
-PAIRS = 8
-HESS = 8
+PAIRS = 16
+HESS = 16
 LEVEL = 16
 LPAIRS = 4
 

time: 57.7 us -> 57.4 us (level)
  no operation moved by 1% of the time
where the time goes in v7:
time: 57.4 us; the launch traced here: 57.2 us
  Pallas kernels  20.3 us (35%)
  starting transfers between devices  18.9 us (33%)
  waiting for transfers between devices  16.6 us (29%)
  between operations  0.77 us (1%)
  other arithmetic  0.75 us (1%)
    pallas_call x9, Pallas kernels, call(): pl.pallas_call(kernel, out_shape=outs, in_specs=[smem()] * len(scalars) +...  20.3 us
    ppermute x7, starting transfers between devices, swap(): return lax.ppermute(x, 'slab', [(i, i ^ bits) for i in range(slabs)])  11.3 us
    ppermute x6, waiting for transfers between devices, pair(): return lax.ppermute(x, 'pencil', [(i, i ^ bits) for i in range(pencils)])  9.42 us
    ppermute x7, waiting for transfers between devices, swap(): return lax.ppermute(x, 'slab', [(i, i ^ bits) for i in range(slabs)])  7.13 us
    ppermute x6, starting transfers between devices, pair(): return lax.ppermute(x, 'pencil', [(i, i ^ bits) for i in range(pencils)])  6.07 us
    ppermute x2, starting transfers between devices, beside(): lax.ppermute(odd, 'pencil', high_pairs + [(j, i) for i, j in high_pairs])  1.34 us
  transfers between devices with their start and end apart: 17, of which 9 were waited for; matrix products, arithmetic and copies ran while one was open for 1% of the time, Pallas kernels for 9%

profile of v7, /device:TPU:0, one launch (start us, length us, event | category | flops | bytes accessed | tf_op | source)
XLA Modules:
  0.0 57.2 jit_solution(17732426191470841108)
XLA Ops:
  0.6 1.2 %pack.1.refs_0_ = f32[264,128]{1,0:T(8,128)S(1)} custom-call(f32[4,32,256]{2,1,0:T(8,128)} %potential_hbm.1, f32[4,2,4,32]{3,2,1,0:T(4,128)} %store_hbm.1), custom_call_target="tpu_custom_call" | custom-call | tf_op jit(solution)/shard_map/pack/pallas_call | solution.py:710
  1.8 4.1 %collective-permute-start = (f32[264,128]{1,0:T(8,128)S(1)}, f32[264,128]{1,0:T(8,128)S(1)}, u32[]{:S(2)}, u32[]{:S(2)}) collective-permute-start(f32[264,128]{1,0:T(8,128)S(1)} %pack.1.refs_0_), channel_id=1, source_target_pairs={{0,16},{4,20},{8,24},{12,28},{16,0},{20,4},{24,8},{28,12},{1,17},{... | collective-permute-start | bytes 405512 | tf_op jit(solution)/shard_map/ppermute | solution.py:747
  5.9 1.6 %collective-permute-start.6 = (f32[264,128]{1,0:T(8,128)S(1)}, f32[264,128]{1,0:T(8,128)S(1)}, u32[]{:S(2)}, u32[]{:S(2)}) collective-permute-start(f32[264,128]{1,0:T(8,128)S(1)} %pack.1.refs_0_), channel_id=1, source_target_pairs={{0,8},{4,12},{8,0},{12,4},{16,24},{20,28},{24,16},{28,20},{1,9},{5... | collective-permute-start | bytes 405512 | tf_op jit(solution)/shard_map/ppermute | solution.py:747
  7.5 1.5 %collective-permute-start.5 = (f32[264,128]{1,0:T(8,128)S(1)}, f32[264,128]{1,0:T(8,128)S(1)}, u32[]{:S(2)}, u32[]{:S(2)}) collective-permute-start(f32[264,128]{1,0:T(8,128)S(1)} %pack.1.refs_0_), channel_id=1, source_target_pairs={{0,4},{4,0},{8,12},{12,8},{16,20},{20,16},{24,28},{28,24},{1,5},{5... | collective-permute-start | bytes 405512 | tf_op jit(solution)/shard_map/ppermute | solution.py:747
  9.0 0.4 collective-permute-start.4
  9.4 3.1 %collective-permute-done.refs_1_.refs_0_ = f32[264,128]{1,0:T(8,128)S(1)} collective-permute-done((f32[264,128]{1,0:T(8,128)S(1)}, f32[264,128]{1,0:T(8,128)S(1)}, u32[]{:S(2)}, u32[]{:S(2)}) %collective-permute-start) | collective-permute-done | bytes 135200 | tf_op jit(solution)/shard_map/ppermute | solution.py:747
  12.5 0.7 %collective-permute-start.3 = (f32[264,128]{1,0:T(8,128)S(1)}, f32[264,128]{1,0:T(8,128)S(1)}, u32[]{:S(2)}, u32[]{:S(2)}) collective-permute-start(f32[264,128]{1,0:T(8,128)S(1)} %collective-permute-done.refs_1_.refs_0_), channel_id=1, source_target_pairs={{0,8},{4,12},{8,0},{12,4},{16,24},{20,28},{24,16},{28,20},{1,9},{5... | collective-permute-start | bytes 405512 | tf_op jit(solution)/shard_map/ppermute | solution.py:747
  13.1 1.5 %collective-permute-start.2 = (f32[264,128]{1,0:T(8,128)S(1)}, f32[264,128]{1,0:T(8,128)S(1)}, u32[]{:S(2)}, u32[]{:S(2)}) collective-permute-start(f32[264,128]{1,0:T(8,128)S(1)} %collective-permute-done.refs_1_.refs_0_), channel_id=1, source_target_pairs={{0,4},{4,0},{8,12},{12,8},{16,20},{20,16},{24,28},{28,24},{1,5},{5... | collective-permute-start | bytes 405512 | tf_op jit(solution)/shard_map/ppermute | solution.py:747
  14.6 1.6 %collective-permute-start.1 = (f32[264,128]{1,0:T(8,128)S(1)}, f32[264,128]{1,0:T(8,128)S(1)}, u32[]{:S(2)}, u32[]{:S(2)}) collective-permute-start(f32[264,128]{1,0:T(8,128)S(1)} %collective-permute-done.refs_1_.refs_0_), channel_id=1, source_target_pairs={{0,12},{4,8},{8,4},{12,0},{16,28},{20,24},{24,20},{28,16},{1,13},{... | collective-permute-start | bytes 405512 | tf_op jit(solution)/shard_map/ppermute | solution.py:747
  16.2 0.7 %pad_add_fusion.scalar_ref = s32[18]{0:T(128)S(1)} fusion(s32[8]{0:T(128)} %param.7, s32[8]{0:T(128)} %param.6, s32[1]{0:T(128)} %bitcast.1, s32[1]{0:T(128)} %bitcast), kind=kLoop, calls=%fused_computation | loop fusion | flops 54 | bytes 144 | tf_op jit(solution)/shard_map/concatenate | solution.py:729
  17.0 0.5 collective-permute-done.4.refs_2_.refs_1_
  17.4 0.6 %early_edges.1 = (f32[40,8,128]{2,1,0:T(8,128)S(1)}, f32[40,8,128]{2,1,0:T(8,128)S(1)}) custom-call(s32[18]{0:T(128)S(1)} %pad_add_fusion.scalar_ref, f32[264,128]{1,0:T(8,128)S(1)} %pack.1.refs_0_, f32[264,128]{1,0:T(8,128)S(1)} %collective-permute-done.refs_1_.refs_0_, f32[264,128]{1,0:T(8,128)S(1)} %collective-permute-done.4.refs_2_.refs_1_, ...), custom_call_target="tpu_custom_call" | custom-call | tf_op jit(solution)/shard_map/early_edges/pallas_call | solution.py:710
  18.0 0.1 collective-permute-start.7
  18.1 0.7 %collective-permute-start.8 = (f32[40,8,128]{2,1,0:T(8,128)S(1)}, f32[40,8,128]{2,1,0:T(8,128)S(1)}, u32[]{:S(2)}, u32[]{:S(2)}) collective-permute-start(f32[40,8,128]{2,1,0:T(8,128)S(1)} %get-tuple-element.25), channel_id=1, source_target_pairs={{1,2},{2,1},{5,6},{6,5},{9,10},{10,9},{13,14},{14,13},{17,18},{18,... | collective-permute-start | bytes 491528 | tf_op jit(solution)/shard_map/ppermute | solution.py:757
  18.8 0.6 %collective-permute-done.3.refs_7_.refs_3_ = f32[264,128]{1,0:T(8,128)S(1)} collective-permute-done((f32[264,128]{1,0:T(8,128)S(1)}, f32[264,128]{1,0:T(8,128)S(1)}, u32[]{:S(2)}, u32[]{:S(2)}) %collective-permute-start.3) | collective-permute-done | bytes 135200 | tf_op jit(solution)/shard_map/ppermute | solution.py:747
  19.3 1.4 %collective-permute-done.2.refs_6_.refs_2_ = f32[264,128]{1,0:T(8,128)S(1)} collective-permute-done((f32[264,128]{1,0:T(8,128)S(1)}, f32[264,128]{1,0:T(8,128)S(1)}, u32[]{:S(2)}, u32[]{:S(2)}) %collective-permute-start.2) | collective-permute-done | bytes 135200 | tf_op jit(solution)/shard_map/ppermute | solution.py:747
  20.8 1.6 %collective-permute-done.1.refs_5_.refs_1_ = f32[264,128]{1,0:T(8,128)S(1)} collective-permute-done((f32[264,128]{1,0:T(8,128)S(1)}, f32[264,128]{1,0:T(8,128)S(1)}, u32[]{:S(2)}, u32[]{:S(2)}) %collective-permute-start.1) | collective-permute-done | bytes 135200 | tf_op jit(solution)/shard_map/ppermute | solution.py:747
  22.3 0.7 %late_edges.1 = (f32[25,8,128]{2,1,0:T(8,128)S(1)}, f32[25,8,128]{2,1,0:T(8,128)S(1)}, f32[32,128]{1,0:T(8,128)S(1)}) custom-call(s32[18]{0:T(128)S(1)} %pad_add_fusion.scalar_ref, f32[264,128]{1,0:T(8,128)S(1)} %pack.1.refs_0_, f32[264,128]{1,0:T(8,128)S(1)} %collective-permute-done.refs_1_.refs_0_, f32[264,128]{1,0:T(8,128)S(1)} %collective-permute-done.4.refs_2_.refs_1_, ...), custom_call_target="tpu_custom_call" | custom-call | tf_op jit(solution)/shard_map/late_edges/pallas_call | solution.py:710
  23.1 0.7 %collective-permute-start.10 = (f32[25,8,128]{2,1,0:T(8,128)S(1)}, f32[25,8,128]{2,1,0:T(8,128)S(1)}, u32[]{:S(2)}, u32[]{:S(2)}) collective-permute-start(f32[25,8,128]{2,1,0:T(8,128)S(1)} %get-tuple-element.27), channel_id=1, source_target_pairs={{1,2},{2,1},{5,6},{6,5},{9,10},{10,9},{13,14},{14,13},{17,18},{18,... | collective-permute-start | bytes 307208 | tf_op jit(solution)/shard_map/ppermute | solution.py:757
  23.8 1.6 %near_half.1 = (f32[18,4,24,128]{3,2,1,0:T(8,128)S(1)}, f32[16,4,16,128]{3,2,1,0:T(8,128)S(1)}, f32[16,4,24,128]{3,2,1,0:T(8,128)S(1)}) custom-call(s32[18]{0:T(128)S(1)} %pad_add_fusion.scalar_ref, f32[264,128]{1,0:T(8,128)S(1)} %pack.1.refs_0_, f32[264,128]{1,0:T(8,128)S(1)} %collective-permute-done.4.refs_2_.refs_1_, ...), custom_call_target="tpu_custom_call" | custom-call | tf_op jit(solution)/shard_map/near_half/pallas_call | solution.py:710
  25.5 3.0 %far_half.1 = (f32[4,4,16,128]{3,2,1,0:T(8,128)S(1)}, f32[36,4,24,128]{3,2,1,0:T(8,128)S(1)}, f32[36,4,24,128]{3,2,1,0:T(8,128)S(1)}, f32[256,128]{1,0:T(8,128)S(1)}) custom-call(s32[18]{0:T(128)S(1)} %pad_add_fusion.scalar_ref, f32[264,128]{1,0:T(8,128)S(1)} %collective-permute-done.refs_1_.refs_0_, f32[264,128]{1,0:T(8,128)S(1)} %collective-permute-done.1.refs_5_.refs_1_, ...), custom_call_target="tpu_custom_call" | custom-call | tf_op jit(solution)/shard_map/far_half/pallas_call | solution.py:710
  28.5 5.2 %collective-permute-start.12 = (f32[256,128]{1,0:T(8,128)S(1)}, f32[256,128]{1,0:T(8,128)S(1)}, u32[]{:S(2)}, u32[]{:S(2)}) collective-permute-start(f32[256,128]{1,0:T(8,128)S(1)} %get-tuple-element.32.c0_ref), channel_id=1, source_target_pairs={{0,2},{1,3},{2,0},{3,1},{4,6},{5,7},{6,4},{7,5},{8,10},{9,11},{10,... | collective-permute-start | bytes 393224 | tf_op jit(solution)/shard_map/ppermute | solution.py:800
  33.7 1.7 %between.1 = (f32[4,32,256]{2,1,0:T(8,128)}, f32[36,4,24,128]{3,2,1,0:T(8,128)S(1)}) custom-call(s32[18]{0:T(128)S(1)} %pad_add_fusion.scalar_ref, f32[36,4,24,128]{3,2,1,0:T(8,128)S(1)} %get-tuple-element.33.q_ref, f32[36,4,24,128]{3,2,1,0:T(8,128)S(1)} %get-tuple-element.34.u_ref, f32[4,4,16,128]{3,2,1,0:T(8,128)S(1)} %get-tuple-element.35.s_ref), custom_call_target="tpu_custom_call" | custom-call | tf_op jit(solution)/shard_map/between/pallas_call | solution.py:710
  35.4 2.7 %collective-permute-done.12.c2_ref = f32[256,128]{1,0:T(8,128)S(1)} collective-permute-done((f32[256,128]{1,0:T(8,128)S(1)}, f32[256,128]{1,0:T(8,128)S(1)}, u32[]{:S(2)}, u32[]{:S(2)}) %collective-permute-start.12) | collective-permute-done | bytes 131104 | tf_op jit(solution)/shard_map/ppermute | solution.py:800
  38.1 0.1 collective-permute-start.13
  38.2 1.2 %collective-permute-done.13.c3_ref = f32[256,128]{1,0:T(8,128)S(1)} collective-permute-done((f32[256,128]{1,0:T(8,128)S(1)}, f32[256,128]{1,0:T(8,128)S(1)}, u32[]{:S(2)}, u32[]{:S(2)}) %collective-permute-start.13) | collective-permute-done | bytes 131104 | tf_op jit(solution)/shard_map/ppermute | solution.py:800
  39.4 6.8 %middle.1 = (f32[6,4,24,128]{3,2,1,0:T(8,128)S(1)}, f32[8,4,24,128]{3,2,1,0:T(8,128)S(1)}, f32[256,128]{1,0:T(8,128)S(1)}) custom-call(s32[18]{0:T(128)S(1)} %pad_add_fusion.scalar_ref, f32[256,128]{1,0:T(8,128)S(1)} %get-tuple-element.32.c0_ref, f32[256,128]{1,0:T(8,128)S(1)} %collective-permute-done.11.c1_ref, ...), custom_call_target="tpu_custom_call" | custom-call | tf_op jit(solution)/shard_map/middle/pallas_call | solution.py:710
  46.2 0.7 %collective-permute-start.15 = (f32[256,128]{1,0:T(8,128)S(1)}, f32[256,128]{1,0:T(8,128)S(1)}, u32[]{:S(2)}, u32[]{:S(2)}) collective-permute-start(f32[256,128]{1,0:T(8,128)S(1)} %get-tuple-element.40.c0_ref), channel_id=1, source_target_pairs={{0,2},{1,3},{2,0},{3,1},{4,6},{5,7},{6,4},{7,5},{8,10},{9,11},{10,... | collective-permute-start | bytes 393224 | tf_op jit(solution)/shard_map/ppermute | solution.py:800
  46.9 0.7 %window.1.win_ref = f32[6,4,24,128]{3,2,1,0:T(8,128)S(1)} custom-call(s32[18]{0:T(128)S(1)} %pad_add_fusion.scalar_ref, f32[6,4,24,128]{3,2,1,0:T(8,128)S(1)} %get-tuple-element.41.qwin_ref, f32[8,4,24,128]{3,2,1,0:T(8,128)S(1)} %get-tuple-element.42.uwin_ref), custom_call_target="tpu_custom_call" | custom-call | tf_op jit(solution)/shard_map/window/pallas_call | solution.py:710
  47.7 4.2 %collective-permute-done.15.c2_ref = f32[256,128]{1,0:T(8,128)S(1)} collective-permute-done((f32[256,128]{1,0:T(8,128)S(1)}, f32[256,128]{1,0:T(8,128)S(1)}, u32[]{:S(2)}, u32[]{:S(2)}) %collective-permute-start.15) | collective-permute-done | bytes 131104 | tf_op jit(solution)/shard_map/ppermute | solution.py:800
  51.9 1.3 %collective-permute-done.16.c3_ref = f32[256,128]{1,0:T(8,128)S(1)} collective-permute-done((f32[256,128]{1,0:T(8,128)S(1)}, f32[256,128]{1,0:T(8,128)S(1)}, u32[]{:S(2)}, u32[]{:S(2)}) %collective-permute-start.16) | collective-permute-done | bytes 131104 | tf_op jit(solution)/shard_map/ppermute | solution.py:800
  53.2 4.0 %last.1 = f32[4,32,256]{2,1,0:T(8,128)} custom-call(s32[18]{0:T(128)S(1)} %pad_add_fusion.scalar_ref, f32[256,128]{1,0:T(8,128)S(1)} %get-tuple-element.40.c0_ref, f32[256,128]{1,0:T(8,128)S(1)} %collective-permute-done.14.c1_ref, f32[256,128]{1,0:T(8,128)S(1)} %collective-permute-done.15.c2_ref, f32[256,128]{1,0:T(8,128)S(1)} %collective-permute-done.16.c3_ref, ...), custom_call_target="tpu_custom_call" | custom-call | tf_op jit(solution)/shard_map/last/pallas_call | solution.py:710
  (12 shorter events, 0.1 us)
Async XLA Ops:
  1.8 10.7 %collective-permute-start = (f32[264,128]{1,0:T(8,128)S(1)}, f32[264,128]{1,0:T(8,128)S(1)}, u32[]{:S(2)}, u32[]{:S(2)}) collective-permute-start(f32[264,128]{1,0:T(8,128)S(1)} %pack.1.refs_0_), channel_id=1, source_target_pairs={{0,16},{4,20},{8,24},{12,28},{16,0},{20,4},{24,8},{28,12},{1,17},{... | collective-permute-start | bytes 405512 | tf_op jit(solution)/shard_map/ppermute | solution.py:747
  5.9 8.7 %collective-permute-start.6 = (f32[264,128]{1,0:T(8,128)S(1)}, f32[264,128]{1,0:T(8,128)S(1)}, u32[]{:S(2)}, u32[]{:S(2)}) collective-permute-start(f32[264,128]{1,0:T(8,128)S(1)} %pack.1.refs_0_), channel_id=1, source_target_pairs={{0,8},{4,12},{8,0},{12,4},{16,24},{20,28},{24,16},{28,20},{1,9},{5... | collective-permute-start | bytes 405512 | tf_op jit(solution)/shard_map/ppermute | solution.py:747
  7.5 9.5 %collective-permute-start.5 = (f32[264,128]{1,0:T(8,128)S(1)}, f32[264,128]{1,0:T(8,128)S(1)}, u32[]{:S(2)}, u32[]{:S(2)}) collective-permute-start(f32[264,128]{1,0:T(8,128)S(1)} %pack.1.refs_0_), channel_id=1, source_target_pairs={{0,4},{4,0},{8,12},{12,8},{16,20},{20,16},{24,28},{28,24},{1,5},{5... | collective-permute-start | bytes 405512 | tf_op jit(solution)/shard_map/ppermute | solution.py:747
  9.0 8.5 %collective-permute-start.4 = (f32[264,128]{1,0:T(8,128)S(1)}, f32[264,128]{1,0:T(8,128)S(1)}, u32[]{:S(2)}, u32[]{:S(2)}) collective-permute-start(f32[264,128]{1,0:T(8,128)S(1)} %pack.1.refs_0_), channel_id=1, source_target_pairs={{0,12},{4,8},{8,4},{12,0},{16,28},{20,24},{24,20},{28,16},{1,13},{... | collective-permute-start | bytes 405512 | tf_op jit(solution)/shard_map/ppermute | solution.py:747
  12.5 6.9 %collective-permute-start.3 = (f32[264,128]{1,0:T(8,128)S(1)}, f32[264,128]{1,0:T(8,128)S(1)}, u32[]{:S(2)}, u32[]{:S(2)}) collective-permute-start(f32[264,128]{1,0:T(8,128)S(1)} %collective-permute-done.refs_1_.refs_0_), channel_id=1, source_target_pairs={{0,8},{4,12},{8,0},{12,4},{16,24},{20,28},{24,16},{28,20},{1,9},{5... | collective-permute-start | bytes 405512 | tf_op jit(solution)/shard_map/ppermute | solution.py:747
  13.1 7.6 %collective-permute-start.2 = (f32[264,128]{1,0:T(8,128)S(1)}, f32[264,128]{1,0:T(8,128)S(1)}, u32[]{:S(2)}, u32[]{:S(2)}) collective-permute-start(f32[264,128]{1,0:T(8,128)S(1)} %collective-permute-done.refs_1_.refs_0_), channel_id=1, source_target_pairs={{0,4},{4,0},{8,12},{12,8},{16,20},{20,16},{24,28},{28,24},{1,5},{5... | collective-permute-start | bytes 405512 | tf_op jit(solution)/shard_map/ppermute | solution.py:747
  14.6 7.7 %collective-permute-start.1 = (f32[264,128]{1,0:T(8,128)S(1)}, f32[264,128]{1,0:T(8,128)S(1)}, u32[]{:S(2)}, u32[]{:S(2)}) collective-permute-start(f32[264,128]{1,0:T(8,128)S(1)} %collective-permute-done.refs_1_.refs_0_), channel_id=1, source_target_pairs={{0,12},{4,8},{8,4},{12,0},{16,28},{20,24},{24,20},{28,16},{1,13},{... | collective-permute-start | bytes 405512 | tf_op jit(solution)/shard_map/ppermute | solution.py:747
  18.0 5.8 %collective-permute-start.7 = (f32[40,8,128]{2,1,0:T(8,128)S(1)}, f32[40,8,128]{2,1,0:T(8,128)S(1)}, u32[]{:S(2)}, u32[]{:S(2)}) collective-permute-start(f32[40,8,128]{2,1,0:T(8,128)S(1)} %get-tuple-element.24), channel_id=1, source_target_pairs={{0,1},{2,3},{1,0},{3,2},{4,5},{6,7},{5,4},{7,6},{8,9},{10,11},{9,8... | collective-permute-start | bytes 491528 | tf_op jit(solution)/shard_map/ppermute | solution.py:756
  18.1 5.7 %collective-permute-start.8 = (f32[40,8,128]{2,1,0:T(8,128)S(1)}, f32[40,8,128]{2,1,0:T(8,128)S(1)}, u32[]{:S(2)}, u32[]{:S(2)}) collective-permute-start(f32[40,8,128]{2,1,0:T(8,128)S(1)} %get-tuple-element.25), channel_id=1, source_target_pairs={{1,2},{2,1},{5,6},{6,5},{9,10},{10,9},{13,14},{14,13},{17,18},{18,... | collective-permute-start | bytes 491528 | tf_op jit(solution)/shard_map/ppermute | solution.py:757
  23.1 2.4 %collective-permute-start.9 = (f32[25,8,128]{2,1,0:T(8,128)S(1)}, f32[25,8,128]{2,1,0:T(8,128)S(1)}, u32[]{:S(2)}, u32[]{:S(2)}) collective-permute-start(f32[25,8,128]{2,1,0:T(8,128)S(1)} %get-tuple-element.26), channel_id=1, source_target_pairs={{0,1},{2,3},{1,0},{3,2},{4,5},{6,7},{5,4},{7,6},{8,9},{10,11},{9,8... | collective-permute-start | bytes 307208 | tf_op jit(solution)/shard_map/ppermute | solution.py:756
  23.1 2.3 %collective-permute-start.10 = (f32[25,8,128]{2,1,0:T(8,128)S(1)}, f32[25,8,128]{2,1,0:T(8,128)S(1)}, u32[]{:S(2)}, u32[]{:S(2)}) collective-permute-start(f32[25,8,128]{2,1,0:T(8,128)S(1)} %get-tuple-element.27), channel_id=1, source_target_pairs={{1,2},{2,1},{5,6},{6,5},{9,10},{10,9},{13,14},{14,13},{17,18},{18,... | collective-permute-start | bytes 307208 | tf_op jit(solution)/shard_map/ppermute | solution.py:757
  28.5 9.6 %collective-permute-start.12 = (f32[256,128]{1,0:T(8,128)S(1)}, f32[256,128]{1,0:T(8,128)S(1)}, u32[]{:S(2)}, u32[]{:S(2)}) collective-permute-start(f32[256,128]{1,0:T(8,128)S(1)} %get-tuple-element.32.c0_ref), channel_id=1, source_target_pairs={{0,2},{1,3},{2,0},{3,1},{4,6},{5,7},{6,4},{7,5},{8,10},{9,11},{10,... | collective-permute-start | bytes 393224 | tf_op jit(solution)/shard_map/ppermute | solution.py:800
  33.7 4.5 %collective-permute-start.11 = (f32[256,128]{1,0:T(8,128)S(1)}, f32[256,128]{1,0:T(8,128)S(1)}, u32[]{:S(2)}, u32[]{:S(2)}) collective-permute-start(f32[256,128]{1,0:T(8,128)S(1)} %get-tuple-element.32.c0_ref), channel_id=1, source_target_pairs={{0,1},{1,0},{2,3},{3,2},{4,5},{5,4},{6,7},{7,6},{8,9},{9,8},{10,11... | collective-permute-start | bytes 393224 | tf_op jit(solution)/shard_map/ppermute | solution.py:800
  38.1 1.3 %collective-permute-start.13 = (f32[256,128]{1,0:T(8,128)S(1)}, f32[256,128]{1,0:T(8,128)S(1)}, u32[]{:S(2)}, u32[]{:S(2)}) collective-permute-start(f32[256,128]{1,0:T(8,128)S(1)} %collective-permute-done.12.c2_ref), channel_id=1, source_target_pairs={{0,1},{1,0},{2,3},{3,2},{4,5},{5,4},{6,7},{7,6},{8,9},{9,8},{10,11... | collective-permute-start | bytes 393224 | tf_op jit(solution)/shard_map/ppermute | solution.py:800
  46.2 5.6 %collective-permute-start.15 = (f32[256,128]{1,0:T(8,128)S(1)}, f32[256,128]{1,0:T(8,128)S(1)}, u32[]{:S(2)}, u32[]{:S(2)}) collective-permute-start(f32[256,128]{1,0:T(8,128)S(1)} %get-tuple-element.40.c0_ref), channel_id=1, source_target_pairs={{0,2},{1,3},{2,0},{3,1},{4,6},{5,7},{6,4},{7,5},{8,10},{9,11},{10,... | collective-permute-start | bytes 393224 | tf_op jit(solution)/shard_map/ppermute | solution.py:800
  46.9 4.9 %collective-permute-start.14 = (f32[256,128]{1,0:T(8,128)S(1)}, f32[256,128]{1,0:T(8,128)S(1)}, u32[]{:S(2)}, u32[]{:S(2)}) collective-permute-start(f32[256,128]{1,0:T(8,128)S(1)} %get-tuple-element.40.c0_ref), channel_id=1, source_target_pairs={{0,1},{1,0},{2,3},{3,2},{4,5},{5,4},{6,7},{7,6},{8,9},{9,8},{10,11... | collective-permute-start | bytes 393224 | tf_op jit(solution)/shard_map/ppermute | solution.py:800
  51.8 1.3 %collective-permute-start.16 = (f32[256,128]{1,0:T(8,128)S(1)}, f32[256,128]{1,0:T(8,128)S(1)}, u32[]{:S(2)}, u32[]{:S(2)}) collective-permute-start(f32[256,128]{1,0:T(8,128)S(1)} %collective-permute-done.15.c2_ref), channel_id=1, source_target_pairs={{0,1},{1,0},{2,3},{3,2},{4,5},{5,4},{6,7},{7,6},{8,9},{9,8},{10,11... | collective-permute-start | bytes 393224 | tf_op jit(solution)/shard_map/ppermute | solution.py:800

commit v8 on v7

--- a/solution.py
+++ b/solution.py
@@ -422,12 +422,16 @@
     return jnp.where(lane == 0, turned, 0.0)
 
 
-def fill_block(p_ref, at, ref, edge_refs, tile, pencil, depth, part):
+def fill_rows(p_ref, at, ref, depth, part):
+    for z in range(depth):
+        for c in range(4):
+            p_ref[at + z, c, pl.ds(0, part), :] = block_rows(ref, (4 * z + c) * part, part)
+
+
+def fill_halo(p_ref, at, edge_refs, tile, pencil, depth, part):
     is_even = (pencil % 2) == 0
     low_half = row_iota((8, LANES)) < 4
     for z in range(depth):
-        for c in range(4):
-            p_ref[at + z, c, pl.ds(0, part), :] = block_rows(ref, (4 * z + c) * part, part)
         for t in range(2):
             first, second = halo_tiles(*edge_refs, tile + 2 * z + t, is_even, low_half)
             p_ref[at + z, 2 * t, pl.ds(part, 8), :] = first
@@ -436,8 +440,7 @@
 
 def near_half_kernel(scalar_ref, *refs, depth, width, pencils):
     near = [k for k in range(EARLY) if OFFSETS[k] < 4]
-    blocks = refs[: len(near)]
-    even_ref, odd_ref, faces_ref, p_ref, s_ref, q_ref = refs[len(near) :]
+    even_ref, odd_ref, faces_ref, p_ref, s_ref, q_ref, far_ref = refs[len(OFFSETS) :]
     slab = scalar_ref[0]
     pencil = scalar_ref[1]
     part = width // 2
@@ -447,9 +450,11 @@
     blank = jnp.zeros(p_ref.shape[1:], jnp.float32)
     p_ref[0] = blank
     p_ref[half + 1] = blank
-    for k, ref in zip(near, blocks):
+    for k, ref in enumerate(refs[: len(OFFSETS)]):
         at = ((slab ^ OFFSETS[k]) % 4) * depth + 1
-        fill_block(p_ref, at, ref, (even_ref, odd_ref), 2 * depth * k, pencil, depth, part)
+        fill_rows(p_ref if k in near else far_ref, at, ref, depth, part)
+        if k in near:
+            fill_halo(p_ref, at, (even_ref, odd_ref), 2 * depth * k, pencil, depth, part)
 
     def body(j, carry):
         source = hessian_parts(parts(p_ref, j), parts(p_ref, j + 1), parts(p_ref, j + 2))
@@ -457,8 +462,9 @@
             s_ref[j, c] = source[c][:part]
             face = faces_ref[pl.ds((c >> 1) * part, part), :]
             face = face_part(face, c, first_plane + j, 2 * half)
-            q_ref[j, c, pl.ds(0, part), :] = W * (face - source[c][:part])
-            q_ref[j, c, pl.ds(part, 8), :] = (-W * mask) * source[c][part:]
+            at = first_plane + j + 2
+            q_ref[at, c, pl.ds(0, part), :] = W * (face - source[c][:part])
+            q_ref[at, c, pl.ds(part, 8), :] = (-W * mask) * source[c][part:]
         return carry
 
     lax.fori_loop(0, half, body, 0, unroll=HESS)
@@ -466,12 +472,9 @@
 
 def far_half_kernel(scalar_ref, *refs, depth, width, pencils):
     far = [k for k in range(len(OFFSETS)) if OFFSETS[k] >= 4]
-    blocks = refs[: len(far)]
-    early_refs = refs[len(far) : len(far) + 2]
-    late_refs = refs[len(far) + 2 : len(far) + 4]
-    faces_ref, pn_ref, sn_ref, qn_ref = refs[len(far) + 4 : len(far) + 8]
-    s_ref, q_ref, u_ref, coarse_ref = refs[len(far) + 8 : len(far) + 12]
-    p_ref, f_ref = refs[len(far) + 12 :]
+    early_refs, late_refs = refs[:2], refs[2:4]
+    faces_ref, pn_ref, sn_ref = refs[4:7]
+    s_ref, q_ref, u_ref, coarse_ref, p_ref, f_ref = refs[9:]
     slab = scalar_ref[0]
     pencil = scalar_ref[1]
     part = width // 2
@@ -489,12 +492,12 @@
             ref[z] = blank
     p_ref[jnp.where(lower, half + 1, 0)] = blank
     p_ref[jnp.where(lower, 0, half + 1)] = pn_ref[jnp.where(lower, half, 1)]
-    for k, ref in zip(far, blocks):
+    for k in far:
         at = ((slab ^ OFFSETS[k]) % 4) * depth + 1
         early = k < EARLY
         tile = 2 * depth * (k if early else k - EARLY)
         edge_refs = early_refs if early else late_refs
-        fill_block(p_ref, at, ref, edge_refs, tile, pencil, depth, part)
+        fill_halo(p_ref, at, edge_refs, tile, pencil, depth, part)
     face_tile = 2 * depth * (len(OFFSETS) - EARLY)
     first, second = halo_tiles(*late_refs, face_tile, is_even, low_half)
     f_ref[0, pl.ds(0, part), :] = faces_ref[pl.ds(0, part), :]
@@ -511,10 +514,8 @@
         z = near_first + j
         for c in range(4):
             face = face_part(f_ref[c >> 1, pl.ds(part, 8), :], c, z, planes)
-            q_ref[z + 2, c, pl.ds(0, part), :] = qn_ref[j, c, pl.ds(0, part), :]
-            q_ref[z + 2, c, pl.ds(part, 8), :] = (
-                qn_ref[j, c, pl.ds(part, 8), :] + (W * mask) * face
-            )
+            tile = pl.ds(part, 8)
+            q_ref[z + 2, c, tile, :] = q_ref[z + 2, c, tile, :] + (W * mask) * face
         return carry
 
     lax.fori_loop(0, half, copy, 0, unroll=UNROLL)
@@ -703,7 +704,7 @@
     return pltpu.VMEM(shape, jnp.float32)
 
 
-def call(kernel, name, scalars, args, outs, scratch=(), space=pltpu.VMEM, out_space=None):
+def call(kernel, name, scalars, args, outs, scratch=(), space=pltpu.VMEM, out_space=None, aliases={}):
     out_specs = jax.tree.map(lambda _: vmem(), outs)
     if out_space is not None:
         out_specs = tuple(pl.BlockSpec(memory_space=one) for one in out_space)
@@ -715,6 +716,7 @@
         scratch_shapes=list(scratch),
         compiler_params=pltpu.CompilerParams(vmem_limit_bytes=16 << 20),
         name=name,
+        input_output_aliases=aliases,
     )(*scalars, *args)
 
 
@@ -784,16 +786,28 @@
         partial(near_half_kernel, depth=depth, width=width, pencils=pencils),
         "near_half",
         [scalars],
-        [b for b, offset in zip(blocks, OFFSETS) if offset < 4] + [*early, faces],
-        (arr(half + 2, 4, rows, LANES), arr(half, 4, part, LANES), arr(half, 4, rows, LANES)),
-    )
-    own_source, q, u, coarse = call(
+        [*blocks, *early, faces],
+        (
+            arr(half + 2, 4, rows, LANES),
+            arr(half, 4, part, LANES),
+            arr(*field),
+            arr(half + 2, 4, rows, LANES),
+        ),
+    )
+    own_source, q, u, coarse, _ = call(
         partial(far_half_kernel, depth=depth, width=width, pencils=pencils),
         "far_half",
         [scalars],
-        [b for b, offset in zip(blocks, OFFSETS) if offset >= 4] + [*early, *late, faces, *near],
-        (arr(depth, 4, part, LANES), arr(*field), arr(*field), coarse_part),
-        [buf(half + 2, 4, rows, LANES), buf(2, rows, LANES)],
+        [*early, *late, faces, *near],
+        (
+            arr(depth, 4, part, LANES),
+            arr(*field),
+            arr(*field),
+            coarse_part,
+            arr(half + 2, 4, rows, LANES),
+        ),
+        [buf(2, rows, LANES)],
+        aliases={8: 1, 9: 4},
     )
 
     def pair(x, bits):

time: 57.4 us -> 57.4 us (level)
  no operation moved by 1% of the time
where the time goes in v8:
time: 57.4 us; the launch traced here: 57.2 us
  Pallas kernels  20.3 us (35%)
  starting transfers between devices  18.8 us (33%)
  waiting for transfers between devices  16.6 us (29%)
  between operations  0.77 us (1%)
  other arithmetic  0.75 us (1%)
    pallas_call x9, Pallas kernels, call(): pl.pallas_call(kernel, out_shape=outs, in_specs=[smem()] * len(scalars) +...  20.3 us
    ppermute x7, starting transfers between devices, swap(): return lax.ppermute(x, 'slab', [(i, i ^ bits) for i in range(slabs)])  11.3 us
    ppermute x6, waiting for transfers between devices, pair(): return lax.ppermute(x, 'pencil', [(i, i ^ bits) for i in range(pencils)])  9.42 us
    ppermute x7, waiting for transfers between devices, swap(): return lax.ppermute(x, 'slab', [(i, i ^ bits) for i in range(slabs)])  7.13 us
    ppermute x6, starting transfers between devices, pair(): return lax.ppermute(x, 'pencil', [(i, i ^ bits) for i in range(pencils)])  6.03 us
    ppermute x2, starting transfers between devices, beside(): lax.ppermute(odd, 'pencil', high_pairs + [(j, i) for i, j in high_pairs])  1.34 us
  transfers between devices with their start and end apart: 17, of which 9 were waited for; matrix products, arithmetic and copies ran while one was open for 1% of the time, Pallas kernels for 9%

profile of v8, /device:TPU:0, one launch (start us, length us, event | category | flops | bytes accessed | tf_op | source)
XLA Modules:
  0.0 57.2 jit_solution(5773298843414866361)
XLA Ops:
  0.6 1.2 %pack.1.refs_0_ = f32[264,128]{1,0:T(8,128)S(1)} custom-call(f32[4,32,256]{2,1,0:T(8,128)} %potential_hbm.1, f32[4,2,4,32]{3,2,1,0:T(4,128)} %store_hbm.1), custom_call_target="tpu_custom_call" | custom-call | tf_op jit(solution)/shard_map/pack/pallas_call | solution.py:711
  1.8 4.1 %collective-permute-start = (f32[264,128]{1,0:T(8,128)S(1)}, f32[264,128]{1,0:T(8,128)S(1)}, u32[]{:S(2)}, u32[]{:S(2)}) collective-permute-start(f32[264,128]{1,0:T(8,128)S(1)} %pack.1.refs_0_), channel_id=1, source_target_pairs={{0,16},{4,20},{8,24},{12,28},{16,0},{20,4},{24,8},{28,12},{1,17},{... | collective-permute-start | bytes 405512 | tf_op jit(solution)/shard_map/ppermute | solution.py:749
  5.9 1.6 %collective-permute-start.3 = (f32[264,128]{1,0:T(8,128)S(1)}, f32[264,128]{1,0:T(8,128)S(1)}, u32[]{:S(2)}, u32[]{:S(2)}) collective-permute-start(f32[264,128]{1,0:T(8,128)S(1)} %pack.1.refs_0_), channel_id=1, source_target_pairs={{0,8},{4,12},{8,0},{12,4},{16,24},{20,28},{24,16},{28,20},{1,9},{5... | collective-permute-start | bytes 405512 | tf_op jit(solution)/shard_map/ppermute | solution.py:749
  7.5 1.5 %collective-permute-start.2 = (f32[264,128]{1,0:T(8,128)S(1)}, f32[264,128]{1,0:T(8,128)S(1)}, u32[]{:S(2)}, u32[]{:S(2)}) collective-permute-start(f32[264,128]{1,0:T(8,128)S(1)} %pack.1.refs_0_), channel_id=1, source_target_pairs={{0,4},{4,0},{8,12},{12,8},{16,20},{20,16},{24,28},{28,24},{1,5},{5... | collective-permute-start | bytes 405512 | tf_op jit(solution)/shard_map/ppermute | solution.py:749
  9.0 0.4 collective-permute-start.1
  9.4 3.1 %collective-permute-done.refs_1_ = f32[264,128]{1,0:T(8,128)S(1)} collective-permute-done((f32[264,128]{1,0:T(8,128)S(1)}, f32[264,128]{1,0:T(8,128)S(1)}, u32[]{:S(2)}, u32[]{:S(2)}) %collective-permute-start) | collective-permute-done | bytes 135200 | tf_op jit(solution)/shard_map/ppermute | solution.py:749
  12.5 0.7 %collective-permute-start.8 = (f32[264,128]{1,0:T(8,128)S(1)}, f32[264,128]{1,0:T(8,128)S(1)}, u32[]{:S(2)}, u32[]{:S(2)}) collective-permute-start(f32[264,128]{1,0:T(8,128)S(1)} %collective-permute-done.refs_1_), channel_id=1, source_target_pairs={{0,8},{4,12},{8,0},{12,4},{16,24},{20,28},{24,16},{28,20},{1,9},{5... | collective-permute-start | bytes 405512 | tf_op jit(solution)/shard_map/ppermute | solution.py:749
  13.1 1.5 %collective-permute-start.7 = (f32[264,128]{1,0:T(8,128)S(1)}, f32[264,128]{1,0:T(8,128)S(1)}, u32[]{:S(2)}, u32[]{:S(2)}) collective-permute-start(f32[264,128]{1,0:T(8,128)S(1)} %collective-permute-done.refs_1_), channel_id=1, source_target_pairs={{0,4},{4,0},{8,12},{12,8},{16,20},{20,16},{24,28},{28,24},{1,5},{5... | collective-permute-start | bytes 405512 | tf_op jit(solution)/shard_map/ppermute | solution.py:749
  14.6 1.6 %collective-permute-start.6 = (f32[264,128]{1,0:T(8,128)S(1)}, f32[264,128]{1,0:T(8,128)S(1)}, u32[]{:S(2)}, u32[]{:S(2)}) collective-permute-start(f32[264,128]{1,0:T(8,128)S(1)} %collective-permute-done.refs_1_), channel_id=1, source_target_pairs={{0,12},{4,8},{8,4},{12,0},{16,28},{20,24},{24,20},{28,16},{1,13},{... | collective-permute-start | bytes 405512 | tf_op jit(solution)/shard_map/ppermute | solution.py:749
  16.2 0.7 %pad_add_fusion.scalar_ref = s32[18]{0:T(128)S(1)} fusion(s32[8]{0:T(128)} %param.7, s32[8]{0:T(128)} %param.6, s32[1]{0:T(128)} %bitcast.1, s32[1]{0:T(128)} %bitcast), kind=kLoop, calls=%fused_computation | loop fusion | flops 54 | bytes 144 | tf_op jit(solution)/shard_map/concatenate | solution.py:731
  17.0 0.5 collective-permute-done.1.refs_2_
  17.4 0.6 %early_edges.1 = (f32[40,8,128]{2,1,0:T(8,128)S(1)}, f32[40,8,128]{2,1,0:T(8,128)S(1)}) custom-call(s32[18]{0:T(128)S(1)} %pad_add_fusion.scalar_ref, f32[264,128]{1,0:T(8,128)S(1)} %pack.1.refs_0_, f32[264,128]{1,0:T(8,128)S(1)} %collective-permute-done.refs_1_, f32[264,128]{1,0:T(8,128)S(1)} %collective-permute-done.1.refs_2_, ...), custom_call_target="tpu_custom_call" | custom-call | tf_op jit(solution)/shard_map/early_edges/pallas_call | solution.py:711
  18.0 0.1 collective-permute-start.4
  18.1 0.7 %collective-permute-start.5 = (f32[40,8,128]{2,1,0:T(8,128)S(1)}, f32[40,8,128]{2,1,0:T(8,128)S(1)}, u32[]{:S(2)}, u32[]{:S(2)}) collective-permute-start(f32[40,8,128]{2,1,0:T(8,128)S(1)} %get-tuple-element.26), channel_id=1, source_target_pairs={{1,2},{2,1},{5,6},{6,5},{9,10},{10,9},{13,14},{14,13},{17,18},{18,... | collective-permute-start | bytes 491528 | tf_op jit(solution)/shard_map/ppermute | solution.py:759
  18.8 0.6 %collective-permute-done.8.refs_7_ = f32[264,128]{1,0:T(8,128)S(1)} collective-permute-done((f32[264,128]{1,0:T(8,128)S(1)}, f32[264,128]{1,0:T(8,128)S(1)}, u32[]{:S(2)}, u32[]{:S(2)}) %collective-permute-start.8) | collective-permute-done | bytes 135200 | tf_op jit(solution)/shard_map/ppermute | solution.py:749
  19.3 1.4 %collective-permute-done.7.refs_6_ = f32[264,128]{1,0:T(8,128)S(1)} collective-permute-done((f32[264,128]{1,0:T(8,128)S(1)}, f32[264,128]{1,0:T(8,128)S(1)}, u32[]{:S(2)}, u32[]{:S(2)}) %collective-permute-start.7) | collective-permute-done | bytes 135200 | tf_op jit(solution)/shard_map/ppermute | solution.py:749
  20.8 1.6 %collective-permute-done.6.refs_5_ = f32[264,128]{1,0:T(8,128)S(1)} collective-permute-done((f32[264,128]{1,0:T(8,128)S(1)}, f32[264,128]{1,0:T(8,128)S(1)}, u32[]{:S(2)}, u32[]{:S(2)}) %collective-permute-start.6) | collective-permute-done | bytes 135200 | tf_op jit(solution)/shard_map/ppermute | solution.py:749
  22.3 0.7 %late_edges.1 = (f32[25,8,128]{2,1,0:T(8,128)S(1)}, f32[25,8,128]{2,1,0:T(8,128)S(1)}, f32[32,128]{1,0:T(8,128)S(1)}) custom-call(s32[18]{0:T(128)S(1)} %pad_add_fusion.scalar_ref, f32[264,128]{1,0:T(8,128)S(1)} %pack.1.refs_0_, f32[264,128]{1,0:T(8,128)S(1)} %collective-permute-done.refs_1_, f32[264,128]{1,0:T(8,128)S(1)} %collective-permute-done.1.refs_2_, ...), custom_call_target="tpu_custom_call" | custom-call | tf_op jit(solution)/shard_map/late_edges/pallas_call | solution.py:711
  23.1 0.7 %collective-permute-start.10 = (f32[25,8,128]{2,1,0:T(8,128)S(1)}, f32[25,8,128]{2,1,0:T(8,128)S(1)}, u32[]{:S(2)}, u32[]{:S(2)}) collective-permute-start(f32[25,8,128]{2,1,0:T(8,128)S(1)} %get-tuple-element.28), channel_id=1, source_target_pairs={{1,2},{2,1},{5,6},{6,5},{9,10},{10,9},{13,14},{14,13},{17,18},{18,... | collective-permute-start | bytes 307208 | tf_op jit(solution)/shard_map/ppermute | solution.py:759
  23.8 1.6 %near_half.1 = (f32[18,4,24,128]{3,2,1,0:T(8,128)S(1)}, f32[16,4,16,128]{3,2,1,0:T(8,128)S(1)}, f32[36,4,24,128]{3,2,1,0:T(8,128)S(1)}, f32[18,4,24,128]{3,2,1,0:T(8,128)S(1)}) custom-call(s32[18]{0:T(128)S(1)} %pad_add_fusion.scalar_ref, f32[264,128]{1,0:T(8,128)S(1)} %pack.1.refs_0_, f32[264,128]{1,0:T(8,128)S(1)} %collective-permute-done.refs_1_, ...), custom_call_target="tpu_custom_call" | custom-call | tf_op jit(solution)/shard_map/near_half/pallas_call | solution.py:711
  25.5 3.0 %far_half.1 = (f32[4,4,16,128]{3,2,1,0:T(8,128)S(1)}, f32[36,4,24,128]{3,2,1,0:T(8,128)S(1)}, f32[36,4,24,128]{3,2,1,0:T(8,128)S(1)}, f32[256,128]{1,0:T(8,128)S(1)}, f32[18,4,24,128]{3,2,1,0:T(8,128)S(1)}) custom-call(s32[18]{0:T(128)S(1)} %pad_add_fusion.scalar_ref, ...), custom_call_target="tpu_custom_call", output_to_operand_aliasing={{1}: (8, {}), {4}: (9, {})} | custom-call | tf_op jit(solution)/shard_map/far_half/pallas_call | solution.py:711
  28.5 5.2 %collective-permute-start.12 = (f32[256,128]{1,0:T(8,128)S(1)}, f32[256,128]{1,0:T(8,128)S(1)}, u32[]{:S(2)}, u32[]{:S(2)}) collective-permute-start(f32[256,128]{1,0:T(8,128)S(1)} %get-tuple-element.34.c0_ref), channel_id=1, source_target_pairs={{0,2},{1,3},{2,0},{3,1},{4,6},{5,7},{6,4},{7,5},{8,10},{9,11},{10,... | collective-permute-start | bytes 393224 | tf_op jit(solution)/shard_map/ppermute | solution.py:814
  33.7 1.7 %between.1 = (f32[4,32,256]{2,1,0:T(8,128)}, f32[36,4,24,128]{3,2,1,0:T(8,128)S(1)}) custom-call(s32[18]{0:T(128)S(1)} %pad_add_fusion.scalar_ref, f32[36,4,24,128]{3,2,1,0:T(8,128)S(1)} %get-tuple-element.35.q_ref, f32[36,4,24,128]{3,2,1,0:T(8,128)S(1)} %get-tuple-element.36.u_ref, f32[4,4,16,128]{3,2,1,0:T(8,128)S(1)} %get-tuple-element.37.s_ref), custom_call_target="tpu_custom_call" | custom-call | tf_op jit(solution)/shard_map/between/pallas_call | solution.py:711
  35.4 2.7 %collective-permute-done.12.c2_ref = f32[256,128]{1,0:T(8,128)S(1)} collective-permute-done((f32[256,128]{1,0:T(8,128)S(1)}, f32[256,128]{1,0:T(8,128)S(1)}, u32[]{:S(2)}, u32[]{:S(2)}) %collective-permute-start.12) | collective-permute-done | bytes 131104 | tf_op jit(solution)/shard_map/ppermute | solution.py:814
  38.1 0.1 collective-permute-start.13
  38.2 1.2 %collective-permute-done.13.c3_ref = f32[256,128]{1,0:T(8,128)S(1)} collective-permute-done((f32[256,128]{1,0:T(8,128)S(1)}, f32[256,128]{1,0:T(8,128)S(1)}, u32[]{:S(2)}, u32[]{:S(2)}) %collective-permute-start.13) | collective-permute-done | bytes 131104 | tf_op jit(solution)/shard_map/ppermute | solution.py:814
  39.4 6.8 %middle.1 = (f32[6,4,24,128]{3,2,1,0:T(8,128)S(1)}, f32[8,4,24,128]{3,2,1,0:T(8,128)S(1)}, f32[256,128]{1,0:T(8,128)S(1)}) custom-call(s32[18]{0:T(128)S(1)} %pad_add_fusion.scalar_ref, f32[256,128]{1,0:T(8,128)S(1)} %get-tuple-element.34.c0_ref, f32[256,128]{1,0:T(8,128)S(1)} %collective-permute-done.11.c1_ref, ...), custom_call_target="tpu_custom_call" | custom-call | tf_op jit(solution)/shard_map/middle/pallas_call | solution.py:711
  46.2 0.7 %collective-permute-start.15 = (f32[256,128]{1,0:T(8,128)S(1)}, f32[256,128]{1,0:T(8,128)S(1)}, u32[]{:S(2)}, u32[]{:S(2)}) collective-permute-start(f32[256,128]{1,0:T(8,128)S(1)} %get-tuple-element.42.c0_ref), channel_id=1, source_target_pairs={{0,2},{1,3},{2,0},{3,1},{4,6},{5,7},{6,4},{7,5},{8,10},{9,11},{10,... | collective-permute-start | bytes 393224 | tf_op jit(solution)/shard_map/ppermute | solution.py:814
  46.9 0.7 %window.1.win_ref = f32[6,4,24,128]{3,2,1,0:T(8,128)S(1)} custom-call(s32[18]{0:T(128)S(1)} %pad_add_fusion.scalar_ref, f32[6,4,24,128]{3,2,1,0:T(8,128)S(1)} %get-tuple-element.43.qwin_ref, f32[8,4,24,128]{3,2,1,0:T(8,128)S(1)} %get-tuple-element.44.uwin_ref), custom_call_target="tpu_custom_call" | custom-call | tf_op jit(solution)/shard_map/window/pallas_call | solution.py:711
  47.7 4.2 %collective-permute-done.15.c2_ref = f32[256,128]{1,0:T(8,128)S(1)} collective-permute-done((f32[256,128]{1,0:T(8,128)S(1)}, f32[256,128]{1,0:T(8,128)S(1)}, u32[]{:S(2)}, u32[]{:S(2)}) %collective-permute-start.15) | collective-permute-done | bytes 131104 | tf_op jit(solution)/shard_map/ppermute | solution.py:814
  51.9 1.3 %collective-permute-done.16.c3_ref = f32[256,128]{1,0:T(8,128)S(1)} collective-permute-done((f32[256,128]{1,0:T(8,128)S(1)}, f32[256,128]{1,0:T(8,128)S(1)}, u32[]{:S(2)}, u32[]{:S(2)}) %collective-permute-start.16) | collective-permute-done | bytes 131104 | tf_op jit(solution)/shard_map/ppermute | solution.py:814
  53.2 4.0 %last.1 = f32[4,32,256]{2,1,0:T(8,128)} custom-call(s32[18]{0:T(128)S(1)} %pad_add_fusion.scalar_ref, f32[256,128]{1,0:T(8,128)S(1)} %get-tuple-element.42.c0_ref, f32[256,128]{1,0:T(8,128)S(1)} %collective-permute-done.14.c1_ref, f32[256,128]{1,0:T(8,128)S(1)} %collective-permute-done.15.c2_ref, f32[256,128]{1,0:T(8,128)S(1)} %collective-permute-done.16.c3_ref, ...), custom_call_target="tpu_custom_call" | custom-call | tf_op jit(solution)/shard_map/last/pallas_call | solution.py:711
  (12 shorter events, 0.1 us)
Async XLA Ops:
  1.8 10.7 %collective-permute-start = (f32[264,128]{1,0:T(8,128)S(1)}, f32[264,128]{1,0:T(8,128)S(1)}, u32[]{:S(2)}, u32[]{:S(2)}) collective-permute-start(f32[264,128]{1,0:T(8,128)S(1)} %pack.1.refs_0_), channel_id=1, source_target_pairs={{0,16},{4,20},{8,24},{12,28},{16,0},{20,4},{24,8},{28,12},{1,17},{... | collective-permute-start | bytes 405512 | tf_op jit(solution)/shard_map/ppermute | solution.py:749
  5.9 8.7 %collective-permute-start.3 = (f32[264,128]{1,0:T(8,128)S(1)}, f32[264,128]{1,0:T(8,128)S(1)}, u32[]{:S(2)}, u32[]{:S(2)}) collective-permute-start(f32[264,128]{1,0:T(8,128)S(1)} %pack.1.refs_0_), channel_id=1, source_target_pairs={{0,8},{4,12},{8,0},{12,4},{16,24},{20,28},{24,16},{28,20},{1,9},{5... | collective-permute-start | bytes 405512 | tf_op jit(solution)/shard_map/ppermute | solution.py:749
  7.5 9.5 %collective-permute-start.2 = (f32[264,128]{1,0:T(8,128)S(1)}, f32[264,128]{1,0:T(8,128)S(1)}, u32[]{:S(2)}, u32[]{:S(2)}) collective-permute-start(f32[264,128]{1,0:T(8,128)S(1)} %pack.1.refs_0_), channel_id=1, source_target_pairs={{0,4},{4,0},{8,12},{12,8},{16,20},{20,16},{24,28},{28,24},{1,5},{5... | collective-permute-start | bytes 405512 | tf_op jit(solution)/shard_map/ppermute | solution.py:749
  9.0 8.5 %collective-permute-start.1 = (f32[264,128]{1,0:T(8,128)S(1)}, f32[264,128]{1,0:T(8,128)S(1)}, u32[]{:S(2)}, u32[]{:S(2)}) collective-permute-start(f32[264,128]{1,0:T(8,128)S(1)} %pack.1.refs_0_), channel_id=1, source_target_pairs={{0,12},{4,8},{8,4},{12,0},{16,28},{20,24},{24,20},{28,16},{1,13},{... | collective-permute-start | bytes 405512 | tf_op jit(solution)/shard_map/ppermute | solution.py:749
  12.5 6.9 %collective-permute-start.8 = (f32[264,128]{1,0:T(8,128)S(1)}, f32[264,128]{1,0:T(8,128)S(1)}, u32[]{:S(2)}, u32[]{:S(2)}) collective-permute-start(f32[264,128]{1,0:T(8,128)S(1)} %collective-permute-done.refs_1_), channel_id=1, source_target_pairs={{0,8},{4,12},{8,0},{12,4},{16,24},{20,28},{24,16},{28,20},{1,9},{5... | collective-permute-start | bytes 405512 | tf_op jit(solution)/shard_map/ppermute | solution.py:749
  13.1 7.6 %collective-permute-start.7 = (f32[264,128]{1,0:T(8,128)S(1)}, f32[264,128]{1,0:T(8,128)S(1)}, u32[]{:S(2)}, u32[]{:S(2)}) collective-permute-start(f32[264,128]{1,0:T(8,128)S(1)} %collective-permute-done.refs_1_), channel_id=1, source_target_pairs={{0,4},{4,0},{8,12},{12,8},{16,20},{20,16},{24,28},{28,24},{1,5},{5... | collective-permute-start | bytes 405512 | tf_op jit(solution)/shard_map/ppermute | solution.py:749
  14.6 7.7 %collective-permute-start.6 = (f32[264,128]{1,0:T(8,128)S(1)}, f32[264,128]{1,0:T(8,128)S(1)}, u32[]{:S(2)}, u32[]{:S(2)}) collective-permute-start(f32[264,128]{1,0:T(8,128)S(1)} %collective-permute-done.refs_1_), channel_id=1, source_target_pairs={{0,12},{4,8},{8,4},{12,0},{16,28},{20,24},{24,20},{28,16},{1,13},{... | collective-permute-start | bytes 405512 | tf_op jit(solution)/shard_map/ppermute | solution.py:749
  18.0 5.8 %collective-permute-start.4 = (f32[40,8,128]{2,1,0:T(8,128)S(1)}, f32[40,8,128]{2,1,0:T(8,128)S(1)}, u32[]{:S(2)}, u32[]{:S(2)}) collective-permute-start(f32[40,8,128]{2,1,0:T(8,128)S(1)} %get-tuple-element.25), channel_id=1, source_target_pairs={{0,1},{2,3},{1,0},{3,2},{4,5},{6,7},{5,4},{7,6},{8,9},{10,11},{9,8... | collective-permute-start | bytes 491528 | tf_op jit(solution)/shard_map/ppermute | solution.py:758
  18.1 5.7 %collective-permute-start.5 = (f32[40,8,128]{2,1,0:T(8,128)S(1)}, f32[40,8,128]{2,1,0:T(8,128)S(1)}, u32[]{:S(2)}, u32[]{:S(2)}) collective-permute-start(f32[40,8,128]{2,1,0:T(8,128)S(1)} %get-tuple-element.26), channel_id=1, source_target_pairs={{1,2},{2,1},{5,6},{6,5},{9,10},{10,9},{13,14},{14,13},{17,18},{18,... | collective-permute-start | bytes 491528 | tf_op jit(solution)/shard_map/ppermute | solution.py:759
  23.1 2.4 %collective-permute-start.9 = (f32[25,8,128]{2,1,0:T(8,128)S(1)}, f32[25,8,128]{2,1,0:T(8,128)S(1)}, u32[]{:S(2)}, u32[]{:S(2)}) collective-permute-start(f32[25,8,128]{2,1,0:T(8,128)S(1)} %get-tuple-element.27), channel_id=1, source_target_pairs={{0,1},{2,3},{1,0},{3,2},{4,5},{6,7},{5,4},{7,6},{8,9},{10,11},{9,8... | collective-permute-start | bytes 307208 | tf_op jit(solution)/shard_map/ppermute | solution.py:758
  23.1 2.3 %collective-permute-start.10 = (f32[25,8,128]{2,1,0:T(8,128)S(1)}, f32[25,8,128]{2,1,0:T(8,128)S(1)}, u32[]{:S(2)}, u32[]{:S(2)}) collective-permute-start(f32[25,8,128]{2,1,0:T(8,128)S(1)} %get-tuple-element.28), channel_id=1, source_target_pairs={{1,2},{2,1},{5,6},{6,5},{9,10},{10,9},{13,14},{14,13},{17,18},{18,... | collective-permute-start | bytes 307208 | tf_op jit(solution)/shard_map/ppermute | solution.py:759
  28.5 9.5 %collective-permute-start.12 = (f32[256,128]{1,0:T(8,128)S(1)}, f32[256,128]{1,0:T(8,128)S(1)}, u32[]{:S(2)}, u32[]{:S(2)}) collective-permute-start(f32[256,128]{1,0:T(8,128)S(1)} %get-tuple-element.34.c0_ref), channel_id=1, source_target_pairs={{0,2},{1,3},{2,0},{3,1},{4,6},{5,7},{6,4},{7,5},{8,10},{9,11},{10,... | collective-permute-start | bytes 393224 | tf_op jit(solution)/shard_map/ppermute | solution.py:814
  33.7 4.5 %collective-permute-start.11 = (f32[256,128]{1,0:T(8,128)S(1)}, f32[256,128]{1,0:T(8,128)S(1)}, u32[]{:S(2)}, u32[]{:S(2)}) collective-permute-start(f32[256,128]{1,0:T(8,128)S(1)} %get-tuple-element.34.c0_ref), channel_id=1, source_target_pairs={{0,1},{1,0},{2,3},{3,2},{4,5},{5,4},{6,7},{7,6},{8,9},{9,8},{10,11... | collective-permute-start | bytes 393224 | tf_op jit(solution)/shard_map/ppermute | solution.py:814
  38.1 1.3 %collective-permute-start.13 = (f32[256,128]{1,0:T(8,128)S(1)}, f32[256,128]{1,0:T(8,128)S(1)}, u32[]{:S(2)}, u32[]{:S(2)}) collective-permute-start(f32[256,128]{1,0:T(8,128)S(1)} %collective-permute-done.12.c2_ref), channel_id=1, source_target_pairs={{0,1},{1,0},{2,3},{3,2},{4,5},{5,4},{6,7},{7,6},{8,9},{9,8},{10,11... | collective-permute-start | bytes 393224 | tf_op jit(solution)/shard_map/ppermute | solution.py:814
  46.2 5.6 %collective-permute-start.15 = (f32[256,128]{1,0:T(8,128)S(1)}, f32[256,128]{1,0:T(8,128)S(1)}, u32[]{:S(2)}, u32[]{:S(2)}) collective-permute-start(f32[256,128]{1,0:T(8,128)S(1)} %get-tuple-element.42.c0_ref), channel_id=1, source_target_pairs={{0,2},{1,3},{2,0},{3,1},{4,6},{5,7},{6,4},{7,5},{8,10},{9,11},{10,... | collective-permute-start | bytes 393224 | tf_op jit(solution)/shard_map/ppermute | solution.py:814
  46.9 4.9 %collective-permute-start.14 = (f32[256,128]{1,0:T(8,128)S(1)}, f32[256,128]{1,0:T(8,128)S(1)}, u32[]{:S(2)}, u32[]{:S(2)}) collective-permute-start(f32[256,128]{1,0:T(8,128)S(1)} %get-tuple-element.42.c0_ref), channel_id=1, source_target_pairs={{0,1},{1,0},{2,3},{3,2},{4,5},{5,4},{6,7},{7,6},{8,9},{9,8},{10,11... | collective-permute-start | bytes 393224 | tf_op jit(solution)/shard_map/ppermute | solution.py:814
  51.9 1.3 %collective-permute-start.16 = (f32[256,128]{1,0:T(8,128)S(1)}, f32[256,128]{1,0:T(8,128)S(1)}, u32[]{:S(2)}, u32[]{:S(2)}) collective-permute-start(f32[256,128]{1,0:T(8,128)S(1)} %collective-permute-done.15.c2_ref), channel_id=1, source_target_pairs={{0,1},{1,0},{2,3},{3,2},{4,5},{5,4},{6,7},{7,6},{8,9},{9,8},{10,11... | collective-permute-start | bytes 393224 | tf_op jit(solution)/shard_map/ppermute | solution.py:814

commit v9 on v8

--- a/solution.py
+++ b/solution.py
@@ -18,7 +18,7 @@
 PAIRS = 16
 HESS = 16
 LEVEL = 16
-LPAIRS = 4
+LPAIRS = 8
 
 
 def is_coarsest(shape):

time: 57.4 us -> 57.5 us (level)
  no operation moved by 1% of the time
where the time goes in v9:
time: 57.5 us; the launch traced here: 57.3 us
  Pallas kernels  20.4 us (35%)
  starting transfers between devices  18.8 us (33%)
  waiting for transfers between devices  16.6 us (29%)
  between operations  0.77 us (1%)
  other arithmetic  0.75 us (1%)
    pallas_call x9, Pallas kernels, call(): pl.pallas_call(kernel, out_shape=outs, in_specs=[smem()] * len(scalars) +...  20.4 us
    ppermute x7, starting transfers between devices, swap(): return lax.ppermute(x, 'slab', [(i, i ^ bits) for i in range(slabs)])  11.3 us
    ppermute x6, waiting for transfers between devices, pair(): return lax.ppermute(x, 'pencil', [(i, i ^ bits) for i in range(pencils)])  9.42 us
    ppermute x7, waiting for transfers between devices, swap(): return lax.ppermute(x, 'slab', [(i, i ^ bits) for i in range(slabs)])  7.13 us
    ppermute x6, starting transfers between devices, pair(): return lax.ppermute(x, 'pencil', [(i, i ^ bits) for i in range(pencils)])  6.03 us
    ppermute x2, starting transfers between devices, beside(): lax.ppermute(odd, 'pencil', high_pairs + [(j, i) for i, j in high_pairs])  1.34 us
  transfers between devices with their start and end apart: 17, of which 9 were waited for; matrix products, arithmetic and copies ran while one was open for 1% of the time, Pallas kernels for 9%

profile of v9, /device:TPU:0, one launch (start us, length us, event | category | flops | bytes accessed | tf_op | source)
XLA Modules:
  0.0 57.3 jit_solution(13286247534216515414)
XLA Ops:
  0.6 1.2 %pack.1.refs_0_ = f32[264,128]{1,0:T(8,128)S(1)} custom-call(f32[4,32,256]{2,1,0:T(8,128)} %potential_hbm.1, f32[4,2,4,32]{3,2,1,0:T(4,128)} %store_hbm.1), custom_call_target="tpu_custom_call" | custom-call | tf_op jit(solution)/shard_map/pack/pallas_call | solution.py:711
  1.8 4.1 %collective-permute-start = (f32[264,128]{1,0:T(8,128)S(1)}, f32[264,128]{1,0:T(8,128)S(1)}, u32[]{:S(2)}, u32[]{:S(2)}) collective-permute-start(f32[264,128]{1,0:T(8,128)S(1)} %pack.1.refs_0_), channel_id=1, source_target_pairs={{0,16},{4,20},{8,24},{12,28},{16,0},{20,4},{24,8},{28,12},{1,17},{... | collective-permute-start | bytes 405512 | tf_op jit(solution)/shard_map/ppermute | solution.py:749
  5.9 1.6 %collective-permute-start.3 = (f32[264,128]{1,0:T(8,128)S(1)}, f32[264,128]{1,0:T(8,128)S(1)}, u32[]{:S(2)}, u32[]{:S(2)}) collective-permute-start(f32[264,128]{1,0:T(8,128)S(1)} %pack.1.refs_0_), channel_id=1, source_target_pairs={{0,8},{4,12},{8,0},{12,4},{16,24},{20,28},{24,16},{28,20},{1,9},{5... | collective-permute-start | bytes 405512 | tf_op jit(solution)/shard_map/ppermute | solution.py:749
  7.5 1.5 %collective-permute-start.2 = (f32[264,128]{1,0:T(8,128)S(1)}, f32[264,128]{1,0:T(8,128)S(1)}, u32[]{:S(2)}, u32[]{:S(2)}) collective-permute-start(f32[264,128]{1,0:T(8,128)S(1)} %pack.1.refs_0_), channel_id=1, source_target_pairs={{0,4},{4,0},{8,12},{12,8},{16,20},{20,16},{24,28},{28,24},{1,5},{5... | collective-permute-start | bytes 405512 | tf_op jit(solution)/shard_map/ppermute | solution.py:749
  9.0 0.4 collective-permute-start.1
  9.4 3.1 %collective-permute-done.refs_1_ = f32[264,128]{1,0:T(8,128)S(1)} collective-permute-done((f32[264,128]{1,0:T(8,128)S(1)}, f32[264,128]{1,0:T(8,128)S(1)}, u32[]{:S(2)}, u32[]{:S(2)}) %collective-permute-start) | collective-permute-done | bytes 135200 | tf_op jit(solution)/shard_map/ppermute | solution.py:749
  12.5 0.7 %collective-permute-start.8 = (f32[264,128]{1,0:T(8,128)S(1)}, f32[264,128]{1,0:T(8,128)S(1)}, u32[]{:S(2)}, u32[]{:S(2)}) collective-permute-start(f32[264,128]{1,0:T(8,128)S(1)} %collective-permute-done.refs_1_), channel_id=1, source_target_pairs={{0,8},{4,12},{8,0},{12,4},{16,24},{20,28},{24,16},{28,20},{1,9},{5... | collective-permute-start | bytes 405512 | tf_op jit(solution)/shard_map/ppermute | solution.py:749
  13.1 1.5 %collective-permute-start.7 = (f32[264,128]{1,0:T(8,128)S(1)}, f32[264,128]{1,0:T(8,128)S(1)}, u32[]{:S(2)}, u32[]{:S(2)}) collective-permute-start(f32[264,128]{1,0:T(8,128)S(1)} %collective-permute-done.refs_1_), channel_id=1, source_target_pairs={{0,4},{4,0},{8,12},{12,8},{16,20},{20,16},{24,28},{28,24},{1,5},{5... | collective-permute-start | bytes 405512 | tf_op jit(solution)/shard_map/ppermute | solution.py:749
  14.6 1.6 %collective-permute-start.6 = (f32[264,128]{1,0:T(8,128)S(1)}, f32[264,128]{1,0:T(8,128)S(1)}, u32[]{:S(2)}, u32[]{:S(2)}) collective-permute-start(f32[264,128]{1,0:T(8,128)S(1)} %collective-permute-done.refs_1_), channel_id=1, source_target_pairs={{0,12},{4,8},{8,4},{12,0},{16,28},{20,24},{24,20},{28,16},{1,13},{... | collective-permute-start | bytes 405512 | tf_op jit(solution)/shard_map/ppermute | solution.py:749
  16.2 0.7 %pad_add_fusion.scalar_ref = s32[18]{0:T(128)S(1)} fusion(s32[8]{0:T(128)} %param.7, s32[8]{0:T(128)} %param.6, s32[1]{0:T(128)} %bitcast.1, s32[1]{0:T(128)} %bitcast), kind=kLoop, calls=%fused_computation | loop fusion | flops 54 | bytes 144 | tf_op jit(solution)/shard_map/concatenate | solution.py:731
  17.0 0.5 collective-permute-done.1.refs_2_
  17.4 0.6 %early_edges.1 = (f32[40,8,128]{2,1,0:T(8,128)S(1)}, f32[40,8,128]{2,1,0:T(8,128)S(1)}) custom-call(s32[18]{0:T(128)S(1)} %pad_add_fusion.scalar_ref, f32[264,128]{1,0:T(8,128)S(1)} %pack.1.refs_0_, f32[264,128]{1,0:T(8,128)S(1)} %collective-permute-done.refs_1_, f32[264,128]{1,0:T(8,128)S(1)} %collective-permute-done.1.refs_2_, ...), custom_call_target="tpu_custom_call" | custom-call | tf_op jit(solution)/shard_map/early_edges/pallas_call | solution.py:711
  18.0 0.1 collective-permute-start.4
  18.1 0.7 %collective-permute-start.5 = (f32[40,8,128]{2,1,0:T(8,128)S(1)}, f32[40,8,128]{2,1,0:T(8,128)S(1)}, u32[]{:S(2)}, u32[]{:S(2)}) collective-permute-start(f32[40,8,128]{2,1,0:T(8,128)S(1)} %get-tuple-element.26), channel_id=1, source_target_pairs={{1,2},{2,1},{5,6},{6,5},{9,10},{10,9},{13,14},{14,13},{17,18},{18,... | collective-permute-start | bytes 491528 | tf_op jit(solution)/shard_map/ppermute | solution.py:759
  18.8 0.6 %collective-permute-done.8.refs_7_ = f32[264,128]{1,0:T(8,128)S(1)} collective-permute-done((f32[264,128]{1,0:T(8,128)S(1)}, f32[264,128]{1,0:T(8,128)S(1)}, u32[]{:S(2)}, u32[]{:S(2)}) %collective-permute-start.8) | collective-permute-done | bytes 135200 | tf_op jit(solution)/shard_map/ppermute | solution.py:749
  19.3 1.4 %collective-permute-done.7.refs_6_ = f32[264,128]{1,0:T(8,128)S(1)} collective-permute-done((f32[264,128]{1,0:T(8,128)S(1)}, f32[264,128]{1,0:T(8,128)S(1)}, u32[]{:S(2)}, u32[]{:S(2)}) %collective-permute-start.7) | collective-permute-done | bytes 135200 | tf_op jit(solution)/shard_map/ppermute | solution.py:749
  20.8 1.6 %collective-permute-done.6.refs_5_ = f32[264,128]{1,0:T(8,128)S(1)} collective-permute-done((f32[264,128]{1,0:T(8,128)S(1)}, f32[264,128]{1,0:T(8,128)S(1)}, u32[]{:S(2)}, u32[]{:S(2)}) %collective-permute-start.6) | collective-permute-done | bytes 135200 | tf_op jit(solution)/shard_map/ppermute | solution.py:749
  22.3 0.7 %late_edges.1 = (f32[25,8,128]{2,1,0:T(8,128)S(1)}, f32[25,8,128]{2,1,0:T(8,128)S(1)}, f32[32,128]{1,0:T(8,128)S(1)}) custom-call(s32[18]{0:T(128)S(1)} %pad_add_fusion.scalar_ref, f32[264,128]{1,0:T(8,128)S(1)} %pack.1.refs_0_, f32[264,128]{1,0:T(8,128)S(1)} %collective-permute-done.refs_1_, f32[264,128]{1,0:T(8,128)S(1)} %collective-permute-done.1.refs_2_, ...), custom_call_target="tpu_custom_call" | custom-call | tf_op jit(solution)/shard_map/late_edges/pallas_call | solution.py:711
  23.1 0.7 %collective-permute-start.10 = (f32[25,8,128]{2,1,0:T(8,128)S(1)}, f32[25,8,128]{2,1,0:T(8,128)S(1)}, u32[]{:S(2)}, u32[]{:S(2)}) collective-permute-start(f32[25,8,128]{2,1,0:T(8,128)S(1)} %get-tuple-element.28), channel_id=1, source_target_pairs={{1,2},{2,1},{5,6},{6,5},{9,10},{10,9},{13,14},{14,13},{17,18},{18,... | collective-permute-start | bytes 307208 | tf_op jit(solution)/shard_map/ppermute | solution.py:759
  23.8 1.6 %near_half.1 = (f32[18,4,24,128]{3,2,1,0:T(8,128)S(1)}, f32[16,4,16,128]{3,2,1,0:T(8,128)S(1)}, f32[36,4,24,128]{3,2,1,0:T(8,128)S(1)}, f32[18,4,24,128]{3,2,1,0:T(8,128)S(1)}) custom-call(s32[18]{0:T(128)S(1)} %pad_add_fusion.scalar_ref, f32[264,128]{1,0:T(8,128)S(1)} %pack.1.refs_0_, f32[264,128]{1,0:T(8,128)S(1)} %collective-permute-done.refs_1_, ...), custom_call_target="tpu_custom_call" | custom-call | tf_op jit(solution)/shard_map/near_half/pallas_call | solution.py:711
  25.5 3.0 %far_half.1 = (f32[4,4,16,128]{3,2,1,0:T(8,128)S(1)}, f32[36,4,24,128]{3,2,1,0:T(8,128)S(1)}, f32[36,4,24,128]{3,2,1,0:T(8,128)S(1)}, f32[256,128]{1,0:T(8,128)S(1)}, f32[18,4,24,128]{3,2,1,0:T(8,128)S(1)}) custom-call(s32[18]{0:T(128)S(1)} %pad_add_fusion.scalar_ref, ...), custom_call_target="tpu_custom_call", output_to_operand_aliasing={{1}: (8, {}), {4}: (9, {})} | custom-call | tf_op jit(solution)/shard_map/far_half/pallas_call | solution.py:711
  28.5 5.2 %collective-permute-start.12 = (f32[256,128]{1,0:T(8,128)S(1)}, f32[256,128]{1,0:T(8,128)S(1)}, u32[]{:S(2)}, u32[]{:S(2)}) collective-permute-start(f32[256,128]{1,0:T(8,128)S(1)} %get-tuple-element.34.c0_ref), channel_id=1, source_target_pairs={{0,2},{1,3},{2,0},{3,1},{4,6},{5,7},{6,4},{7,5},{8,10},{9,11},{10,... | collective-permute-start | bytes 393224 | tf_op jit(solution)/shard_map/ppermute | solution.py:814
  33.7 1.7 %between.1 = (f32[4,32,256]{2,1,0:T(8,128)}, f32[36,4,24,128]{3,2,1,0:T(8,128)S(1)}) custom-call(s32[18]{0:T(128)S(1)} %pad_add_fusion.scalar_ref, f32[36,4,24,128]{3,2,1,0:T(8,128)S(1)} %get-tuple-element.35.q_ref, f32[36,4,24,128]{3,2,1,0:T(8,128)S(1)} %get-tuple-element.36.u_ref, f32[4,4,16,128]{3,2,1,0:T(8,128)S(1)} %get-tuple-element.37.s_ref), custom_call_target="tpu_custom_call" | custom-call | tf_op jit(solution)/shard_map/between/pallas_call | solution.py:711
  35.4 2.7 %collective-permute-done.12.c2_ref = f32[256,128]{1,0:T(8,128)S(1)} collective-permute-done((f32[256,128]{1,0:T(8,128)S(1)}, f32[256,128]{1,0:T(8,128)S(1)}, u32[]{:S(2)}, u32[]{:S(2)}) %collective-permute-start.12) | collective-permute-done | bytes 131104 | tf_op jit(solution)/shard_map/ppermute | solution.py:814
  38.1 0.1 collective-permute-start.13
  38.2 1.2 %collective-permute-done.13.c3_ref = f32[256,128]{1,0:T(8,128)S(1)} collective-permute-done((f32[256,128]{1,0:T(8,128)S(1)}, f32[256,128]{1,0:T(8,128)S(1)}, u32[]{:S(2)}, u32[]{:S(2)}) %collective-permute-start.13) | collective-permute-done | bytes 131104 | tf_op jit(solution)/shard_map/ppermute | solution.py:814
  39.4 6.9 %middle.1 = (f32[6,4,24,128]{3,2,1,0:T(8,128)S(1)}, f32[8,4,24,128]{3,2,1,0:T(8,128)S(1)}, f32[256,128]{1,0:T(8,128)S(1)}) custom-call(s32[18]{0:T(128)S(1)} %pad_add_fusion.scalar_ref, f32[256,128]{1,0:T(8,128)S(1)} %get-tuple-element.34.c0_ref, f32[256,128]{1,0:T(8,128)S(1)} %collective-permute-done.11.c1_ref, ...), custom_call_target="tpu_custom_call" | custom-call | tf_op jit(solution)/shard_map/middle/pallas_call | solution.py:711
  46.3 0.7 %collective-permute-start.15 = (f32[256,128]{1,0:T(8,128)S(1)}, f32[256,128]{1,0:T(8,128)S(1)}, u32[]{:S(2)}, u32[]{:S(2)}) collective-permute-start(f32[256,128]{1,0:T(8,128)S(1)} %get-tuple-element.42.c0_ref), channel_id=1, source_target_pairs={{0,2},{1,3},{2,0},{3,1},{4,6},{5,7},{6,4},{7,5},{8,10},{9,11},{10,... | collective-permute-start | bytes 393224 | tf_op jit(solution)/shard_map/ppermute | solution.py:814
  47.0 0.7 %window.1.win_ref = f32[6,4,24,128]{3,2,1,0:T(8,128)S(1)} custom-call(s32[18]{0:T(128)S(1)} %pad_add_fusion.scalar_ref, f32[6,4,24,128]{3,2,1,0:T(8,128)S(1)} %get-tuple-element.43.qwin_ref, f32[8,4,24,128]{3,2,1,0:T(8,128)S(1)} %get-tuple-element.44.uwin_ref), custom_call_target="tpu_custom_call" | custom-call | tf_op jit(solution)/shard_map/window/pallas_call | solution.py:711
  47.8 4.2 %collective-permute-done.15.c2_ref = f32[256,128]{1,0:T(8,128)S(1)} collective-permute-done((f32[256,128]{1,0:T(8,128)S(1)}, f32[256,128]{1,0:T(8,128)S(1)}, u32[]{:S(2)}, u32[]{:S(2)}) %collective-permute-start.15) | collective-permute-done | bytes 131104 | tf_op jit(solution)/shard_map/ppermute | solution.py:814
  51.9 1.3 %collective-permute-done.16.c3_ref = f32[256,128]{1,0:T(8,128)S(1)} collective-permute-done((f32[256,128]{1,0:T(8,128)S(1)}, f32[256,128]{1,0:T(8,128)S(1)}, u32[]{:S(2)}, u32[]{:S(2)}) %collective-permute-start.16) | collective-permute-done | bytes 131104 | tf_op jit(solution)/shard_map/ppermute | solution.py:814
  53.3 4.0 %last.1 = f32[4,32,256]{2,1,0:T(8,128)} custom-call(s32[18]{0:T(128)S(1)} %pad_add_fusion.scalar_ref, f32[256,128]{1,0:T(8,128)S(1)} %get-tuple-element.42.c0_ref, f32[256,128]{1,0:T(8,128)S(1)} %collective-permute-done.14.c1_ref, f32[256,128]{1,0:T(8,128)S(1)} %collective-permute-done.15.c2_ref, f32[256,128]{1,0:T(8,128)S(1)} %collective-permute-done.16.c3_ref, ...), custom_call_target="tpu_custom_call" | custom-call | tf_op jit(solution)/shard_map/last/pallas_call | solution.py:711
  (12 shorter events, 0.1 us)
Async XLA Ops:
  1.8 10.7 %collective-permute-start = (f32[264,128]{1,0:T(8,128)S(1)}, f32[264,128]{1,0:T(8,128)S(1)}, u32[]{:S(2)}, u32[]{:S(2)}) collective-permute-start(f32[264,128]{1,0:T(8,128)S(1)} %pack.1.refs_0_), channel_id=1, source_target_pairs={{0,16},{4,20},{8,24},{12,28},{16,0},{20,4},{24,8},{28,12},{1,17},{... | collective-permute-start | bytes 405512 | tf_op jit(solution)/shard_map/ppermute | solution.py:749
  5.9 8.7 %collective-permute-start.3 = (f32[264,128]{1,0:T(8,128)S(1)}, f32[264,128]{1,0:T(8,128)S(1)}, u32[]{:S(2)}, u32[]{:S(2)}) collective-permute-start(f32[264,128]{1,0:T(8,128)S(1)} %pack.1.refs_0_), channel_id=1, source_target_pairs={{0,8},{4,12},{8,0},{12,4},{16,24},{20,28},{24,16},{28,20},{1,9},{5... | collective-permute-start | bytes 405512 | tf_op jit(solution)/shard_map/ppermute | solution.py:749
  7.5 9.5 %collective-permute-start.2 = (f32[264,128]{1,0:T(8,128)S(1)}, f32[264,128]{1,0:T(8,128)S(1)}, u32[]{:S(2)}, u32[]{:S(2)}) collective-permute-start(f32[264,128]{1,0:T(8,128)S(1)} %pack.1.refs_0_), channel_id=1, source_target_pairs={{0,4},{4,0},{8,12},{12,8},{16,20},{20,16},{24,28},{28,24},{1,5},{5... | collective-permute-start | bytes 405512 | tf_op jit(solution)/shard_map/ppermute | solution.py:749
  9.0 8.5 %collective-permute-start.1 = (f32[264,128]{1,0:T(8,128)S(1)}, f32[264,128]{1,0:T(8,128)S(1)}, u32[]{:S(2)}, u32[]{:S(2)}) collective-permute-start(f32[264,128]{1,0:T(8,128)S(1)} %pack.1.refs_0_), channel_id=1, source_target_pairs={{0,12},{4,8},{8,4},{12,0},{16,28},{20,24},{24,20},{28,16},{1,13},{... | collective-permute-start | bytes 405512 | tf_op jit(solution)/shard_map/ppermute | solution.py:749
  12.5 6.9 %collective-permute-start.8 = (f32[264,128]{1,0:T(8,128)S(1)}, f32[264,128]{1,0:T(8,128)S(1)}, u32[]{:S(2)}, u32[]{:S(2)}) collective-permute-start(f32[264,128]{1,0:T(8,128)S(1)} %collective-permute-done.refs_1_), channel_id=1, source_target_pairs={{0,8},{4,12},{8,0},{12,4},{16,24},{20,28},{24,16},{28,20},{1,9},{5... | collective-permute-start | bytes 405512 | tf_op jit(solution)/shard_map/ppermute | solution.py:749
  13.1 7.6 %collective-permute-start.7 = (f32[264,128]{1,0:T(8,128)S(1)}, f32[264,128]{1,0:T(8,128)S(1)}, u32[]{:S(2)}, u32[]{:S(2)}) collective-permute-start(f32[264,128]{1,0:T(8,128)S(1)} %collective-permute-done.refs_1_), channel_id=1, source_target_pairs={{0,4},{4,0},{8,12},{12,8},{16,20},{20,16},{24,28},{28,24},{1,5},{5... | collective-permute-start | bytes 405512 | tf_op jit(solution)/shard_map/ppermute | solution.py:749
  14.6 7.7 %collective-permute-start.6 = (f32[264,128]{1,0:T(8,128)S(1)}, f32[264,128]{1,0:T(8,128)S(1)}, u32[]{:S(2)}, u32[]{:S(2)}) collective-permute-start(f32[264,128]{1,0:T(8,128)S(1)} %collective-permute-done.refs_1_), channel_id=1, source_target_pairs={{0,12},{4,8},{8,4},{12,0},{16,28},{20,24},{24,20},{28,16},{1,13},{... | collective-permute-start | bytes 405512 | tf_op jit(solution)/shard_map/ppermute | solution.py:749
  18.0 5.8 %collective-permute-start.4 = (f32[40,8,128]{2,1,0:T(8,128)S(1)}, f32[40,8,128]{2,1,0:T(8,128)S(1)}, u32[]{:S(2)}, u32[]{:S(2)}) collective-permute-start(f32[40,8,128]{2,1,0:T(8,128)S(1)} %get-tuple-element.25), channel_id=1, source_target_pairs={{0,1},{2,3},{1,0},{3,2},{4,5},{6,7},{5,4},{7,6},{8,9},{10,11},{9,8... | collective-permute-start | bytes 491528 | tf_op jit(solution)/shard_map/ppermute | solution.py:758
  18.1 5.8 %collective-permute-start.5 = (f32[40,8,128]{2,1,0:T(8,128)S(1)}, f32[40,8,128]{2,1,0:T(8,128)S(1)}, u32[]{:S(2)}, u32[]{:S(2)}) collective-permute-start(f32[40,8,128]{2,1,0:T(8,128)S(1)} %get-tuple-element.26), channel_id=1, source_target_pairs={{1,2},{2,1},{5,6},{6,5},{9,10},{10,9},{13,14},{14,13},{17,18},{18,... | collective-permute-start | bytes 491528 | tf_op jit(solution)/shard_map/ppermute | solution.py:759
  23.1 2.4 %collective-permute-start.9 = (f32[25,8,128]{2,1,0:T(8,128)S(1)}, f32[25,8,128]{2,1,0:T(8,128)S(1)}, u32[]{:S(2)}, u32[]{:S(2)}) collective-permute-start(f32[25,8,128]{2,1,0:T(8,128)S(1)} %get-tuple-element.27), channel_id=1, source_target_pairs={{0,1},{2,3},{1,0},{3,2},{4,5},{6,7},{5,4},{7,6},{8,9},{10,11},{9,8... | collective-permute-start | bytes 307208 | tf_op jit(solution)/shard_map/ppermute | solution.py:758
  23.1 2.3 %collective-permute-start.10 = (f32[25,8,128]{2,1,0:T(8,128)S(1)}, f32[25,8,128]{2,1,0:T(8,128)S(1)}, u32[]{:S(2)}, u32[]{:S(2)}) collective-permute-start(f32[25,8,128]{2,1,0:T(8,128)S(1)} %get-tuple-element.28), channel_id=1, source_target_pairs={{1,2},{2,1},{5,6},{6,5},{9,10},{10,9},{13,14},{14,13},{17,18},{18,... | collective-permute-start | bytes 307208 | tf_op jit(solution)/shard_map/ppermute | solution.py:759
  28.5 9.5 %collective-permute-start.12 = (f32[256,128]{1,0:T(8,128)S(1)}, f32[256,128]{1,0:T(8,128)S(1)}, u32[]{:S(2)}, u32[]{:S(2)}) collective-permute-start(f32[256,128]{1,0:T(8,128)S(1)} %get-tuple-element.34.c0_ref), channel_id=1, source_target_pairs={{0,2},{1,3},{2,0},{3,1},{4,6},{5,7},{6,4},{7,5},{8,10},{9,11},{10,... | collective-permute-start | bytes 393224 | tf_op jit(solution)/shard_map/ppermute | solution.py:814
  33.7 4.5 %collective-permute-start.11 = (f32[256,128]{1,0:T(8,128)S(1)}, f32[256,128]{1,0:T(8,128)S(1)}, u32[]{:S(2)}, u32[]{:S(2)}) collective-permute-start(f32[256,128]{1,0:T(8,128)S(1)} %get-tuple-element.34.c0_ref), channel_id=1, source_target_pairs={{0,1},{1,0},{2,3},{3,2},{4,5},{5,4},{6,7},{7,6},{8,9},{9,8},{10,11... | collective-permute-start | bytes 393224 | tf_op jit(solution)/shard_map/ppermute | solution.py:814
  38.1 1.3 %collective-permute-start.13 = (f32[256,128]{1,0:T(8,128)S(1)}, f32[256,128]{1,0:T(8,128)S(1)}, u32[]{:S(2)}, u32[]{:S(2)}) collective-permute-start(f32[256,128]{1,0:T(8,128)S(1)} %collective-permute-done.12.c2_ref), channel_id=1, source_target_pairs={{0,1},{1,0},{2,3},{3,2},{4,5},{5,4},{6,7},{7,6},{8,9},{9,8},{10,11... | collective-permute-start | bytes 393224 | tf_op jit(solution)/shard_map/ppermute | solution.py:814
  46.3 5.6 %collective-permute-start.15 = (f32[256,128]{1,0:T(8,128)S(1)}, f32[256,128]{1,0:T(8,128)S(1)}, u32[]{:S(2)}, u32[]{:S(2)}) collective-permute-start(f32[256,128]{1,0:T(8,128)S(1)} %get-tuple-element.42.c0_ref), channel_id=1, source_target_pairs={{0,2},{1,3},{2,0},{3,1},{4,6},{5,7},{6,4},{7,5},{8,10},{9,11},{10,... | collective-permute-start | bytes 393224 | tf_op jit(solution)/shard_map/ppermute | solution.py:814
  47.0 4.9 %collective-permute-start.14 = (f32[256,128]{1,0:T(8,128)S(1)}, f32[256,128]{1,0:T(8,128)S(1)}, u32[]{:S(2)}, u32[]{:S(2)}) collective-permute-start(f32[256,128]{1,0:T(8,128)S(1)} %get-tuple-element.42.c0_ref), channel_id=1, source_target_pairs={{0,1},{1,0},{2,3},{3,2},{4,5},{5,4},{6,7},{7,6},{8,9},{9,8},{10,11... | collective-permute-start | bytes 393224 | tf_op jit(solution)/shard_map/ppermute | solution.py:814
  51.9 1.3 %collective-permute-start.16 = (f32[256,128]{1,0:T(8,128)S(1)}, f32[256,128]{1,0:T(8,128)S(1)}, u32[]{:S(2)}, u32[]{:S(2)}) collective-permute-start(f32[256,128]{1,0:T(8,128)S(1)} %collective-permute-done.15.c2_ref), channel_id=1, source_target_pairs={{0,1},{1,0},{2,3},{3,2},{4,5},{5,4},{6,7},{7,6},{8,9},{9,8},{10,11... | collective-permute-start | bytes 393224 | tf_op jit(solution)/shard_map/ppermute | solution.py:814
